TPU v7x, 512 devices: a whole 4x4x16 slice. The times are simulated.
512 devices in a mesh: frame: 16 (over y, z_lo), tile: 32 (over x, z_hi, core).
Axes of the slice: x: 4, y: 4, z: 16 (z_hi: 4, z_lo: 4; z = z_hi * 4 + z_lo), core: 2. Of those that a mesh axis runs over, the one named last changes fastest.
Arguments:
- latents: bfloat16 [16, 320, 8192], P('frame', None, 'tile'), may hold values from -80 to 80
- out_grad: bfloat16 [16, 320, 8192], P('frame', None, 'tile'), may hold values from -6 to 6
- w_spatial: bfloat16 [320, 2880], P('tile', 'frame'), may hold values from -0.109375 to 0.109375
- w_temporal: bfloat16 [320, 960], P('tile', 'frame'), may hold values from -0.1875 to 0.1875
- norm_gain: float32 [320], replicated, may hold values from 0.5 to 1.5
- norm_shift: float32 [320], replicated, may hold values from -1 to 1
- heights: int32 [32], P('tile'), may hold values from 8 to 16, as said below
Outputs:
- grad_input: bfloat16 [16, 320, 8192], P('frame', None, 'tile')
- grad_spatial: float32 [320, 2880], P('tile', 'frame')
- grad_temporal: float32 [320, 960], P('tile', 'frame')
- grad_gain: float32 [320], replicated
- grad_shift: float32 [320], replicated
Inputs may be any that keep to these rules, and one draw needn't show every extreme that they name: `heights`: each entry is a multiple of 8; in every draw at least one strip has 16 live rows.
All inputs are finite; a program needn't handle non-finite values.
Results may differ from a plain program's by a relative error of at most 0.028.
Values may be sent and summed in bfloat16 or wider, within the bound.
No kernel may reach another device: no remote copies, remote signals or barrier semaphores. Data moves between devices by JAX's collectives and lax.ppermute only.
A program may use at most 64 MiB of HBM per device.

v0:
```python
import jax
import jax.numpy as jnp
from jax import lax
from jax.sharding import Mesh
from jax.sharding import PartitionSpec as P

GROUPS = 32
COLUMNS = 16
STRIP_ROWS = 16
TILE = ("tile_0", "tile_1", "tile_2")
FRAME = ("frame_0", "frame_1")
FRAME_TILE = ("frame_0", "frame_1", "tile_0", "tile_1", "tile_2")


EPSILON = 1e-05


def sent_together(arrays, axis, dim, along):
    both = jnp.concatenate(arrays, axis=along)
    result, at, outs = (lax.all_gather(both, axis, axis=dim, tiled=True), 0, [])
    for a in arrays:
        outs.append(lax.slice_in_dim(result, at, at + a.shape[along], axis=along))
        at += a.shape[along]
    return tuple(outs)


def joined_along(tiles, dim):
    dims = list(tiles.shape[1:])
    dims[dim] *= tiles.shape[0]
    return jnp.moveaxis(tiles, 0, dim).reshape(dims)


def gather_together(arrays, axis, dims):
    ravelled = jnp.concatenate([a.reshape(-1) for a in arrays])
    lines, at, outs = (lax.all_gather(ravelled, axis), 0, [])
    for a, dim in zip(arrays, dims):
        tiles = lines[:, at : at + a.size].reshape(-1, *a.shape)
        outs.append(joined_along(tiles, dim))
        at += a.size
    return tuple(outs)


def over_axes(shard, axes):
    for axis in axes:
        shard = lax.psum(shard, axis)
    return shard


def from_behind(shard, axis, by):
    peers = lax.axis_size(axis)
    pairs = [(i, i + by) for i in range(peers) if 0 <= i + by < peers]
    return lax.ppermute(shard, axis, pairs)


def padded_2(cells, sides, width):
    for axis, dim in sides:
        count = lax.axis_size(axis)
        ends = count - 1
        head = lax.slice_in_dim(cells, 0, width, axis=dim)
        tail = lax.slice_in_dim(cells, cells.shape[dim] - width, cells.shape[dim], axis=dim)
        cells = jnp.concatenate(
            [
                lax.ppermute(tail, axis, [(i, (i + 1) % count) for i in range(ends)]),
                cells,
                lax.ppermute(head, axis, [((i + 1) % count, i) for i in range(ends)]),
            ],
            axis=dim,
        )
    return cells


def cut_along(shard, dim, peers):
    before, after = (shard.shape[:dim], shard.shape[dim + 1 :])
    return jnp.moveaxis(shard.reshape(*before, peers, -1, *after), dim, 0)


def sum_packed(arrays, axis, dims):
    peers = lax.axis_size(axis)
    tiles = [cut_along(a, dim, peers) for a, dim in zip(arrays, dims)]
    lines = jnp.concatenate([b.reshape(peers, -1) for b in tiles], axis=1)
    extent = max(16, -(-lines.shape[1] // 1024) * 8)
    lines = jnp.pad(lines, ((0, 0), (0, extent * 128 - lines.shape[1]))).reshape(-1, 128)
    ravelled, at, outs = (lax.psum_scatter(lines, axis, tiled=True).reshape(-1), 0, [])
    for b in tiles:
        part = b[0]
        outs.append(ravelled[at : at + part.size].reshape(part.shape))
        at += part.size
    return tuple(outs)


def sent_and_summed(shard, axis, dim):
    peers = lax.axis_size(axis)
    tiles = lax.all_to_all(cut_along(shard, dim, peers), axis, 0, 0, tiled=True)
    return jnp.sum(tiles.astype(jnp.float32), axis=0)


def flip_taps(weight, tap_count):
    outputs = weight.shape[0]
    return jnp.transpose(weight.reshape(outputs, tap_count, -1)[:, ::-1, :], (2, 1, 0)).reshape(
        -1, tap_count * outputs
    )


def padded_rows(row_grid, above_row, below_row, height):
    channel_count = row_grid.shape[0]
    padded = jnp.zeros((channel_count, STRIP_ROWS + 2, COLUMNS + 2), row_grid.dtype)
    padded = padded.at[:, 1 : STRIP_ROWS + 1, 1 : COLUMNS + 1].set(row_grid)
    padded = padded.at[:, 0, 1 : COLUMNS + 1].set(above_row)
    below_block = jnp.pad(below_row, ((0, 0), (1, 1)))[:, None, :]
    return lax.dynamic_update_slice(padded, below_block, (jnp.int32(0), height + 1, jnp.int32(0)))


def tap_columns(padded, row_count):
    pieces = [
        padded[:, row_step : row_step + row_count, col_step : col_step + COLUMNS]
        for row_step in range(3)
        for col_step in range(3)
    ]
    return jnp.stack(pieces, axis=0).reshape(9 * padded.shape[0], row_count * COLUMNS)


def local(latents, out_grad, w_spatial, w_temporal, norm_gain, norm_shift, heights):
    channel_count = latents.shape[1]
    cell_count = latents.shape[2]
    group_size = channel_count // GROUPS
    height = heights[0]
    slot_row = jnp.arange(cell_count, dtype=jnp.int32) // COLUMNS
    live_cells = slot_row < height
    live_float = live_cells.astype(jnp.float32)
    contract_last = (((1,), (1,)), ((), ()))
    part_spatial_w, part_temporal_w = sent_together((w_spatial, w_temporal), TILE, 0, 1)
    spatial_full, temporal_full = gather_together((part_spatial_w, part_temporal_w), FRAME, (1, 1))
    latent_full = latents[0].astype(jnp.float32)
    masked = latent_full * live_float[None, :]
    group_sum = masked.reshape(GROUPS, group_size, cell_count).sum(axis=(1, 2))
    group_square = (masked * latent_full).reshape(GROUPS, group_size, cell_count).sum(axis=(1, 2))
    own_count = height.astype(jnp.float32) * COLUMNS
    total_sum, total_square, position_count = (
        over_axes(group_sum, FRAME_TILE),
        over_axes(group_square, FRAME_TILE),
        over_axes(own_count, FRAME_TILE),
    )
    group_count = position_count * group_size
    group_mean = total_sum / group_count
    group_rstd = lax.rsqrt(total_square / group_count - group_mean * group_mean + EPSILON)
    mean_column = jnp.repeat(group_mean, group_size)[:, None]
    rstd_column = jnp.repeat(group_rstd, group_size)[:, None]
    gain_column = norm_gain[:, None]
    normed = (latent_full - mean_column) * rstd_column
    pre_act = gain_column * normed + norm_shift[:, None]
    activated = jnp.where(live_cells[None, :], jax.nn.silu(pre_act), 0.0).astype(jnp.bfloat16)
    act_grid = activated.reshape(channel_count, STRIP_ROWS, COLUMNS)
    last_live = lax.dynamic_slice_in_dim(act_grid, height - 1, 1, 1)[:, 0, :]
    from_above = from_behind(last_live, TILE, 1)
    from_below = from_behind(act_grid[:, 0, :], TILE, -1)
    act_padded = padded_rows(act_grid, from_above, from_below, height)
    act_columns = tap_columns(act_padded, STRIP_ROWS)
    spatial_raw = jnp.dot(spatial_full, act_columns, preferred_element_type=jnp.float32)
    spatial_out = jnp.where(live_cells[None, :], spatial_raw, 0.0).astype(jnp.bfloat16)
    spatial_frames = padded_2(spatial_out[None], ((FRAME, 0),), 1)
    grad_here = jnp.where(live_cells[None, :], out_grad[0], jnp.zeros((), jnp.bfloat16))
    grad_frames = padded_2(grad_here[None], ((FRAME, 0),), 1)
    part_temporal = lax.dot_general(
        grad_here,
        spatial_frames.reshape(3 * channel_count, cell_count),
        contract_last,
        preferred_element_type=jnp.float32,
    )
    grad_spat = jnp.dot(
        flip_taps(temporal_full, 3),
        grad_frames.reshape(3 * channel_count, cell_count),
        preferred_element_type=jnp.float32,
    )
    grad_spat = jnp.where(live_cells[None, :], grad_spat, 0.0).astype(jnp.bfloat16)
    spat_grid = grad_spat.reshape(channel_count, STRIP_ROWS, COLUMNS)
    grad_last = lax.dynamic_slice_in_dim(spat_grid, height - 1, 1, 1)[:, 0, :]
    grad_above = from_behind(grad_last, TILE, 1)
    grad_below = from_behind(spat_grid[:, 0, :], TILE, -1)
    grad_padded = padded_rows(spat_grid, grad_above, grad_below, height)
    spatial_flip = flip_taps(spatial_full, 9)
    grad_act = jnp.dot(
        spatial_flip, tap_columns(grad_padded, STRIP_ROWS), preferred_element_type=jnp.float32
    )
    part_spatial = lax.dot_general(
        grad_spat, act_columns, contract_last, preferred_element_type=jnp.float32
    )
    sigmoid_act = jax.nn.sigmoid(pre_act)
    grad_pre = jnp.where(
        live_cells[None, :], grad_act * sigmoid_act * (1.0 + pre_act * (1.0 - sigmoid_act)), 0.0
    )
    chan_gain, chan_shift = (
        over_axes(jnp.sum(grad_pre * normed, axis=1), FRAME_TILE),
        over_axes(jnp.sum(grad_pre, axis=1), FRAME_TILE),
    )
    shift_sum = (norm_gain * chan_shift).reshape(GROUPS, group_size).sum(1) / group_count
    gain_sum = (norm_gain * chan_gain).reshape(GROUPS, group_size).sum(1) / group_count
    result = grad_here.astype(jnp.float32) + rstd_column * (
        gain_column * grad_pre
        - jnp.repeat(shift_sum, group_size)[:, None]
        - normed * jnp.repeat(gain_sum, group_size)[:, None]
    )
    grad_input = jnp.where(live_cells[None, :], result, 0.0).astype(jnp.bfloat16)[None]
    tile_spatial, tile_temporal = tuple(
        (
            part.astype(jnp.float32)
            for part in sum_packed(
                (part_spatial.astype(jnp.bfloat16), part_temporal.astype(jnp.bfloat16)),
                TILE,
                (0, 0),
            )
        )
    )
    grad_spatial, grad_temporal = (
        sent_and_summed(tile_spatial.astype(jnp.bfloat16), FRAME, 1),
        sent_and_summed(tile_temporal.astype(jnp.bfloat16), FRAME, 1),
    )
    grad_scale = lax.rsqrt(position_count)
    return (
        grad_input,
        grad_scale * grad_spatial,
        grad_scale * grad_temporal,
        grad_scale * chan_gain,
        grad_scale * chan_shift,
    )


def solution(mesh):
    split = Mesh(
        mesh.devices.reshape(4, 4, 4, 4, 2), ("frame_0", "frame_1", "tile_0", "tile_1", "tile_2")
    )
    placed = (
        P(FRAME, None, TILE),
        P(FRAME, None, TILE),
        P(TILE, FRAME),
        P(TILE, FRAME),
        P(),
        P(),
        P(TILE),
    )
    return jax.shard_map(
        local,
        mesh=split,
        in_specs=placed,
        out_specs=(P(FRAME, None, TILE), P(TILE, FRAME), P(TILE, FRAME), P(), P()),
        check_vma=False,
    )
```

profile of v0, /device:TPU:4, one launch (start us, length us, event | category | flops | bytes accessed | tf_op | source)
XLA Modules:
  0.0 367.9 jit_solution(7472396379796567899)
XLA Ops:
  8.1 52.7 %all-gather.1 = bf16[32,10,240]{2,1,0:T(8,128)(2,1)S(1)} all-gather(bf16[1,10,240]{2,1,0:T(8,128)(2,1)S(1)} %maximum_bitcast_fusion), channel_id=1, replica_groups=mesh['frame_0'=4,'frame_1'=4,'tile_0'=4,'tile_1'=4,'tile_2'=2] {'tile_0'..., dimensions={0}, use_global_device_ids=true | all-gather | bytes 158400 | tf_op jit(solution)/shard_map/all_gather | solution.py:20
  63.0 3.5 collective-permute-start
  68.6 15.0 %all-reduce.12 = (f32[32]{0:T(128)S(1)}, f32[]{:T(128)}, f32[32]{0:T(128)S(1)}) all-reduce(f32[32]{0:T(128)S(1)} %reduce_sum.91, f32[]{:T(128)S(6)} %mul.127, f32[32]{0:T(128)S(1)} %reduce_sum.88), channel_id=1, replica_groups=mesh['frame_0'=4,'frame_1'=4,'tile_0'=4,'tile_1'=4,'tile_2'=2] {'frame_0'}, use_global_device_ids=true, to_apply=%region_14.15 | all-reduce | flops 65 | bytes 520 | tf_op jit(solution)/shard_map/psum | solution.py:45
  83.6 9.0 %all-reduce.10 = (f32[32]{0:T(128)S(1)}, f32[]{:T(128)}, f32[32]{0:T(128)S(1)}) all-reduce(f32[32]{0:T(128)S(1)} %get-tuple-element.74, f32[]{:T(128)} %get-tuple-element.75, f32[32]{0:T(128)S(1)} %get-tuple-element.76), channel_id=1, replica_groups=mesh['frame_0'=4,'frame_1'=4,'tile_0'=4,'tile_1'=4,'tile_2'=2] {'frame_1'}, use_global_device_ids=true, to_apply=%region_15.16 | all-reduce | flops 65 | bytes 520 | tf_op jit(solution)/shard_map/psum | solution.py:45
  92.6 13.7 %all-reduce.8 = (f32[32]{0:T(128)S(1)}, f32[]{:T(128)}, f32[32]{0:T(128)S(1)}) all-reduce(f32[32]{0:T(128)S(1)} %get-tuple-element.69, f32[]{:T(128)} %get-tuple-element.70, f32[32]{0:T(128)S(1)} %get-tuple-element.71), channel_id=1, replica_groups=mesh['frame_0'=4,'frame_1'=4,'tile_0'=4,'tile_1'=4,'tile_2'=2] {'tile_0'}, use_global_device_ids=true, to_apply=%region_16.17 | all-reduce | flops 65 | bytes 520 | tf_op jit(solution)/shard_map/psum | solution.py:45
  106.4 13.2 %all-reduce.6 = (f32[32]{0:T(128)S(1)}, f32[]{:T(128)}, f32[32]{0:T(128)S(1)}) all-reduce(f32[32]{0:T(128)S(1)} %get-tuple-element.64, f32[]{:T(128)} %get-tuple-element.65, f32[32]{0:T(128)S(1)} %get-tuple-element.66), channel_id=1, replica_groups=mesh['frame_0'=4,'frame_1'=4,'tile_0'=4,'tile_1'=4,'tile_2'=2] {'tile_1'}, use_global_device_ids=true, to_apply=%region_17.18 | all-reduce | flops 65 | bytes 520 | tf_op jit(solution)/shard_map/psum | solution.py:45
  125.9 8.3 %collective-permute-start.5 = (bf16[320,16]{0,1:T(8,128)(2,1)S(1)}, bf16[320,16]{0,1:T(8,128)(2,1)S(1)}, u32[]{:S(2)}, u32[]{:S(2)}) collective-permute-start(bf16[320,16]{0,1:T(8,128)(2,1)S(1)} %get-tuple-element.84), channel_id=1, source_target_pairs={{1,0},{2,1},{3,2},{4,3},{5,4},{6,5},{7,6},{8,7},{9,8},{10,9},{11,1... | collective-permute-start | bytes 30728 | tf_op jit(solution)/shard_map/ppermute | solution.py:52
  141.2 12.6 %all-gather.4.cloned.1.call-done = bf16[1228800]{0:T(1024)(128)(2,1)} async-done(((bf16[76800]{0:T(1024)(128)(2,1)}), bf16[1228800]{0:T(1024)(128)(2,1)}) %all-gather.4.cloned.1.call-update) | async-done | bytes 2457616 | tf_op jit(solution)/shard_map/all_gather | solution.py:35
  158.2 10.2 %reshape.316 = bf16[16,320,180]{2,1,0:T(8,128)(2,1)} reshape(bf16[16,57600]{1,0:T(8,128)(2,1)} %slice.213) | data formatting | bytes 3686400 | tf_op jit(solution)/shard_map/reshape | solution.py:37
  168.4 3.2 copy.30
  181.5 5.1 %reshape.318 = bf16[16,320,60]{2,1,0:T(8,128)(2,1)} reshape(bf16[16,19200]{1,0:T(8,128)(2,1)S(1)} %slice-done) | data formatting | bytes 1228800 | tf_op jit(solution)/shard_map/reshape | solution.py:37
  194.9 5.0 %reshape_reshape.14 = bf16[32,28800]{1,0:T(8,128)(2,1)} reshape(bf16[320,2880]{1,0:T(8,128)(2,1)} %convolution_convert_fusion) | data formatting | bytes 3686400 | tf_op jit(solution)/shard_map/reshape;reshape | solution.py:80
  205.3 4.4 %reshape.330 = bf16[9728,128]{1,0:T(8,128)(2,1)} reshape(bf16[32,38912]{1,0:T(8,128)(2,1)} %fusion.2) | data formatting | bytes 4980736 | tf_op jit(solution)/shard_map/reshape | solution.py:82
  214.9 8.4 %collective-permute-start.3 = (bf16[320,16]{0,1:T(8,128)(2,1)S(1)}, bf16[320,16]{0,1:T(8,128)(2,1)S(1)}, u32[]{:S(2)}, u32[]{:S(2)}) collective-permute-start(bf16[320,16]{0,1:T(8,128)(2,1)S(1)} %get-tuple-element.86), channel_id=1, source_target_pairs={{1,0},{2,1},{3,2},{4,3},{5,4},{6,5},{7,6},{8,7},{9,8},{10,9},{11,1... | collective-permute-start | bytes 30728 | tf_op jit(solution)/shard_map/ppermute | solution.py:52
  234.1 3.2 fusion.42
  237.3 9.1 %all-reduce.11 = (f32[320]{0:T(512)S(1)}, f32[320]{0:T(512)S(1)}) all-reduce(f32[320]{0:T(512)S(1)} %get-tuple-element.54, f32[320]{0:T(512)S(1)} %get-tuple-element.53), channel_id=1, replica_groups=mesh['frame_0'=4,'frame_1'=4,'tile_0'=4,'tile_1'=4,'tile_2'=2] {'frame_0'}, use_global_device_ids=true, to_apply=%region_27.28 | all-reduce | flops 640 | bytes 5120 | tf_op jit(solution)/shard_map/psum | solution.py:45
  246.3 14.1 %all-reduce.9 = (f32[320]{0:T(512)S(1)}, f32[320]{0:T(512)S(1)}) all-reduce(f32[320]{0:T(512)S(1)} %get-tuple-element.72, f32[320]{0:T(512)S(1)} %get-tuple-element.73), channel_id=1, replica_groups=mesh['frame_0'=4,'frame_1'=4,'tile_0'=4,'tile_1'=4,'tile_2'=2] {'frame_1'}, use_global_device_ids=true, to_apply=%region_28.29 | all-reduce | flops 640 | bytes 5120 | tf_op jit(solution)/shard_map/psum | solution.py:45
  260.5 9.0 %all-reduce.7 = (f32[320]{0:T(512)S(1)}, f32[320]{0:T(512)S(1)}) all-reduce(f32[320]{0:T(512)S(1)} %get-tuple-element.67, f32[320]{0:T(512)S(1)} %get-tuple-element.68), channel_id=1, replica_groups=mesh['frame_0'=4,'frame_1'=4,'tile_0'=4,'tile_1'=4,'tile_2'=2] {'tile_0'}, use_global_device_ids=true, to_apply=%region_29.30 | all-reduce | flops 640 | bytes 5120 | tf_op jit(solution)/shard_map/psum | solution.py:45
  269.5 18.8 %all-reduce.5 = (f32[320]{0:T(512)S(1)}, f32[320]{0:T(512)S(1)}) all-reduce(f32[320]{0:T(512)S(1)} %get-tuple-element.62, f32[320]{0:T(512)S(1)} %get-tuple-element.63), channel_id=1, replica_groups=mesh['frame_0'=4,'frame_1'=4,'tile_0'=4,'tile_1'=4,'tile_2'=2] {'tile_1'}, use_global_device_ids=true, to_apply=%region_30.31 | all-reduce | flops 640 | bytes 5120 | tf_op jit(solution)/shard_map/psum | solution.py:45
  292.1 41.2 %reduce-scatter.2.cloned.1.call-done = bf16[304,128]{1,0:T(8,128)(2,1)} async-done(((bf16[9728,128]{1,0:T(8,128)(2,1)}), bf16[304,128]{1,0:T(8,128)(2,1)}) %reduce-scatter.2.cloned.1.call-update) | async-done | bytes 77840 | tf_op jit(solution)/shard_map/reduce_scatter | solution.py:83
  335.0 5.7 %all-to-all-start.1 = ((bf16[16,2,300]{2,1,0:T(2,128)(2,1)}), bf16[16,2,300]{2,1,0:T(2,128)(2,1)S(1)}, u32[]{:S(2)}, u32[]{:S(2)}) async-start(bf16[16,2,300]{2,1,0:T(2,128)(2,1)} %reshape.341), calls=%async_computation.2 | async-start | bytes 49152 | tf_op jit(solution)/shard_map/all_to_all | solution.py:93
  343.5 5.1 %all-to-all-done.1 = bf16[16,2,300]{2,1,0:T(2,128)(2,1)S(1)} async-done(((bf16[16,2,300]{2,1,0:T(2,128)(2,1)}), bf16[16,2,300]{2,1,0:T(2,128)(2,1)S(1)}, u32[]{:S(2)}, u32[]{:S(2)}) %all-to-all-start.1) | async-done | bytes 19232 | tf_op jit(solution)/shard_map/all_to_all | solution.py:93
  348.6 3.5 all-to-all-start
  352.9 7.3 %all-to-all-done = bf16[16,2,900]{2,1,0:T(2,128)(2,1)S(1)} async-done(((bf16[16,2,900]{2,1,0:T(2,128)(2,1)}), bf16[16,2,900]{2,1,0:T(2,128)(2,1)S(1)}, u32[]{:S(2)}, u32[]{:S(2)}) %all-to-all-start) | async-done | bytes 57632 | tf_op jit(solution)/shard_map/all_to_all | solution.py:93
  (137 shorter events, 69.9 us)
Async XLA Ops:
  7.2 55.8 %copy-start.6 = (bf16[1,320,256]{2,1,0:T(8,128)(2,1)S(1)}, bf16[1,320,256]{2,1,0:T(8,128)(2,1)}, u32[]{:S(2)}) copy-start(bf16[1,320,256]{2,1,0:T(8,128)(2,1)} %param.16) | copy-start | bytes 491524
  7.2 60.7 %copy-start.2 = (bf16[1,320,256]{2,1,0:T(8,128)(2,1)S(1)}, bf16[1,320,256]{2,1,0:T(8,128)(2,1)}, u32[]{:S(2)}) copy-start(bf16[1,320,256]{2,1,0:T(8,128)(2,1)} %param.15) | copy-start | bytes 491524
  7.2 116.5 %copy-start.8 = (f32[320]{0:T(512)S(1)}, f32[320]{0:T(512)}, u32[]{:S(2)}) copy-start(f32[320]{0:T(512)} %param.19) | copy-start | bytes 3844
  7.2 116.5 %copy-start.9 = (f32[320]{0:T(512)S(1)}, f32[320]{0:T(512)}, u32[]{:S(2)}) copy-start(f32[320]{0:T(512)} %param.20) | copy-start | bytes 3844
  7.2 146.6 %all-gather.4.cloned.1.call-start = ((), (), s32[]{:S(2)}) async-start(), calls=%async_computation.4 | async-start | bytes 2611200 | tf_op jit(solution)/shard_map/all_gather | solution.py:35
  62.3 271.0 %reduce-scatter.2.cloned.1.call-start = ((), (), s32[]{:S(2)}) async-start(), calls=%async_computation.3 | async-start | bytes 2568192 | tf_op jit(solution)/shard_map/reduce_scatter | solution.py:83
  63.0 127.7 %collective-permute-start = (bf16[1,320,256]{2,1,0:T(8,128)(2,1)S(1)}, bf16[1,320,256]{2,1,0:T(8,128)(2,1)}, u32[]{:S(2)}, u32[]{:S(2)}) collective-permute-start(bf16[1,320,256]{2,1,0:T(8,128)(2,1)S(1)} %broadcast_select_fusion), channel_id=1, source_target_pairs={{0,32},{32,64},{64,96},{96,128},{128,160},{160,192},{192,224},{224... | collective-permute-start | bytes 491528 | tf_op jit(solution)/shard_map/ppermute | solution.py:63
  66.5 124.2 %collective-permute-start.1 = (bf16[1,320,256]{2,1,0:T(8,128)(2,1)S(1)}, bf16[1,320,256]{2,1,0:T(8,128)(2,1)}, u32[]{:S(2)}, u32[]{:S(2)}) collective-permute-start(bf16[1,320,256]{2,1,0:T(8,128)(2,1)S(1)} %broadcast_select_fusion), channel_id=1, source_target_pairs={{32,0},{64,32},{96,64},{128,96},{160,128},{192,160},{224,192},{256... | collective-permute-start | bytes 491528 | tf_op jit(solution)/shard_map/ppermute | solution.py:65
  123.9 11.1 %collective-permute-start.4 = (bf16[320,16]{0,1:T(8,128)(2,1)S(1)}, bf16[320,16]{0,1:T(8,128)(2,1)S(1)}, u32[]{:S(2)}, u32[]{:S(2)}) collective-permute-start(bf16[320,16]{0,1:T(8,128)(2,1)S(1)} %get-tuple-element.85), channel_id=1, source_target_pairs={{0,1},{1,2},{2,3},{3,4},{4,5},{5,6},{6,7},{7,8},{8,9},{9,10},{10,1... | collective-permute-start | bytes 30728 | tf_op jit(solution)/shard_map/ppermute | solution.py:52
  125.9 10.6 %collective-permute-start.5 = (bf16[320,16]{0,1:T(8,128)(2,1)S(1)}, bf16[320,16]{0,1:T(8,128)(2,1)S(1)}, u32[]{:S(2)}, u32[]{:S(2)}) collective-permute-start(bf16[320,16]{0,1:T(8,128)(2,1)S(1)} %get-tuple-element.84), channel_id=1, source_target_pairs={{1,0},{2,1},{3,2},{4,3},{5,4},{6,5},{7,6},{8,7},{9,8},{10,9},{11,1... | collective-permute-start | bytes 30728 | tf_op jit(solution)/shard_map/ppermute | solution.py:52
  156.2 2.0 copy-start
  173.9 7.6 %slice-start = ((bf16[16,76800]{1,0:T(8,128)(2,1)}), bf16[16,19200]{1,0:T(8,128)(2,1)S(1)}, s32[]{:S(2)}) async-start(bf16[16,76800]{1,0:T(8,128)(2,1)} %copy-done), calls=%async_computation.5 | async-start | bytes 1228800 | tf_op jit(solution)/shard_map/slice | solution.py:37
  176.9 23.0 %collective-permute-start.6 = (bf16[1,320,256]{2,1,0:T(8,128)(2,1)S(1)}, bf16[1,320,256]{2,1,0:T(8,128)(2,1)}, u32[]{:S(2)}, u32[]{:S(2)}) collective-permute-start(bf16[1,320,256]{2,1,0:T(8,128)(2,1)S(1)} %fusion.8), channel_id=1, source_target_pairs={{0,32},{32,64},{64,96},{96,128},{128,160},{160,192},{192,224},{224... | collective-permute-start | bytes 491528 | tf_op jit(solution)/shard_map/ppermute | solution.py:63
  180.0 19.8 %collective-permute-start.7 = (bf16[1,320,256]{2,1,0:T(8,128)(2,1)S(1)}, bf16[1,320,256]{2,1,0:T(8,128)(2,1)}, u32[]{:S(2)}, u32[]{:S(2)}) collective-permute-start(bf16[1,320,256]{2,1,0:T(8,128)(2,1)S(1)} %fusion.8), channel_id=1, source_target_pairs={{32,0},{64,32},{96,64},{128,96},{160,128},{192,160},{224,192},{256... | collective-permute-start | bytes 491528 | tf_op jit(solution)/shard_map/ppermute | solution.py:65
  190.7 2.2 copy-start.1
  192.3 0.7 copy-start.4
  209.7 0.9 copy-start.5
  213.0 14.8 %collective-permute-start.2 = (bf16[320,16]{0,1:T(8,128)(2,1)S(1)}, bf16[320,16]{0,1:T(8,128)(2,1)S(1)}, u32[]{:S(2)}, u32[]{:S(2)}) collective-permute-start(bf16[320,16]{0,1:T(8,128)(2,1)S(1)} %get-tuple-element.87), channel_id=1, source_target_pairs={{0,1},{1,2},{2,3},{3,4},{4,5},{5,6},{6,7},{7,8},{8,9},{9,10},{10,1... | collective-permute-start | bytes 30728 | tf_op jit(solution)/shard_map/ppermute | solution.py:52
  214.9 14.5 %collective-permute-start.3 = (bf16[320,16]{0,1:T(8,128)(2,1)S(1)}, bf16[320,16]{0,1:T(8,128)(2,1)S(1)}, u32[]{:S(2)}, u32[]{:S(2)}) collective-permute-start(bf16[320,16]{0,1:T(8,128)(2,1)S(1)} %get-tuple-element.86), channel_id=1, source_target_pairs={{1,0},{2,1},{3,2},{4,3},{5,4},{6,5},{7,6},{8,7},{9,8},{10,9},{11,1... | collective-permute-start | bytes 30728 | tf_op jit(solution)/shard_map/ppermute | solution.py:52
  231.3 2.8 copy-start.3
  234.1 106.6 %copy-start.7 = (bf16[1,320,256]{2,1,0:T(8,128)(2,1)S(1)}, bf16[1,320,256]{2,1,0:T(8,128)(2,1)}, u32[]{:S(2)}) copy-start(bf16[1,320,256]{2,1,0:T(8,128)(2,1)} %param.16) | copy-start | bytes 491524
  335.0 13.7 %all-to-all-start.1 = ((bf16[16,2,300]{2,1,0:T(2,128)(2,1)}), bf16[16,2,300]{2,1,0:T(2,128)(2,1)S(1)}, u32[]{:S(2)}, u32[]{:S(2)}) async-start(bf16[16,2,300]{2,1,0:T(2,128)(2,1)} %reshape.341), calls=%async_computation.2 | async-start | bytes 49152 | tf_op jit(solution)/shard_map/all_to_all | solution.py:93
  348.6 11.6 %all-to-all-start = ((bf16[16,2,900]{2,1,0:T(2,128)(2,1)}), bf16[16,2,900]{2,1,0:T(2,128)(2,1)S(1)}, u32[]{:S(2)}, u32[]{:S(2)}) async-start(bf16[16,2,900]{2,1,0:T(2,128)(2,1)} %reshape.339), calls=%async_computation.1 | async-start | bytes 131072 | tf_op jit(solution)/shard_map/all_to_all | solution.py:93
Sparse Core Ops, SparseCore 0:
  62.4 91.3 all-gather.3
  209.8 123.4 reduce-scatter.1
where the time goes:
time: 369 us; the launch traced here: 368 us
  blocking collectives  160 us (43%)
  waiting for transfers between devices  66.2 us (18%)
  local copies, waits for them, and re-layouts  66.1 us (18%)
  starting transfers between devices  39.4 us (11%)
  between operations  16.7 us (5%)
  matrix products  9.99 us (3%)
  other arithmetic  9.43 us (3%)
    psum x10, blocking collectives, over_axes(): shard = lax.psum(shard, axis)  107 us
    all_gather x1, blocking collectives, sent_together(): result, at, outs = (lax.all_gather(both, axis, axis=dim, tiled=True), 0, [])  52.7 us
    reduce_scatter x1, waiting for transfers between devices, sum_packed(): lax.psum_scatter(lines, axis, tiled=True).reshape(-1)  41.2 us
    ppermute x4, starting transfers between devices, from_behind(): return lax.ppermute(shard, axis, pairs)  20.7 us
    reshape x2, local copies, waits for them, and re-layouts, gather_together(): tiles = lines[:, at:at + a.size].reshape(-1, *a.shape)  15.3 us
    all_gather x1, waiting for transfers between devices, gather_together(): lines, at, outs = (lax.all_gather(ravelled, axis), 0, [])  12.6 us
    all_to_all x2, waiting for transfers between devices, sent_and_summed(): tiles = lax.all_to_all(cut_along(shard, dim, peers), axis, 0, 0, tiled=True)  12.4 us
    all_to_all x2, starting transfers between devices, sent_and_summed(): tiles = lax.all_to_all(cut_along(shard, dim, peers), axis, 0, 0, tiled=True)  9.18 us
  transfers between devices with their start and end apart: 12, of which 4 were waited for; matrix products, arithmetic and copies ran while one was open for 19% of the time, Pallas kernels for 0%

commit v1 on v0

v1 whole, which is shorter than its diff:
```python
import functools

import jax
import jax.numpy as jnp
from jax import lax
from jax.experimental import pallas as pl
from jax.experimental.pallas import tpu as pltpu
from jax.sharding import Mesh
from jax.sharding import PartitionSpec as P

GROUPS = 32
GROUP_SIZE = 10
CHANNELS = 320
COLUMNS = 16
STRIPS = 32
FRAMES = 16
CELLS = 256
EXT = 384
BELOW = 256
ABOVE = 368
SPAN = 720
SPAN_T = 240
WIDE = 768
PACK = 1024
EPSILON = 1e-05

TILE = ("tile_0", "tile_1", "tile_2")
FRAME = ("frame_0", "frame_1")
ROW_Z = ("frame_1", "tile_1")
PLANE = ("frame_0", "tile_0")
PLANE_CORE = ("frame_0", "tile_0", "tile_2")

bf16 = jnp.bfloat16
f32 = jnp.float32
NT = (((1,), (1,)), ((), ()))


def iota(shape, dim):
    return lax.broadcasted_iota(jnp.int32, shape, dim)


def dot(a, b):
    return jnp.dot(a, b, preferred_element_type=f32)


def dot_nt(a, b):
    return lax.dot_general(a, b, NT, preferred_element_type=f32)


def zero_one(mask):
    return jnp.where(mask, 1.0, 0.0).astype(bf16)


def to_all(value, axes):
    peers = lax.axis_size(axes)
    copies = jnp.broadcast_to(value[None], (peers, *value.shape))
    return lax.all_to_all(copies, axes, 0, 0, tiled=True)


def column_place(z_low):
    source = iota((256, PACK), 0)
    place = iota((256, PACK), 1)
    spatial = (source < 180) & (place == source + z_low * 180)
    temporal = (source >= 180) & (source < 240)
    temporal &= place == source + (WIDE - 180 + z_low * 60)
    return zero_one(spatial | temporal)


def row_place(shape, dim_small, dim_padded):
    small = iota(shape, dim_small)
    padded = iota(shape, dim_padded)
    match = small < 0
    for a in range(4):
        match |= (small >= 10 * a) & (small < 10 * a + 10) & (padded == small + 6 * a)
    return zero_one(match)


def pack_kernel(blocks, out):
    total = jnp.zeros((64, PACK), f32)
    for z_low in range(4):
        total += dot(blocks[z_low], column_place(z_low))
    out[...] = dot(row_place((40, 64), 0, 1), total.astype(bf16)).astype(bf16)


def unpack_kernel(terms, out):
    total = terms[0].astype(f32)
    for n in range(1, 16):
        total += terms[n].astype(f32)
    rows = dot(row_place((64, 40), 1, 0), total.astype(bf16)).astype(bf16)
    for z_low in range(4):
        out[z_low] = dot_nt(rows, column_place(z_low)).astype(bf16)


def stat_columns(stats, group):
    total = jnp.sum(stats[...], axis=0, keepdims=True)
    lane = iota((CHANNELS, 128), 1)

    def pick(mask):
        return jnp.sum(jnp.where(mask, total, 0.0), axis=1, keepdims=True)

    positions = pick(lane == 2 * GROUPS)
    count = positions * GROUP_SIZE
    mean = pick(lane == group) / count
    rstd = lax.rsqrt(pick(lane == group + GROUPS) / count - mean * mean + EPSILON)
    return positions, count, mean, rstd


def turned(row):
    eye = iota((CHANNELS, CHANNELS), 0) == iota((CHANNELS, CHANNELS), 1)
    return jnp.sum(jnp.where(eye, row, 0.0), axis=1, keepdims=True)


def turned_back(column):
    eye = iota((CHANNELS, CHANNELS), 0) == iota((CHANNELS, CHANNELS), 1)
    return jnp.sum(jnp.where(eye, column, 0.0), axis=0, keepdims=True)


def pieces_of(start, stop, span):
    while start < stop:
        end = min(stop, (start // span + 1) * span)
        yield start // span, start % span, start, end - start
        start = end


def main_kernel(
    place, stats, gain, shift, order, order_row, group, latent, g_next, g_here, g_last,
    w_own, w_other, grad_own, grad_other, pre_grad, sums, cols, turned_s, turned_t, frames, taps,
):
    height = place[0]
    strip = place[1]
    lane = iota((1, EXT), 1)
    live = ((lane < CELLS) & ((lane >> 4) < height)) | (
        (lane >= BELOW) & (lane < BELOW + COLUMNS) & (strip < STRIPS - 1)
    ) | ((lane >= ABOVE) & (strip > 0))
    to_packed = zero_one(order[...] == iota((CHANNELS, CHANNELS), 1))
    to_plain = zero_one(iota((CHANNELS, CHANNELS), 0) == order_row[...])

    for y in range(4):
        whole = jnp.concatenate([w_own[y], w_other[y]], axis=0)
        across = whole.T
        turned_s[y * SPAN : (y + 1) * SPAN, :] = across[:SPAN]
        turned_t[y * SPAN_T : (y + 1) * SPAN_T, :] = across[WIDE : WIDE + SPAN_T]

    _, _, mean, rstd = stat_columns(stats, group[...])
    gain_column = turned(gain[...])
    shift_column = turned(shift[...])
    normed = (latent[...].astype(f32) - mean) * rstd
    pre_act = gain_column * normed + shift_column
    sigmoid = 1.0 / (1.0 + jnp.exp(-pre_act))
    active = jnp.where(live, pre_act * sigmoid, 0.0).astype(bf16)

    grad_spat = jnp.zeros((CHANNELS, EXT), f32)
    for k, ref in enumerate((g_next, g_here, g_last)):
        packed = dot(to_packed, ref[...]).astype(bf16)
        taps[:, k * CELLS : (k + 1) * CELLS] = packed[:, :CELLS]
        grad_spat += dot(turned_t[k * CHANNELS : (k + 1) * CHANNELS, :], packed)
    grad_spat = jnp.where(live, grad_spat, 0.0).astype(bf16)
    spat_packed = dot(to_packed, grad_spat).astype(bf16)

    for y in range(4):
        cols[y, SPAN:, :] = jnp.zeros((WIDE - SPAN, CELLS), bf16)
    cell = iota((1, CELLS), 1)
    source = iota((EXT, CELLS), 0)
    grad_act = jnp.zeros((CHANNELS, CELLS), f32)
    for k in range(9):
        row = (cell >> 4) + (k // 3 - 1)
        column = (cell & 15) + (k % 3 - 1)
        base = jnp.where(row < 0, ABOVE, jnp.where(row == height, BELOW, row * COLUMNS))
        wanted = jnp.where((column >= 0) & (column < COLUMNS), base + column, -1)
        move = zero_one(source == wanted)
        moved = dot(active, move).astype(bf16)
        for y, at, start, size in pieces_of(k * CHANNELS, (k + 1) * CHANNELS, SPAN):
            first = start - k * CHANNELS
            cols[y, at : at + size, :] = moved[first : first + size]
        back = 8 - k
        grad_act += dot(
            turned_s[back * CHANNELS : (back + 1) * CHANNELS, :],
            dot(spat_packed, move).astype(bf16),
        )

    spatial = jnp.zeros((CHANNELS, CELLS), f32)
    left = spat_packed[:, :CELLS]
    for y in range(4):
        whole = jnp.concatenate([w_own[y, :, :WIDE], w_other[y, :, :WIDE]], axis=0)
        spatial += dot(whole, cols[y])
        part = dot_nt(left, cols[y]).astype(bf16)
        grad_own[y, :, :WIDE] = part[:160]
        grad_other[y, :, :WIDE] = part[160:]
    own_live = live[:, :CELLS]
    spatial = jnp.where(own_live, spatial, 0.0).astype(bf16)
    spatial = dot(to_plain, spatial).astype(bf16)

    frames[...] = jnp.zeros(frames.shape, bf16)
    for k in range(3):
        for y, at, start, size in pieces_of(k * CHANNELS, (k + 1) * CHANNELS, SPAN_T):
            first = start - k * CHANNELS
            frames[y, at : at + size, k * CELLS : (k + 1) * CELLS] = spatial[first : first + size]
    for y in range(4):
        part = dot_nt(taps[...], frames[y]).astype(bf16)
        grad_own[y, :, WIDE:] = part[:160]
        grad_other[y, :, WIDE:] = part[160:]

    act = pre_act[:, :CELLS]
    sig = sigmoid[:, :CELLS]
    grad_pre = jnp.where(own_live, grad_act * sig * (1.0 + act * (1.0 - sig)), 0.0)
    pre_grad[...] = grad_pre
    chan_gain = jnp.sum(grad_pre * normed[:, :CELLS], axis=1, keepdims=True)
    chan_shift = jnp.sum(grad_pre, axis=1, keepdims=True)
    sums[...] = jnp.zeros(sums.shape, f32)
    sums[:, :CHANNELS] = turned_back(chan_gain)
    sums[:, EXT : EXT + CHANNELS] = turned_back(chan_shift)


def input_kernel(
    place, stats, gain, group, group_row, latent, g_here, pre_grad, sums, result, totals
):
    height = place[0]
    own_live = (iota((1, CELLS), 1) >> 4) < height
    positions, count, mean, rstd = stat_columns(stats, group[...])
    total = jnp.sum(sums[...], axis=0, keepdims=True)
    scale = lax.rsqrt(positions[:1, :1])
    totals[...] = total * scale
    same = group[...] == group_row[...]

    def over_group(row):
        return jnp.sum(jnp.where(same, gain[...] * row, 0.0), axis=1, keepdims=True) / count

    gain_sum = over_group(total[:, :CHANNELS])
    shift_sum = over_group(total[:, EXT : EXT + CHANNELS])
    normed = (latent[:, :CELLS].astype(f32) - mean) * rstd
    value = g_here[:, :CELLS].astype(f32) + rstd * (
        turned(gain[...]) * pre_grad[...] - shift_sum - normed * gain_sum
    )
    result[...] = jnp.where(own_live, value, 0.0).astype(bf16)


def call(kernel, outs, smem=0, scratch=(), inputs=1, flops=0, moved=0):
    vmem = pl.BlockSpec(memory_space=pltpu.VMEM)
    specs = [pl.BlockSpec(memory_space=pltpu.SMEM)] * smem + [vmem] * (inputs - smem)
    many = isinstance(outs, tuple)
    return pl.pallas_call(
        kernel,
        out_shape=outs,
        in_specs=specs,
        out_specs=tuple(vmem for _ in outs) if many else vmem,
        scratch_shapes=list(scratch),
        compiler_params=pltpu.CompilerParams(vmem_limit_bytes=48 << 20),
        cost_estimate=pl.CostEstimate(flops=flops, bytes_accessed=moved, transcendentals=0),
    )


def shape(dims, kind):
    return jax.ShapeDtypeStruct(dims, kind)


def step_by(value, axes, by):
    peers = lax.axis_size(axes)
    pairs = [(i, i + by) for i in range(peers) if 0 <= i + by < peers]
    return lax.ppermute(value, axes, pairs)


def swap_cores(value):
    return lax.ppermute(value, "tile_2", [(0, 1), (1, 0)])


def extended(own, above, below):
    gap = jnp.zeros((CHANNELS, ABOVE - BELOW - COLUMNS), own.dtype)
    return jnp.concatenate([own, below, gap, above], axis=1)


def local(latents, out_grad, w_spatial, w_temporal, norm_gain, norm_shift, heights):
    height = heights[0]
    core = lax.axis_index("tile_2")
    strip = lax.axis_index(TILE)
    place = jnp.stack([height, strip]).astype(jnp.int32)
    live = (jnp.arange(CELLS, dtype=jnp.int32) // COLUMNS < height)[None, :]
    latent = latents[0]
    grad = jnp.where(live, out_grad[0], jnp.zeros((), bf16))

    shard = jnp.concatenate([w_spatial, w_temporal], axis=1)
    shard = jnp.pad(shard, ((0, 6), (0, 16)))
    near = to_all(shard, ROW_Z).reshape(4, 64, 256)
    packed = call(pack_kernel, shape((40, PACK), bf16), flops=1 << 27, moved=1 << 18)(near)
    w_own = to_all(packed, PLANE).reshape(4, 160, PACK)
    w_other = swap_cores(w_own)

    wide = jnp.where(live, latent, jnp.zeros((), bf16)).astype(f32)
    chan_sum = jnp.sum(wide, axis=1)
    chan_square = jnp.sum(wide * wide, axis=1)
    own_stats = jnp.concatenate(
        [
            chan_sum.reshape(GROUPS, GROUP_SIZE).sum(1),
            chan_square.reshape(GROUPS, GROUP_SIZE).sum(1),
            (height * COLUMNS).astype(f32)[None],
            jnp.zeros((63,), f32),
        ]
    )[None]
    stats = jnp.sum(to_all(own_stats, ROW_Z), axis=0)
    stats = to_all(stats, PLANE_CORE)[:, 0]

    both = jnp.stack([latent, grad])
    tall = height == 16
    last = jnp.where(tall, both[:, :, 240:256], both[:, :, 112:128])
    above = step_by(last, TILE, 1)
    below = step_by(both[:, :, :COLUMNS], TILE, -1)
    latent_ext = extended(latent, above[0], below[0])
    grad_ext = extended(grad, above[1], below[1])
    grad_last = step_by(grad_ext, FRAME, 1)
    grad_next = step_by(grad_ext, FRAME, -1)

    packed_row = jnp.arange(CHANNELS, dtype=jnp.int32)
    half, rest = packed_row // 160, packed_row % 160
    order = rest // 40 * 80 + rest % 40 // 10 * 20 + rest % 10
    order = order + jnp.where(half == 0, core, 1 - core) * 10
    group = jnp.arange(CHANNELS, dtype=jnp.int32) // GROUP_SIZE
    gain_row, shift_row = norm_gain[None], norm_shift[None]
    block = shape((4, 160, PACK), bf16)
    grad_own, grad_other, pre_grad, sums = call(
        main_kernel,
        (block, block, shape((CHANNELS, CELLS), f32), shape((1, 2 * EXT), f32)),
        smem=1,
        inputs=13,
        scratch=(
            pltpu.VMEM((4, WIDE, CELLS), bf16),
            pltpu.VMEM((4 * SPAN, CHANNELS), bf16),
            pltpu.VMEM((4 * SPAN_T, CHANNELS), bf16),
            pltpu.VMEM((4, CELLS, 3 * CELLS), bf16),
            pltpu.VMEM((CHANNELS, 3 * CELLS), bf16),
        ),
        flops=5 << 30,
        moved=8 << 20,
    )(
        place, stats, gain_row, shift_row, order[:, None], order[None, :], group[:, None],
        latent_ext, grad_next, grad_ext, grad_last, w_own, w_other,
    )

    chan = jnp.sum(to_all(sums, ROW_Z), axis=0)
    chan = to_all(chan, PLANE_CORE)[:, 0]
    grad_input, totals = call(
        input_kernel,
        (shape((CHANNELS, CELLS), bf16), shape((1, 2 * EXT), f32)),
        smem=1,
        inputs=9,
        flops=1 << 22,
        moved=1 << 20,
    )(
        place, stats, gain_row, group[:, None], group[None, :], latent_ext, grad_ext,
        pre_grad, chan,
    )

    pair = grad_own.astype(f32) + swap_cores(grad_other).astype(f32)
    terms = lax.all_to_all(
        pair.astype(bf16).reshape(16, 40, PACK), PLANE, 0, 0, tiled=True
    )
    parts = call(unpack_kernel, shape((4, 64, 256), bf16), flops=1 << 27, moved=1 << 21)(terms)
    mine = lax.all_to_all(parts.reshape(16, 16, 256), ROW_Z, 0, 0, tiled=True)
    scale = lax.rsqrt(jnp.sum(stats[:, 2 * GROUPS]))
    mine = jnp.sum(mine.astype(f32), axis=0) * scale
    return (
        grad_input[None],
        mine[:10, :180],
        mine[:10, 180:240],
        totals[0, :CHANNELS],
        totals[0, EXT : EXT + CHANNELS],
    )


def solution(mesh):
    split = Mesh(
        mesh.devices.reshape(4, 4, 4, 4, 2), ("frame_0", "frame_1", "tile_0", "tile_1", "tile_2")
    )
    placed = (
        P(FRAME, None, TILE),
        P(FRAME, None, TILE),
        P(TILE, FRAME),
        P(TILE, FRAME),
        P(),
        P(),
        P(TILE),
    )
    return jax.shard_map(
        local,
        mesh=split,
        in_specs=placed,
        out_specs=(P(FRAME, None, TILE), P(TILE, FRAME), P(TILE, FRAME), P(), P()),
        check_vma=False,
    )
```

time: 369 us -> 183 us (0.50)
  the two profiles are of different devices: /device:TPU:4 before, /device:TPU:32 now
where the time goes in v1:
time: 183 us; the launch traced here: 182 us
  waiting for transfers between devices  73.3 us (40%)
  starting transfers between devices  50.4 us (28%)
  blocking collectives  29.8 us (16%)
  Pallas kernels  12.3 us (7%)
  local copies, waits for them, and re-layouts  9.43 us (5%)
  other arithmetic  4.61 us (3%)
  between operations  2.28 us (1%)
    all_to_all x5, waiting for transfers between devices, to_all(): return lax.all_to_all(copies, axes, 0, 0, tiled=True)  41.8 us
    all_to_all x1, blocking collectives, to_all(): return lax.all_to_all(copies, axes, 0, 0, tiled=True)  29.8 us
    all_to_all x5, starting transfers between devices, to_all(): return lax.all_to_all(copies, axes, 0, 0, tiled=True)  28.1 us
    all_to_all x1, waiting for transfers between devices, local(): lax.all_to_all(pair.astype(bf16).reshape(16, 40, PACK), PLANE, 0, 0, tile...  20.4 us
    all_to_all x1, waiting for transfers between devices, local(): mine = lax.all_to_all(parts.reshape(16, 16, 256), ROW_Z, 0, 0, tiled=True)  11.1 us
    ppermute x4, starting transfers between devices, step_by(): return lax.ppermute(value, axes, pairs)  10.2 us
    pallas_call x1, Pallas kernels, local(): call(main_kernel, (block, block, shape((CHANNELS, CELLS), f32), shape((1,...  8.55 us
    all_to_all x1, starting transfers between devices, local(): mine = lax.all_to_all(parts.reshape(16, 16, 256), ROW_Z, 0, 0, tiled=True)  4.61 us
  transfers between devices with their start and end apart: 13, of which 7 were waited for; matrix products, arithmetic and copies ran while one was open for 4% of the time, Pallas kernels for 2%

profile of v1, /device:TPU:32, one launch (start us, length us, event | category | flops | bytes accessed | tf_op | source)
XLA Modules:
  0.0 182.2 jit_solution(13541063520240077752)
XLA Ops:
  1.4 29.8 %all_to_all.40 = bf16[16,16,256]{2,1,0:T(8,128)(2,1)S(1)} all-to-all(bf16[16,16,256]{2,1,0:T(8,128)(2,1)S(1)} %broadcast_in_dim.104), channel_id=1, replica_groups=mesh['frame_0'=4,'frame_1'=4,'tile_0'=4,'tile_1'=4,'tile_2'=2] {'frame_1..., dimensions={0} | all-to-all | bytes 262144 | tf_op jit(solution)/shard_map/all_to_all | solution.py:57
  32.9 7.2 %all-to-all-start.3 = ((bf16[16,40,1024]{2,1,0:T(8,128)(2,1)}), bf16[16,40,1024]{2,1,0:T(8,128)(2,1)S(1)}, u32[]{:S(2)}, u32[]{:S(2)}) async-start(bf16[16,40,1024]{2,1,0:T(8,128)(2,1)} %broadcast_in_dim.105), calls=%async_computation.3 | async-start | bytes 2621440 | tf_op jit(solution)/shard_map/all_to_all | solution.py:57
  42.3 3.0 %collective-permute-start.1 = (bf16[2,320,16]{2,1,0:T(8,128)(2,1)S(1)}, bf16[2,320,16]{2,1,0:T(8,128)(2,1)S(1)}, u32[]{:S(2)}, u32[]{:S(2)}) collective-permute-start(bf16[2,320,16]{2,1,0:T(8,128)(2,1)S(1)} %get-tuple-element.22), channel_id=1, source_target_pairs={{0,1},{1,2},{2,3},{3,4},{4,5},{5,6},{6,7},{7,8},{8,9},{9,10},{10,1... | collective-permute-start | bytes 61448 | tf_op jit(solution)/shard_map/ppermute | solution.py:259
  46.0 13.5 %all-to-all-done.3 = bf16[16,40,1024]{2,1,0:T(8,128)(2,1)S(1)} async-done(((bf16[16,40,1024]{2,1,0:T(8,128)(2,1)}), bf16[16,40,1024]{2,1,0:T(8,128)(2,1)S(1)}, u32[]{:S(2)}, u32[]{:S(2)}) %all-to-all-start.3) | async-done | bytes 1310752 | tf_op jit(solution)/shard_map/all_to_all | solution.py:57
  59.5 1.9 %collective-permute-start.4 = (bf16[4,160,1024]{2,1,0:T(8,128)(2,1)S(1)}, bf16[4,160,1024]{2,1,0:T(8,128)(2,1)}, u32[]{:S(2)}, u32[]{:S(2)}) collective-permute-start(bf16[4,160,1024]{2,1,0:T(8,128)(2,1)S(1)} %bitcast.30), channel_id=1, source_target_pairs={{0,1},{1,0},{2,3},{3,2},{4,5},{5,4},{6,7},{7,6},{8,9},{9,8},{10,11... | collective-permute-start | bytes 3932168 | tf_op jit(solution)/shard_map/ppermute | solution.py:263
  62.1 5.1 %all-to-all-start = ((f32[16,1,128]{2,1,0:T(1,128)}), f32[16,1,128]{2,1,0:T(1,128)S(1)}, u32[]{:S(2)}, u32[]{:S(2)}) async-start(f32[16,1,128]{2,1,0:T(1,128)} %broadcast_in_dim.94), calls=%async_computation | async-start | bytes 16384 | tf_op jit(solution)/shard_map/all_to_all | solution.py:57
  67.5 2.0 %collective-permute-start.2 = (bf16[320,384]{1,0:T(8,128)(2,1)S(1)}, bf16[320,384]{1,0:T(8,128)(2,1)S(1)}, u32[]{:S(2)}, u32[]{:S(2)}) collective-permute-start(bf16[320,384]{1,0:T(8,128)(2,1)S(1)} %get-tuple-element.27.g_here), channel_id=1, source_target_pairs={{32,0},{64,32},{96,64},{128,96},{160,128},{192,160},{224,192},{256... | collective-permute-start | bytes 737288 | tf_op jit(solution)/shard_map/ppermute | solution.py:259
  69.6 3.8 %collective-permute-start.3 = (bf16[320,384]{1,0:T(8,128)(2,1)S(1)}, bf16[320,384]{1,0:T(8,128)(2,1)S(1)}, u32[]{:S(2)}, u32[]{:S(2)}) collective-permute-start(bf16[320,384]{1,0:T(8,128)(2,1)S(1)} %get-tuple-element.27.g_here), channel_id=1, source_target_pairs={{0,32},{32,64},{64,96},{96,128},{128,160},{160,192},{192,224},{224... | collective-permute-start | bytes 737288 | tf_op jit(solution)/shard_map/ppermute | solution.py:259
  73.9 4.5 %all-to-all-done = f32[16,1,128]{2,1,0:T(1,128)S(1)} async-done(((f32[16,1,128]{2,1,0:T(1,128)}), f32[16,1,128]{2,1,0:T(1,128)S(1)}, u32[]{:S(2)}, u32[]{:S(2)}) %all-to-all-start) | async-done | bytes 8224 | tf_op jit(solution)/shard_map/all_to_all | solution.py:57
  79.0 3.8 %all-to-all-start.1 = ((f32[32,1,128]{2,1,0:T(1,128)}), f32[32,1,128]{2,1,0:T(1,128)S(1)}, u32[]{:S(2)}, u32[]{:S(2)}) async-start(f32[32,1,128]{2,1,0:T(1,128)} %broadcast_in_dim.95), calls=%async_computation.1 | async-start | bytes 32768 | tf_op jit(solution)/shard_map/all_to_all | solution.py:57
  83.0 7.2 %all-to-all-done.1 = f32[32,1,128]{2,1,0:T(1,128)S(1)} async-done(((f32[32,1,128]{2,1,0:T(1,128)}), f32[32,1,128]{2,1,0:T(1,128)S(1)}, u32[]{:S(2)}, u32[]{:S(2)}) %all-to-all-start.1) | async-done | bytes 16416 | tf_op jit(solution)/shard_map/all_to_all | solution.py:57
  93.5 8.5 %shard_map.111 = (bf16[4,160,1024]{2,1,0:T(8,128)(2,1)S(1)}, bf16[4,160,1024]{2,1,0:T(8,128)(2,1)}, f32[320,256]{1,0:T(8,128)S(1)}, f32[1,768]{1,0:T(1,128)S(1)}) custom-call(s32[2]{0:T(128)S(1)} %pad_add_fusion.place, f32[32,128]{1,0:T(8,128)S(1)} %bitcast.33, f32[1,320]{1,0:T(1,128)S(1)} %broadcast_in_dim.96.gain, f32[1,320]{1,0:T(1,128)S(1)} %broadcast_in_dim.99.shift, ...), custom_call_target="tpu_custom_call" | custom-call | flops 5368709120 | bytes 8388608 | tf_op jit(solution)/shard_map/pallas_call | solution.py:318
  102.7 1.9 %collective-permute-start.5 = (bf16[4,160,1024]{2,1,0:T(8,128)(2,1)}, bf16[4,160,1024]{2,1,0:T(8,128)(2,1)S(1)}, u32[]{:S(2)}, u32[]{:S(2)}) collective-permute-start(bf16[4,160,1024]{2,1,0:T(8,128)(2,1)} %get-tuple-element.15), channel_id=1, source_target_pairs={{0,1},{1,0},{2,3},{3,2},{4,5},{5,4},{6,7},{7,6},{8,9},{9,8},{10,11... | collective-permute-start | bytes 3932168 | tf_op jit(solution)/shard_map/ppermute | solution.py:263
  105.3 8.1 %all-to-all-start.4 = ((f32[16,1,768]{2,1,0:T(1,128)}), f32[16,1,768]{2,1,0:T(1,128)S(1)}, u32[]{:S(2)}, u32[]{:S(2)}) async-start(f32[16,1,768]{2,1,0:T(1,128)} %broadcast_in_dim.107), calls=%async_computation.4 | async-start | bytes 98304 | tf_op jit(solution)/shard_map/all_to_all | solution.py:57
  113.5 1.6 add_convert_fusion
  115.1 10.5 %all-to-all-done.4 = f32[16,1,768]{2,1,0:T(1,128)S(1)} async-done(((f32[16,1,768]{2,1,0:T(1,128)}), f32[16,1,768]{2,1,0:T(1,128)S(1)}, u32[]{:S(2)}, u32[]{:S(2)}) %all-to-all-start.4) | async-done | bytes 49184 | tf_op jit(solution)/shard_map/all_to_all | solution.py:57
  125.5 3.7 %all-to-all-start.6 = ((bf16[16,40,1024]{2,1,0:T(8,128)(2,1)}), bf16[16,40,1024]{2,1,0:T(8,128)(2,1)S(1)}, u32[]{:S(2)}, u32[]{:S(2)}) async-start(bf16[16,40,1024]{2,1,0:T(8,128)(2,1)} %bitcast.14), calls=%async_computation.6 | async-start | bytes 2621440 | tf_op jit(solution)/shard_map/all_to_all | solution.py:352
  129.3 20.4 %all-to-all-done.6.terms = bf16[16,40,1024]{2,1,0:T(8,128)(2,1)S(1)} async-done(((bf16[16,40,1024]{2,1,0:T(8,128)(2,1)}), bf16[16,40,1024]{2,1,0:T(8,128)(2,1)S(1)}, u32[]{:S(2)}, u32[]{:S(2)}) %all-to-all-start.6) | async-done | bytes 1310752 | tf_op jit(solution)/shard_map/all_to_all | solution.py:352
  150.4 3.9 %all-to-all-start.5 = ((f32[32,1,768]{2,1,0:T(1,128)}), f32[32,1,768]{2,1,0:T(1,128)S(1)}, u32[]{:S(2)}, u32[]{:S(2)}) async-start(f32[32,1,768]{2,1,0:T(1,128)} %broadcast_in_dim.108), calls=%async_computation.5 | async-start | bytes 196608 | tf_op jit(solution)/shard_map/all_to_all | solution.py:57
  154.2 1.4 shard_map.113
  155.6 6.2 %all-to-all-done.5 = f32[32,1,768]{2,1,0:T(1,128)S(1)} async-done(((f32[32,1,768]{2,1,0:T(1,128)}), f32[32,1,768]{2,1,0:T(1,128)S(1)}, u32[]{:S(2)}, u32[]{:S(2)}) %all-to-all-start.5) | async-done | bytes 98336 | tf_op jit(solution)/shard_map/all_to_all | solution.py:57
  161.8 4.6 %all-to-all-start.7 = ((bf16[16,16,256]{2,1,0:T(8,128)(2,1)}), bf16[16,16,256]{2,1,0:T(8,128)(2,1)S(1)}, u32[]{:S(2)}, u32[]{:S(2)}) async-start(bf16[16,16,256]{2,1,0:T(8,128)(2,1)} %bitcast.15), calls=%async_computation.7 | async-start | bytes 262144 | tf_op jit(solution)/shard_map/all_to_all | solution.py:356
  167.8 1.9 %shard_map.112 = (bf16[320,256]{1,0:T(8,128)(2,1)}, f32[1,768]{1,0:T(1,128)S(1)}) custom-call(s32[2]{0:T(128)S(1)} %pad_add_fusion.place, f32[32,128]{1,0:T(8,128)S(1)} %bitcast.35, f32[1,320]{1,0:T(1,128)S(1)} %broadcast_in_dim.96.gain, s32[320,1]{1,0:T(8,128)S(1)} %get-tuple-element.29.group, s32[1,320]{1,0:T(1,128)S(1)} %and_select_fusion.6.group_row, ...), custom_call_target="tpu_custom_call" | custom-call | flops 4194304 | bytes 1048576 | tf_op jit(solution)/shard_map/pallas_call | solution.py:339
  170.3 11.1 %all-to-all-done.7 = bf16[16,16,256]{2,1,0:T(8,128)(2,1)S(1)} async-done(((bf16[16,16,256]{2,1,0:T(8,128)(2,1)}), bf16[16,16,256]{2,1,0:T(8,128)(2,1)S(1)}, u32[]{:S(2)}, u32[]{:S(2)}) %all-to-all-start.7) | async-done | bytes 131104 | tf_op jit(solution)/shard_map/all_to_all | solution.py:356
  (68 shorter events, 14.2 us)
Async XLA Ops:
  32.9 7.8 %copy-start.7 = (bf16[1,320,256]{2,1,0:T(8,128)(2,1)S(1)}, bf16[1,320,256]{2,1,0:T(8,128)(2,1)}, u32[]{:S(2)}) copy-start(bf16[1,320,256]{2,1,0:T(8,128)(2,1)} %param.8) | copy-start | bytes 491524
  32.9 7.9 %copy-start.6 = (bf16[1,320,256]{2,1,0:T(8,128)(2,1)S(1)}, bf16[1,320,256]{2,1,0:T(8,128)(2,1)}, u32[]{:S(2)}) copy-start(bf16[1,320,256]{2,1,0:T(8,128)(2,1)} %param.7) | copy-start | bytes 491524
  32.9 26.5 %all-to-all-start.3 = ((bf16[16,40,1024]{2,1,0:T(8,128)(2,1)}), bf16[16,40,1024]{2,1,0:T(8,128)(2,1)S(1)}, u32[]{:S(2)}, u32[]{:S(2)}) async-start(bf16[16,40,1024]{2,1,0:T(8,128)(2,1)} %broadcast_in_dim.105), calls=%async_computation.3 | async-start | bytes 2621440 | tf_op jit(solution)/shard_map/all_to_all | solution.py:57
  41.0 26.3 %collective-permute-start = (bf16[2,320,16]{2,1,0:T(8,128)(2,1)S(1)}, bf16[2,320,16]{2,1,0:T(8,128)(2,1)S(1)}, u32[]{:S(2)}, u32[]{:S(2)}) collective-permute-start(bf16[2,320,16]{2,1,0:T(8,128)(2,1)S(1)} %get-tuple-element.21), channel_id=1, source_target_pairs={{1,0},{2,1},{3,2},{4,3},{5,4},{6,5},{7,6},{8,7},{9,8},{10,9},{11,1... | collective-permute-start | bytes 61448 | tf_op jit(solution)/shard_map/ppermute | solution.py:259
  42.3 25.0 %collective-permute-start.1 = (bf16[2,320,16]{2,1,0:T(8,128)(2,1)S(1)}, bf16[2,320,16]{2,1,0:T(8,128)(2,1)S(1)}, u32[]{:S(2)}, u32[]{:S(2)}) collective-permute-start(bf16[2,320,16]{2,1,0:T(8,128)(2,1)S(1)} %get-tuple-element.22), channel_id=1, source_target_pairs={{0,1},{1,2},{2,3},{3,4},{4,5},{5,6},{6,7},{7,8},{8,9},{9,10},{10,1... | collective-permute-start | bytes 61448 | tf_op jit(solution)/shard_map/ppermute | solution.py:259
  45.9 37.1 %copy-start.9 = (f32[320]{0:T(512)S(1)}, f32[320]{0:T(512)}, u32[]{:S(2)}) copy-start(f32[320]{0:T(512)} %param.11) | copy-start | bytes 3844
  46.0 37.0 %copy-start.10 = (f32[320]{0:T(512)S(1)}, f32[320]{0:T(512)}, u32[]{:S(2)}) copy-start(f32[320]{0:T(512)} %param.12) | copy-start | bytes 3844
  59.5 32.1 %collective-permute-start.4 = (bf16[4,160,1024]{2,1,0:T(8,128)(2,1)S(1)}, bf16[4,160,1024]{2,1,0:T(8,128)(2,1)}, u32[]{:S(2)}, u32[]{:S(2)}) collective-permute-start(bf16[4,160,1024]{2,1,0:T(8,128)(2,1)S(1)} %bitcast.30), channel_id=1, source_target_pairs={{0,1},{1,0},{2,3},{3,2},{4,5},{5,4},{6,7},{7,6},{8,9},{9,8},{10,11... | collective-permute-start | bytes 3932168 | tf_op jit(solution)/shard_map/ppermute | solution.py:263
  62.1 16.3 %all-to-all-start = ((f32[16,1,128]{2,1,0:T(1,128)}), f32[16,1,128]{2,1,0:T(1,128)S(1)}, u32[]{:S(2)}, u32[]{:S(2)}) async-start(f32[16,1,128]{2,1,0:T(1,128)} %broadcast_in_dim.94), calls=%async_computation | async-start | bytes 16384 | tf_op jit(solution)/shard_map/all_to_all | solution.py:57
  67.5 22.6 %collective-permute-start.2 = (bf16[320,384]{1,0:T(8,128)(2,1)S(1)}, bf16[320,384]{1,0:T(8,128)(2,1)S(1)}, u32[]{:S(2)}, u32[]{:S(2)}) collective-permute-start(bf16[320,384]{1,0:T(8,128)(2,1)S(1)} %get-tuple-element.27.g_here), channel_id=1, source_target_pairs={{32,0},{64,32},{96,64},{128,96},{160,128},{192,160},{224,192},{256... | collective-permute-start | bytes 737288 | tf_op jit(solution)/shard_map/ppermute | solution.py:259
  69.6 21.3 %collective-permute-start.3 = (bf16[320,384]{1,0:T(8,128)(2,1)S(1)}, bf16[320,384]{1,0:T(8,128)(2,1)S(1)}, u32[]{:S(2)}, u32[]{:S(2)}) collective-permute-start(bf16[320,384]{1,0:T(8,128)(2,1)S(1)} %get-tuple-element.27.g_here), channel_id=1, source_target_pairs={{0,32},{32,64},{64,96},{96,128},{128,160},{160,192},{192,224},{224... | collective-permute-start | bytes 737288 | tf_op jit(solution)/shard_map/ppermute | solution.py:259
  79.0 11.1 %all-to-all-start.1 = ((f32[32,1,128]{2,1,0:T(1,128)}), f32[32,1,128]{2,1,0:T(1,128)S(1)}, u32[]{:S(2)}, u32[]{:S(2)}) async-start(f32[32,1,128]{2,1,0:T(1,128)} %broadcast_in_dim.95), calls=%async_computation.1 | async-start | bytes 32768 | tf_op jit(solution)/shard_map/all_to_all | solution.py:57
  90.2 0.7 copy-start.2
  90.9 0.7 copy-start.4
  91.6 0.9 copy-start.3
  92.5 0.9 copy-start.5
  102.0 0.7 copy-start
  102.7 10.7 %collective-permute-start.5 = (bf16[4,160,1024]{2,1,0:T(8,128)(2,1)}, bf16[4,160,1024]{2,1,0:T(8,128)(2,1)S(1)}, u32[]{:S(2)}, u32[]{:S(2)}) collective-permute-start(bf16[4,160,1024]{2,1,0:T(8,128)(2,1)} %get-tuple-element.15), channel_id=1, source_target_pairs={{0,1},{1,0},{2,3},{3,2},{4,5},{5,4},{6,7},{7,6},{8,9},{9,8},{10,11... | collective-permute-start | bytes 3932168 | tf_op jit(solution)/shard_map/ppermute | solution.py:263
  105.3 20.2 %all-to-all-start.4 = ((f32[16,1,768]{2,1,0:T(1,128)}), f32[16,1,768]{2,1,0:T(1,128)S(1)}, u32[]{:S(2)}, u32[]{:S(2)}) async-start(f32[16,1,768]{2,1,0:T(1,128)} %broadcast_in_dim.107), calls=%async_computation.4 | async-start | bytes 98304 | tf_op jit(solution)/shard_map/all_to_all | solution.py:57
  125.5 24.2 %all-to-all-start.6 = ((bf16[16,40,1024]{2,1,0:T(8,128)(2,1)}), bf16[16,40,1024]{2,1,0:T(8,128)(2,1)S(1)}, u32[]{:S(2)}, u32[]{:S(2)}) async-start(bf16[16,40,1024]{2,1,0:T(8,128)(2,1)} %bitcast.14), calls=%async_computation.6 | async-start | bytes 2621440 | tf_op jit(solution)/shard_map/all_to_all | solution.py:352
  129.2 38.6 %copy-start.1 = (f32[320,256]{1,0:T(8,128)S(1)}, f32[320,256]{1,0:T(8,128)}, u32[]{:S(2)}) copy-start(f32[320,256]{1,0:T(8,128)} %copy-done) | copy-start | bytes 983044
  150.4 11.4 %all-to-all-start.5 = ((f32[32,1,768]{2,1,0:T(1,128)}), f32[32,1,768]{2,1,0:T(1,128)S(1)}, u32[]{:S(2)}, u32[]{:S(2)}) async-start(f32[32,1,768]{2,1,0:T(1,128)} %broadcast_in_dim.108), calls=%async_computation.5 | async-start | bytes 196608 | tf_op jit(solution)/shard_map/all_to_all | solution.py:57
  161.8 19.7 %all-to-all-start.7 = ((bf16[16,16,256]{2,1,0:T(8,128)(2,1)}), bf16[16,16,256]{2,1,0:T(8,128)(2,1)S(1)}, u32[]{:S(2)}, u32[]{:S(2)}) async-start(bf16[16,16,256]{2,1,0:T(8,128)(2,1)} %bitcast.15), calls=%async_computation.7 | async-start | bytes 262144 | tf_op jit(solution)/shard_map/all_to_all | solution.py:356
  181.5 0.7 copy-start.8

commit v2 on v1

--- a/solution.py
+++ b/solution.py
@@ -23,6 +23,9 @@
 WIDE = 768
 PACK = 1024
 EPSILON = 1e-05
+SPARE = 10
+TILE_AT = 640
+FREE = 80
 
 TILE = ("tile_0", "tile_1", "tile_2")
 FRAME = ("frame_0", "frame_1")
@@ -51,10 +54,8 @@
     return jnp.where(mask, 1.0, 0.0).astype(bf16)
 
 
-def to_all(value, axes):
-    peers = lax.axis_size(axes)
-    copies = jnp.broadcast_to(value[None], (peers, *value.shape))
-    return lax.all_to_all(copies, axes, 0, 0, tiled=True)
+def exchange(blocks, axes):
+    return lax.all_to_all(blocks, axes, 0, 0, tiled=True)
 
 
 def column_place(z_low):
@@ -75,34 +76,137 @@
     return zero_one(match)
 
 
+def rounded(value):
+    return value.astype(bf16).astype(f32)
+
+
+def pieces_in(value):
+    first = rounded(value)
+    second = rounded(value - first)
+    return first, second, rounded(value - first - second)
+
+
+def with_tile(block, tile):
+    return jnp.concatenate([block[:, :TILE_AT], tile, block[:, WIDE:]], axis=1)
+
+
+def start_kernel(place, latent, group, shard, out):
+    height = place[0]
+    live = (iota((1, CELLS), 1) >> 4) < height
+    value = jnp.where(live, latent[...].astype(f32), 0.0)
+    chan_sum = jnp.sum(value, axis=1, keepdims=True)
+    chan_square = jnp.sum(value * value, axis=1, keepdims=True)
+    lane = iota((CHANNELS, 128), 1)
+    terms = jnp.where(lane == group[...], chan_sum, 0.0)
+    terms += jnp.where(lane == group[...] + GROUPS, chan_square, 0.0)
+    cells = (height * COLUMNS).astype(f32)
+    stats = jnp.sum(terms, axis=0, keepdims=True)
+    stats += jnp.where(iota((1, 128), 1) == 2 * GROUPS, cells, 0.0)
+    row = iota((16, 128), 0)
+    extra = jnp.zeros((16, 128), f32)
+    for n, piece in enumerate(pieces_in(stats)):
+        extra += jnp.where(row == SPARE + n, piece, 0.0)
+    extra = jnp.concatenate([extra, jnp.zeros((16, 128), f32)], axis=1)
+    block = (shard[...].astype(f32) + extra).astype(bf16)
+    for n in range(16):
+        out[n] = block
+
+
 def pack_kernel(blocks, out):
     total = jnp.zeros((64, PACK), f32)
+    stats = jnp.zeros((64, 128), f32)
     for z_low in range(4):
         total += dot(blocks[z_low], column_place(z_low))
-    out[...] = dot(row_place((40, 64), 0, 1), total.astype(bf16)).astype(bf16)
+        stats += blocks[z_low, :, :128].astype(f32)
+    packed = dot(row_place((40, 64), 0, 1), total.astype(bf16))
+    row = iota((64, 128), 0) & 15
+    stats = jnp.where((row >= SPARE) & (row < SPARE + 3), stats, 0.0)
+    stats = jnp.sum(stats, axis=0, keepdims=True)
+    line = iota((40, 128), 0)
+    lane = iota((40, 128), 1)
+    wanted = (line, line + GROUPS, 0 * line + 2 * GROUPS)
+    tile = packed[:, TILE_AT:WIDE]
+    for q in range(3):
+        mask = (lane == wanted[q]) & ((line < GROUPS) | (q == 2))
+        column = jnp.sum(jnp.where(mask, stats, 0.0), axis=1, keepdims=True)
+        for n, piece in enumerate(pieces_in(column)):
+            tile += jnp.where(lane == FREE + 3 * q + n, piece, 0.0)
+    packed = with_tile(packed, tile).astype(bf16)
+    for n in range(16):
+        out[n] = packed
+
+
+def stat_columns(w_own, w_other, group):
+    halves = []
+    for ref in (w_own, w_other):
+        half = jnp.zeros((40, 128), f32)
+        for y in range(4):
+            tile = ref[y, :, TILE_AT:WIDE].astype(f32).reshape(4, 40, 128)
+            half += tile[0] + tile[1] + tile[2] + tile[3]
+        halves.append(half)
+    total = halves[0] + halves[1]
+    line = iota((40, 128), 0)
+    lane = iota((40, 128), 1)
+
+    def quantity(q):
+        mask = (lane >= FREE + 3 * q) & (lane < FREE + 3 * q + 3)
+        return jnp.sum(jnp.where(mask, total, 0.0), axis=1, keepdims=True)
+
+    def pick(q):
+        across = jnp.sum(jnp.where(line == lane, quantity(q), 0.0), axis=0, keepdims=True)
+        wide = iota((CHANNELS, 128), 1)
+        return jnp.sum(jnp.where(wide == group, across, 0.0), axis=1, keepdims=True)
+
+    positions = quantity(2)[:1]
+    count = positions * GROUP_SIZE
+    mean = pick(0) / count
+    rstd = lax.rsqrt(pick(1) / count - mean * mean + EPSILON)
+    return positions, mean, rstd
+
+
+def sums_split(value):
+    first = rounded(value)
+    return first + pltpu.roll(rounded(value - first), 16, 1)
+
+
+def sums_joined(tile):
+    lane = iota((40, 128), 1)
+    mask = (lane >= FREE) & (lane < FREE + 16)
+    return jnp.where(mask, tile + pltpu.roll(tile, 112, 1), 0.0)
+
+
+def pair_kernel(own, other, out):
+    lane = iota((40, 128), 1)
+
+    def body(n, _):
+        total = own[n].astype(f32) + other[n].astype(f32)
+        tile = total[:, TILE_AT:WIDE]
+        tile = jnp.where(lane < FREE, tile, sums_split(sums_joined(tile)))
+        out[n] = with_tile(total, tile).astype(bf16)
+        return 0
+
+    lax.fori_loop(0, 16, body, 0)
 
 
 def unpack_kernel(terms, out):
     total = terms[0].astype(f32)
     for n in range(1, 16):
         total += terms[n].astype(f32)
+    sums = pltpu.roll(sums_joined(total[:, TILE_AT:WIDE]), 128 - FREE, 1)
+    for step in (16, 32, 64):
+        sums += pltpu.roll(sums, step, 1)
+    mine = (iota((40, 128), 1) >> 4) == (iota((40, 128), 0) & 7)
+    sums = jnp.sum(jnp.where(mine, sums, 0.0).reshape(5, 8, 128), axis=1)
+    first = rounded(sums)
+    sums = jnp.concatenate([first, rounded(sums - first)], axis=1)
+    row = iota((16, 256), 0)
+    extra = jnp.zeros((16, 256), f32)
+    for n in range(5):
+        extra += jnp.where(row == SPARE + n, sums[n : n + 1], 0.0)
+    extra = jnp.concatenate([extra] * 4, axis=0)
     rows = dot(row_place((64, 40), 1, 0), total.astype(bf16)).astype(bf16)
     for z_low in range(4):
-        out[z_low] = dot_nt(rows, column_place(z_low)).astype(bf16)
-
-
-def stat_columns(stats, group):
-    total = jnp.sum(stats[...], axis=0, keepdims=True)
-    lane = iota((CHANNELS, 128), 1)
-
-    def pick(mask):
-        return jnp.sum(jnp.where(mask, total, 0.0), axis=1, keepdims=True)
-
-    positions = pick(lane == 2 * GROUPS)
-    count = positions * GROUP_SIZE
-    mean = pick(lane == group) / count
-    rstd = lax.rsqrt(pick(lane == group + GROUPS) / count - mean * mean + EPSILON)
-    return positions, count, mean, rstd
+        out[z_low] = (dot_nt(rows, column_place(z_low)) + extra).astype(bf16)
 
 
 def turned(row):
@@ -123,8 +227,8 @@
 
 
 def main_kernel(
-    place, stats, gain, shift, order, order_row, group, latent, g_next, g_here, g_last,
-    w_own, w_other, grad_own, grad_other, pre_grad, sums, cols, turned_s, turned_t, frames, taps,
+    place, gain, shift, order, order_row, group, latent, g_next, g_here, g_last,
+    w_own, w_other, grad_own, grad_other, pre_grad, norm, cols, turned_s, turned_t, frames, taps,
 ):
     height = place[0]
     strip = place[1]
@@ -141,7 +245,9 @@
         turned_s[y * SPAN : (y + 1) * SPAN, :] = across[:SPAN]
         turned_t[y * SPAN_T : (y + 1) * SPAN_T, :] = across[WIDE : WIDE + SPAN_T]
 
-    _, _, mean, rstd = stat_columns(stats, group[...])
+    positions, mean, rstd = stat_columns(w_own, w_other, group[...])
+    lane_n = iota((CHANNELS, 128), 1)
+    norm[...] = jnp.where(lane_n == 0, mean, jnp.where(lane_n == 1, rstd, positions))
     gain_column = turned(gain[...])
     shift_column = turned(shift[...])
     normed = (latent[...].astype(f32) - mean) * rstd
@@ -178,15 +284,28 @@
             dot(spat_packed, move).astype(bf16),
         )
 
+    own_live = live[:, :CELLS]
+    act = pre_act[:, :CELLS]
+    sig = sigmoid[:, :CELLS]
+    grad_pre = jnp.where(own_live, grad_act * sig * (1.0 + act * (1.0 - sig)), 0.0)
+    pre_grad[...] = grad_pre
+    chan_gain = jnp.sum(grad_pre * normed[:, :CELLS], axis=1, keepdims=True)
+    chan_shift = jnp.sum(grad_pre, axis=1, keepdims=True)
+    spot = (iota((CHANNELS, 128), 0) & 7) + FREE
+    sums = jnp.where(lane_n == spot, chan_gain, 0.0)
+    sums += jnp.where(lane_n == spot + 8, chan_shift, 0.0)
+    sums = sums_split(jnp.sum(sums.reshape(40, 8, 128), axis=1))
+    sums = jnp.concatenate([sums] * 4, axis=0)
+
     spatial = jnp.zeros((CHANNELS, CELLS), f32)
     left = spat_packed[:, :CELLS]
     for y in range(4):
         whole = jnp.concatenate([w_own[y, :, :WIDE], w_other[y, :, :WIDE]], axis=0)
         spatial += dot(whole, cols[y])
-        part = dot_nt(left, cols[y]).astype(bf16)
-        grad_own[y, :, :WIDE] = part[:160]
-        grad_other[y, :, :WIDE] = part[160:]
-    own_live = live[:, :CELLS]
+        part = dot_nt(left, cols[y])
+        for half, ref in ((part[:160], grad_own), (part[160:], grad_other)):
+            ref[y, :, :TILE_AT] = half[:, :TILE_AT].astype(bf16)
+            ref[y, :, TILE_AT:WIDE] = (half[:, TILE_AT:] + sums).astype(bf16)
     spatial = jnp.where(own_live, spatial, 0.0).astype(bf16)
     spatial = dot(to_plain, spatial).astype(bf16)
 
@@ -200,41 +319,49 @@
         grad_own[y, :, WIDE:] = part[:160]
         grad_other[y, :, WIDE:] = part[160:]
 
-    act = pre_act[:, :CELLS]
-    sig = sigmoid[:, :CELLS]
-    grad_pre = jnp.where(own_live, grad_act * sig * (1.0 + act * (1.0 - sig)), 0.0)
-    pre_grad[...] = grad_pre
-    chan_gain = jnp.sum(grad_pre * normed[:, :CELLS], axis=1, keepdims=True)
-    chan_shift = jnp.sum(grad_pre, axis=1, keepdims=True)
-    sums[...] = jnp.zeros(sums.shape, f32)
-    sums[:, :CHANNELS] = turned_back(chan_gain)
-    sums[:, EXT : EXT + CHANNELS] = turned_back(chan_shift)
-
-
-def input_kernel(
-    place, stats, gain, group, group_row, latent, g_here, pre_grad, sums, result, totals
+
+def end_kernel(
+    place, norm, gain, group, group_row, latent, g_here, pre_grad, terms,
+    result, grad_s, grad_t, grad_gain, grad_shift,
 ):
     height = place[0]
     own_live = (iota((1, CELLS), 1) >> 4) < height
-    positions, count, mean, rstd = stat_columns(stats, group[...])
-    total = jnp.sum(sums[...], axis=0, keepdims=True)
-    scale = lax.rsqrt(positions[:1, :1])
-    totals[...] = total * scale
+    mean, rstd, positions = norm[:, 0:1], norm[:, 1:2], norm[:1, 2:3]
+    scale = lax.rsqrt(positions)
+    count = positions * GROUP_SIZE
+    total = terms[0].astype(f32)
+    for n in range(1, 16):
+        total += terms[n].astype(f32)
+    scaled = total * scale
+    grad_s[...] = scaled[:10, :180]
+    grad_t[...] = pltpu.roll(scaled, 76, 1)[:10, :60]
+    sums = total[:, :128] + total[:, 128:]
+    wide = [jnp.broadcast_to(sums[SPARE + n : SPARE + n + 1], (64, 128)) for n in range(5)]
+    wide = jnp.concatenate(wide, axis=0)
+    channel = iota((CHANNELS, 128), 0)
+    spot = ((channel >> 3) & 7) * 16 + (channel & 7)
+    lane = iota((CHANNELS, 128), 1)
     same = group[...] == group_row[...]
+
+    def chan_row(offset):
+        column = jnp.sum(jnp.where(lane == spot + offset, wide, 0.0), axis=1, keepdims=True)
+        return turned_back(column)
 
     def over_group(row):
         return jnp.sum(jnp.where(same, gain[...] * row, 0.0), axis=1, keepdims=True) / count
 
-    gain_sum = over_group(total[:, :CHANNELS])
-    shift_sum = over_group(total[:, EXT : EXT + CHANNELS])
-    normed = (latent[:, :CELLS].astype(f32) - mean) * rstd
+    gain_row = chan_row(0)
+    shift_row = chan_row(8)
+    grad_gain[...] = gain_row * scale
+    grad_shift[...] = shift_row * scale
+    normed = (latent[...].astype(f32) - mean) * rstd
     value = g_here[:, :CELLS].astype(f32) + rstd * (
-        turned(gain[...]) * pre_grad[...] - shift_sum - normed * gain_sum
+        turned(gain[...]) * pre_grad[...] - over_group(shift_row) - normed * over_group(gain_row)
     )
     result[...] = jnp.where(own_live, value, 0.0).astype(bf16)
 
 
-def call(kernel, outs, smem=0, scratch=(), inputs=1, flops=0, moved=0):
+def call(kernel, outs, smem=0, scratch=(), inputs=1, flops=0, moved=0, room=16):
     vmem = pl.BlockSpec(memory_space=pltpu.VMEM)
     specs = [pl.BlockSpec(memory_space=pltpu.SMEM)] * smem + [vmem] * (inputs - smem)
     many = isinstance(outs, tuple)
@@ -244,7 +371,7 @@
         in_specs=specs,
         out_specs=tuple(vmem for _ in outs) if many else vmem,
         scratch_shapes=list(scratch),
-        compiler_params=pltpu.CompilerParams(vmem_limit_bytes=48 << 20),
+        compiler_params=pltpu.CompilerParams(vmem_limit_bytes=room << 20),
         cost_estimate=pl.CostEstimate(flops=flops, bytes_accessed=moved, transcendentals=0),
     )
 
@@ -277,32 +404,25 @@
     latent = latents[0]
     grad = jnp.where(live, out_grad[0], jnp.zeros((), bf16))
 
+    group = jnp.arange(CHANNELS, dtype=jnp.int32) // GROUP_SIZE
+    group_column = group[:, None]
+
     shard = jnp.concatenate([w_spatial, w_temporal], axis=1)
     shard = jnp.pad(shard, ((0, 6), (0, 16)))
-    near = to_all(shard, ROW_Z).reshape(4, 64, 256)
-    packed = call(pack_kernel, shape((40, PACK), bf16), flops=1 << 27, moved=1 << 18)(near)
-    w_own = to_all(packed, PLANE).reshape(4, 160, PACK)
-    w_other = swap_cores(w_own)
-
-    wide = jnp.where(live, latent, jnp.zeros((), bf16)).astype(f32)
-    chan_sum = jnp.sum(wide, axis=1)
-    chan_square = jnp.sum(wide * wide, axis=1)
-    own_stats = jnp.concatenate(
-        [
-            chan_sum.reshape(GROUPS, GROUP_SIZE).sum(1),
-            chan_square.reshape(GROUPS, GROUP_SIZE).sum(1),
-            (height * COLUMNS).astype(f32)[None],
-            jnp.zeros((63,), f32),
-        ]
-    )[None]
-    stats = jnp.sum(to_all(own_stats, ROW_Z), axis=0)
-    stats = to_all(stats, PLANE_CORE)[:, 0]
+    near = call(
+        start_kernel, shape((16, 16, 256), bf16), smem=1, inputs=4, flops=1 << 20, moved=1 << 18
+    )(place, latent, group_column, shard)
+    near = exchange(near, ROW_Z).reshape(4, 64, 256)
+    packed = call(pack_kernel, shape((16, 40, PACK), bf16), flops=1 << 27, moved=3 << 19)(near)
+    w_own = exchange(packed, PLANE).reshape(4, 160, PACK)
 
     both = jnp.stack([latent, grad])
     tall = height == 16
     last = jnp.where(tall, both[:, :, 240:256], both[:, :, 112:128])
     above = step_by(last, TILE, 1)
     below = step_by(both[:, :, :COLUMNS], TILE, -1)
+    w_own, above, below = lax.optimization_barrier((w_own, above, below))
+    w_other = swap_cores(w_own)
     latent_ext = extended(latent, above[0], below[0])
     grad_ext = extended(grad, above[1], below[1])
     grad_last = step_by(grad_ext, FRAME, 1)
@@ -312,14 +432,13 @@
     half, rest = packed_row // 160, packed_row % 160
     order = rest // 40 * 80 + rest % 40 // 10 * 20 + rest % 10
     order = order + jnp.where(half == 0, core, 1 - core) * 10
-    group = jnp.arange(CHANNELS, dtype=jnp.int32) // GROUP_SIZE
     gain_row, shift_row = norm_gain[None], norm_shift[None]
     block = shape((4, 160, PACK), bf16)
-    grad_own, grad_other, pre_grad, sums = call(
+    grad_own, grad_other, pre_grad, norm = call(
         main_kernel,
-        (block, block, shape((CHANNELS, CELLS), f32), shape((1, 2 * EXT), f32)),
+        (block, block, shape((CHANNELS, CELLS), f32), shape((CHANNELS, 128), f32)),
         smem=1,
-        inputs=13,
+        inputs=12,
         scratch=(
             pltpu.VMEM((4, WIDE, CELLS), bf16),
             pltpu.VMEM((4 * SPAN, CHANNELS), bf16),
@@ -329,40 +448,36 @@
         ),
         flops=5 << 30,
         moved=8 << 20,
+        room=28,
     )(
-        place, stats, gain_row, shift_row, order[:, None], order[None, :], group[:, None],
+        place, gain_row, shift_row, order[:, None], order[None, :], group_column,
         latent_ext, grad_next, grad_ext, grad_last, w_own, w_other,
     )
 
-    chan = jnp.sum(to_all(sums, ROW_Z), axis=0)
-    chan = to_all(chan, PLANE_CORE)[:, 0]
-    grad_input, totals = call(
-        input_kernel,
-        (shape((CHANNELS, CELLS), bf16), shape((1, 2 * EXT), f32)),
+    blocks = (16, 40, PACK)
+    pair = call(pair_kernel, shape(blocks, bf16), inputs=2, flops=1 << 20, moved=1 << 22)(
+        grad_own.reshape(blocks), swap_cores(grad_other).reshape(blocks)
+    )
+    terms = exchange(pair, PLANE)
+    parts = call(unpack_kernel, shape((4, 64, 256), bf16), flops=1 << 27, moved=1 << 21)(terms)
+    parts = exchange(parts.reshape(16, 16, 256), ROW_Z)
+    grad_input, grad_spatial, grad_temporal, grad_gain, grad_shift = call(
+        end_kernel,
+        (
+            shape((CHANNELS, CELLS), bf16),
+            shape((10, 180), f32),
+            shape((10, 60), f32),
+            shape((1, CHANNELS), f32),
+            shape((1, CHANNELS), f32),
+        ),
         smem=1,
         inputs=9,
         flops=1 << 22,
         moved=1 << 20,
     )(
-        place, stats, gain_row, group[:, None], group[None, :], latent_ext, grad_ext,
-        pre_grad, chan,
-    )
-
-    pair = grad_own.astype(f32) + swap_cores(grad_other).astype(f32)
-    terms = lax.all_to_all(
-        pair.astype(bf16).reshape(16, 40, PACK), PLANE, 0, 0, tiled=True
-    )
-    parts = call(unpack_kernel, shape((4, 64, 256), bf16), flops=1 << 27, moved=1 << 21)(terms)
-    mine = lax.all_to_all(parts.reshape(16, 16, 256), ROW_Z, 0, 0, tiled=True)
-    scale = lax.rsqrt(jnp.sum(stats[:, 2 * GROUPS]))
-    mine = jnp.sum(mine.astype(f32), axis=0) * scale
-    return (
-        grad_input[None],
-        mine[:10, :180],
-        mine[:10, 180:240],
-        totals[0, :CHANNELS],
-        totals[0, EXT : EXT + CHANNELS],
-    )
+        place, norm, gain_row, group_column, group[None, :], latent, grad_ext, pre_grad, parts,
+    )
+    return grad_input[None], grad_spatial, grad_temporal, grad_gain[0], grad_shift[0]
 
 
 def solution(mesh):

time: 183 us -> 149 us (0.81)
  waiting for transfers between devices: 73.3 us -> 39.3 us
  blocking collectives: 29.8 us -> 58.1 us
  starting transfers between devices: 50.4 us -> 29.9 us
  local copies, waits for them, and re-layouts: 9.43 us -> 1.05 us
  Pallas kernels: 12.3 us -> 15.9 us
    all_to_all x7 -> x2, waiting for transfers between devices: 73.3 us -> 27.6 us  [exchange(): return lax.all_to_all(blocks, axes, 0, 0, tiled=True)]
    all_to_all x1 -> x2, blocking collectives: 29.8 us -> 58.1 us  [exchange(): return lax.all_to_all(blocks, axes, 0, 0, tiled=True)]
    all_to_all x7 -> x2, starting transfers between devices: 36.4 us -> 17.7 us  [exchange(): return lax.all_to_all(blocks, axes, 0, 0, tiled=True)]
    ppermute x4, waiting for transfers between devices: 0.01 us -> 8.76 us  [step_by(): return lax.ppermute(value, axes, pairs)]
    broadcast_in_dim x7 -> x0, local copies, waits for them, and re-layouts: 3.82 us -> none  [the longest x6 3.82 us: to_all(): copies = jnp.broadcast_to(value[None], (peers, *value.shape))]
    pallas_call x3 -> x5, Pallas kernels: 11 us -> 14.4 us  [the longest x1 7.53 us: local(): call(main_kernel, (block, block, shape((CHANNELS, CELLS), f32), shape((CH...]
    unnamed x23 -> x10, local copies, waits for them, and re-layouts: 4.03 us -> 0.94 us
    ppermute x2, waiting for transfers between devices: 0.01 us -> 3 us  [swap_cores(): return lax.ppermute(value, 'tile_2', [(0, 1), (1, 0)])]
  transfers between devices with their start and end apart: 13 -> 8, of which waited for: 7 -> 6; matrix products, arithmetic and copies ran while one was open for 4% -> 1% of each run, Pallas kernels for 2% -> 0%
where the time goes in v2:
time: 149 us
  blocking collectives  58.1 us (39%)
  waiting for transfers between devices  39.3 us (26%)
  starting transfers between devices  29.9 us (20%)
  Pallas kernels  15.9 us (11%)
  other arithmetic  2.94 us (2%)
  between operations  1.51 us (1%)
    all_to_all x2, blocking collectives, exchange(): return lax.all_to_all(blocks, axes, 0, 0, tiled=True)  58.1 us
    all_to_all x2, waiting for transfers between devices, exchange(): return lax.all_to_all(blocks, axes, 0, 0, tiled=True)  27.6 us
    all_to_all x2, starting transfers between devices, exchange(): return lax.all_to_all(blocks, axes, 0, 0, tiled=True)  17.7 us
    ppermute x4, waiting for transfers between devices, step_by(): return lax.ppermute(value, axes, pairs)  8.76 us
    ppermute x4, starting transfers between devices, step_by(): return lax.ppermute(value, axes, pairs)  8.43 us
    pallas_call x1, Pallas kernels, local(): call(main_kernel, (block, block, shape((CHANNELS, CELLS), f32), shape((CH...  7.53 us
    ppermute x2, starting transfers between devices, swap_cores(): return lax.ppermute(value, 'tile_2', [(0, 1), (1, 0)])  3.83 us
    ppermute x2, waiting for transfers between devices, swap_cores(): return lax.ppermute(value, 'tile_2', [(0, 1), (1, 0)])  3 us
  transfers between devices with their start and end apart: 8, of which 6 were waited for; matrix products, arithmetic and copies ran while one was open for 1% of the time, Pallas kernels for 0%

profile of v2, /device:TPU:32, one launch (start us, length us, event | category | flops | bytes accessed | tf_op | source)
XLA Modules:
  0.0 148.7 jit_solution(2871072340133067800)
XLA Ops:
  1.4 0.8 fusion.31.shard
  2.2 0.9 copy-done
  3.1 0.8 shard_map.110
  4.0 29.8 %all_to_all.20 = bf16[16,16,256]{2,1,0:T(8,128)(2,1)S(1)} all-to-all(bf16[16,16,256]{2,1,0:T(8,128)(2,1)S(1)} %shard_map.110), channel_id=1, replica_groups=mesh['frame_0'=4,'frame_1'=4,'tile_0'=4,'tile_1'=4,'tile_2'=2] {'frame_1..., dimensions={0} | all-to-all | bytes 262144 | tf_op jit(solution)/shard_map/all_to_all | solution.py:58
  33.7 1.6 %shard_map.111 = bf16[16,40,1024]{2,1,0:T(8,128)(2,1)} custom-call(bf16[4,64,256]{2,1,0:T(8,128)(2,1)S(1)} %bitcast.28), custom_call_target="tpu_custom_call" | custom-call | flops 134217728 | bytes 1572864 | tf_op jit(solution)/shard_map/pallas_call | solution.py:416
  35.4 7.2 %all-to-all-start.1 = ((bf16[16,40,1024]{2,1,0:T(8,128)(2,1)}), bf16[16,40,1024]{2,1,0:T(8,128)(2,1)S(1)}, u32[]{:S(2)}, u32[]{:S(2)}) async-start(bf16[16,40,1024]{2,1,0:T(8,128)(2,1)} %shard_map.111), calls=%async_computation.1 | async-start | bytes 2621440 | tf_op jit(solution)/shard_map/all_to_all | solution.py:58
  42.8 1.3 collective-permute-start
  44.1 1.3 collective-permute-start.1
  45.4 3.0 %collective-permute-done.1 = bf16[2,320,16]{2,1,0:T(8,128)(2,1)S(1)} collective-permute-done((bf16[2,320,16]{2,1,0:T(8,128)(2,1)S(1)}, bf16[2,320,16]{2,1,0:T(8,128)(2,1)S(1)}, u32[]{:S(2)}, u32[]{:S(2)}) %collective-permute-start.1) | collective-permute-done | bytes 20512 | tf_op jit(solution)/shard_map/ppermute | solution.py:386
  48.4 13.6 %all-to-all-done.1 = bf16[16,40,1024]{2,1,0:T(8,128)(2,1)S(1)} async-done(((bf16[16,40,1024]{2,1,0:T(8,128)(2,1)}), bf16[16,40,1024]{2,1,0:T(8,128)(2,1)S(1)}, u32[]{:S(2)}, u32[]{:S(2)}) %all-to-all-start.1) | async-done | bytes 1310752 | tf_op jit(solution)/shard_map/all_to_all | solution.py:58
  62.0 1.9 %collective-permute-start.4 = (bf16[4,160,1024]{2,1,0:T(8,128)(2,1)S(1)}, bf16[4,160,1024]{2,1,0:T(8,128)(2,1)}, u32[]{:S(2)}, u32[]{:S(2)}) collective-permute-start(bf16[4,160,1024]{2,1,0:T(8,128)(2,1)S(1)} %bitcast.24), channel_id=1, source_target_pairs={{0,1},{1,0},{2,3},{3,2},{4,5},{5,4},{6,7},{7,6},{8,9},{9,8},{10,11... | collective-permute-start | bytes 3932168 | tf_op jit(solution)/shard_map/ppermute | solution.py:390
  64.2 1.9 %collective-permute-start.2 = (bf16[320,384]{1,0:T(8,128)(2,1)S(1)}, bf16[320,384]{1,0:T(8,128)(2,1)S(1)}, u32[]{:S(2)}, u32[]{:S(2)}) collective-permute-start(bf16[320,384]{1,0:T(8,128)(2,1)S(1)} %get-tuple-element.35.g_here), channel_id=1, source_target_pairs={{32,0},{64,32},{96,64},{128,96},{160,128},{192,160},{224,192},{256... | collective-permute-start | bytes 737288 | tf_op jit(solution)/shard_map/ppermute | solution.py:386
  66.2 3.9 %collective-permute-start.3 = (bf16[320,384]{1,0:T(8,128)(2,1)S(1)}, bf16[320,384]{1,0:T(8,128)(2,1)S(1)}, u32[]{:S(2)}, u32[]{:S(2)}) collective-permute-start(bf16[320,384]{1,0:T(8,128)(2,1)S(1)} %get-tuple-element.35.g_here), channel_id=1, source_target_pairs={{0,32},{32,64},{64,96},{96,128},{128,160},{160,192},{192,224},{224... | collective-permute-start | bytes 737288 | tf_op jit(solution)/shard_map/ppermute | solution.py:386
  70.6 3.9 %collective-permute-done.2.g_next = bf16[320,384]{1,0:T(8,128)(2,1)S(1)} collective-permute-done((bf16[320,384]{1,0:T(8,128)(2,1)S(1)}, bf16[320,384]{1,0:T(8,128)(2,1)S(1)}, u32[]{:S(2)}, u32[]{:S(2)}) %collective-permute-start.2) | collective-permute-done | bytes 245792 | tf_op jit(solution)/shard_map/ppermute | solution.py:386
  74.5 1.9 %collective-permute-done.3.g_last = bf16[320,384]{1,0:T(8,128)(2,1)S(1)} collective-permute-done((bf16[320,384]{1,0:T(8,128)(2,1)S(1)}, bf16[320,384]{1,0:T(8,128)(2,1)S(1)}, u32[]{:S(2)}, u32[]{:S(2)}) %collective-permute-start.3) | collective-permute-done | bytes 245792 | tf_op jit(solution)/shard_map/ppermute | solution.py:386
  76.4 7.5 %shard_map.112 = (bf16[4,160,1024]{2,1,0:T(8,128)(2,1)S(1)}, bf16[4,160,1024]{2,1,0:T(8,128)(2,1)S(1)}, f32[320,256]{1,0:T(8,128)S(1)}, f32[320,128]{1,0:T(8,128)S(1)}) custom-call(s32[2]{0:T(128)S(1)} %pad_add_fusion.place, f32[1,320]{1,0:T(1,128)S(1)} %broadcast_in_dim.42.gain, f32[1,320]{1,0:T(1,128)S(1)} %broadcast_in_dim.43.shift, ...), custom_call_target="tpu_custom_call" | custom-call | flops 5368709120 | bytes 8388608 | tf_op jit(solution)/shard_map/pallas_call | solution.py:437
  83.9 1.9 %collective-permute-start.5 = (bf16[4,160,1024]{2,1,0:T(8,128)(2,1)S(1)}, bf16[4,160,1024]{2,1,0:T(8,128)(2,1)S(1)}, u32[]{:S(2)}, u32[]{:S(2)}) collective-permute-start(bf16[4,160,1024]{2,1,0:T(8,128)(2,1)S(1)} %get-tuple-element.23), channel_id=1, source_target_pairs={{0,1},{1,0},{2,3},{3,2},{4,5},{5,4},{6,7},{7,6},{8,9},{9,8},{10,11... | collective-permute-start | bytes 3932168 | tf_op jit(solution)/shard_map/ppermute | solution.py:390
  85.9 3.0 %collective-permute-done.5 = bf16[4,160,1024]{2,1,0:T(8,128)(2,1)S(1)} collective-permute-done((bf16[4,160,1024]{2,1,0:T(8,128)(2,1)S(1)}, bf16[4,160,1024]{2,1,0:T(8,128)(2,1)S(1)}, u32[]{:S(2)}, u32[]{:S(2)}) %collective-permute-start.5) | collective-permute-done | bytes 1310752 | tf_op jit(solution)/shard_map/ppermute | solution.py:390
  88.9 2.5 %shard_map.113 = bf16[16,40,1024]{2,1,0:T(8,128)(2,1)S(1)} custom-call(bf16[16,40,1024]{2,1,0:T(8,128)(2,1)S(1)} %bitcast.26, bf16[16,40,1024]{2,1,0:T(8,128)(2,1)S(1)} %bitcast.27), custom_call_target="tpu_custom_call" | custom-call | flops 1048576 | bytes 4194304 | tf_op jit(solution)/shard_map/pallas_call | solution.py:458
  91.4 28.3 %all_to_all.21.terms = bf16[16,40,1024]{2,1,0:T(8,128)(2,1)S(1)} all-to-all(bf16[16,40,1024]{2,1,0:T(8,128)(2,1)S(1)} %shard_map.113), channel_id=1, replica_groups=mesh['frame_0'=4,'frame_1'=4,'tile_0'=4,'tile_1'=4,'tile_2'=2] {'frame_0..., dimensions={0} | all-to-all | bytes 2621440 | tf_op jit(solution)/shard_map/all_to_all | solution.py:58
  119.7 1.4 shard_map.114
  121.1 10.5 %all-to-all-start.3 = ((bf16[16,16,256]{2,1,0:T(8,128)(2,1)}), bf16[16,16,256]{2,1,0:T(8,128)(2,1)S(1)}, u32[]{:S(2)}, u32[]{:S(2)}) async-start(bf16[16,16,256]{2,1,0:T(8,128)(2,1)} %bitcast.12), calls=%async_computation.3 | async-start | bytes 262144 | tf_op jit(solution)/shard_map/all_to_all | solution.py:58
  131.6 14.0 %all-to-all-done.3.terms = bf16[16,16,256]{2,1,0:T(8,128)(2,1)S(1)} async-done(((bf16[16,16,256]{2,1,0:T(8,128)(2,1)}), bf16[16,16,256]{2,1,0:T(8,128)(2,1)S(1)}, u32[]{:S(2)}, u32[]{:S(2)}) %all-to-all-start.3) | async-done | bytes 131104 | tf_op jit(solution)/shard_map/all_to_all | solution.py:58
  145.6 1.9 %shard_map.115 = (bf16[320,256]{1,0:T(8,128)(2,1)}, f32[10,180]{1,0:T(8,128)}, f32[10,60]{1,0:T(8,128)}, f32[1,320]{1,0:T(1,128)S(1)}, f32[1,320]{1,0:T(1,128)S(1)}) custom-call(s32[2]{0:T(128)S(1)} %pad_add_fusion.place, f32[320,128]{1,0:T(8,128)S(1)} %get-tuple-element.20.norm, f32[1,320]{1,0:T(1,128)S(1)} %broadcast_in_dim.42.gain, ...), custom_call_target="tpu_custom_call" | custom-call | flops 4194304 | bytes 1048576 | tf_op jit(solution)/shard_map/pallas_call | solution.py:464
  (28 shorter events, 2.3 us)
Async XLA Ops:
  2.2 0.9 copy-start
  35.4 7.2 %copy-start.2 = (bf16[1,320,256]{2,1,0:T(8,128)(2,1)S(1)}, bf16[1,320,256]{2,1,0:T(8,128)(2,1)}, u32[]{:S(2)}) copy-start(bf16[1,320,256]{2,1,0:T(8,128)(2,1)} %param.8) | copy-start | bytes 491524
  35.4 7.2 %copy-start.1 = (bf16[1,320,256]{2,1,0:T(8,128)(2,1)S(1)}, bf16[1,320,256]{2,1,0:T(8,128)(2,1)}, u32[]{:S(2)}) copy-start(bf16[1,320,256]{2,1,0:T(8,128)(2,1)} %param.7) | copy-start | bytes 491524
  35.4 26.6 %all-to-all-start.1 = ((bf16[16,40,1024]{2,1,0:T(8,128)(2,1)}), bf16[16,40,1024]{2,1,0:T(8,128)(2,1)S(1)}, u32[]{:S(2)}, u32[]{:S(2)}) async-start(bf16[16,40,1024]{2,1,0:T(8,128)(2,1)} %shard_map.111), calls=%async_computation.1 | async-start | bytes 2621440 | tf_op jit(solution)/shard_map/all_to_all | solution.py:58
  42.6 27.4 %copy-start.3 = (f32[320]{0:T(512)S(1)}, f32[320]{0:T(512)}, u32[]{:S(2)}) copy-start(f32[320]{0:T(512)} %param.11) | copy-start | bytes 3844
  42.6 27.5 %copy-start.4 = (f32[320]{0:T(512)S(1)}, f32[320]{0:T(512)}, u32[]{:S(2)}) copy-start(f32[320]{0:T(512)} %param.12) | copy-start | bytes 3844
  42.8 2.6 %collective-permute-start = (bf16[2,320,16]{2,1,0:T(8,128)(2,1)S(1)}, bf16[2,320,16]{2,1,0:T(8,128)(2,1)S(1)}, u32[]{:S(2)}, u32[]{:S(2)}) collective-permute-start(bf16[2,320,16]{2,1,0:T(8,128)(2,1)S(1)} %get-tuple-element.30), channel_id=1, source_target_pairs={{0,1},{1,2},{2,3},{3,4},{4,5},{5,6},{6,7},{7,8},{8,9},{9,10},{10,1... | collective-permute-start | bytes 61448 | tf_op jit(solution)/shard_map/ppermute | solution.py:386
  44.1 4.3 %collective-permute-start.1 = (bf16[2,320,16]{2,1,0:T(8,128)(2,1)S(1)}, bf16[2,320,16]{2,1,0:T(8,128)(2,1)S(1)}, u32[]{:S(2)}, u32[]{:S(2)}) collective-permute-start(bf16[2,320,16]{2,1,0:T(8,128)(2,1)S(1)} %get-tuple-element.29), channel_id=1, source_target_pairs={{1,0},{2,1},{3,2},{4,3},{5,4},{6,5},{7,6},{8,7},{9,8},{10,9},{11,1... | collective-permute-start | bytes 61448 | tf_op jit(solution)/shard_map/ppermute | solution.py:386
  62.0 14.4 %collective-permute-start.4 = (bf16[4,160,1024]{2,1,0:T(8,128)(2,1)S(1)}, bf16[4,160,1024]{2,1,0:T(8,128)(2,1)}, u32[]{:S(2)}, u32[]{:S(2)}) collective-permute-start(bf16[4,160,1024]{2,1,0:T(8,128)(2,1)S(1)} %bitcast.24), channel_id=1, source_target_pairs={{0,1},{1,0},{2,3},{3,2},{4,5},{5,4},{6,7},{7,6},{8,9},{9,8},{10,11... | collective-permute-start | bytes 3932168 | tf_op jit(solution)/shard_map/ppermute | solution.py:390
  64.2 10.3 %collective-permute-start.2 = (bf16[320,384]{1,0:T(8,128)(2,1)S(1)}, bf16[320,384]{1,0:T(8,128)(2,1)S(1)}, u32[]{:S(2)}, u32[]{:S(2)}) collective-permute-start(bf16[320,384]{1,0:T(8,128)(2,1)S(1)} %get-tuple-element.35.g_here), channel_id=1, source_target_pairs={{32,0},{64,32},{96,64},{128,96},{160,128},{192,160},{224,192},{256... | collective-permute-start | bytes 737288 | tf_op jit(solution)/shard_map/ppermute | solution.py:386
  66.2 10.3 %collective-permute-start.3 = (bf16[320,384]{1,0:T(8,128)(2,1)S(1)}, bf16[320,384]{1,0:T(8,128)(2,1)S(1)}, u32[]{:S(2)}, u32[]{:S(2)}) collective-permute-start(bf16[320,384]{1,0:T(8,128)(2,1)S(1)} %get-tuple-element.35.g_here), channel_id=1, source_target_pairs={{0,32},{32,64},{64,96},{96,128},{128,160},{160,192},{192,224},{224... | collective-permute-start | bytes 737288 | tf_op jit(solution)/shard_map/ppermute | solution.py:386
  83.9 4.9 %collective-permute-start.5 = (bf16[4,160,1024]{2,1,0:T(8,128)(2,1)S(1)}, bf16[4,160,1024]{2,1,0:T(8,128)(2,1)S(1)}, u32[]{:S(2)}, u32[]{:S(2)}) collective-permute-start(bf16[4,160,1024]{2,1,0:T(8,128)(2,1)S(1)} %get-tuple-element.23), channel_id=1, source_target_pairs={{0,1},{1,0},{2,3},{3,2},{4,5},{5,4},{6,7},{7,6},{8,9},{9,8},{10,11... | collective-permute-start | bytes 3932168 | tf_op jit(solution)/shard_map/ppermute | solution.py:390
  121.1 24.5 %all-to-all-start.3 = ((bf16[16,16,256]{2,1,0:T(8,128)(2,1)}), bf16[16,16,256]{2,1,0:T(8,128)(2,1)S(1)}, u32[]{:S(2)}, u32[]{:S(2)}) async-start(bf16[16,16,256]{2,1,0:T(8,128)(2,1)} %bitcast.12), calls=%async_computation.3 | async-start | bytes 262144 | tf_op jit(solution)/shard_map/all_to_all | solution.py:58

commit v3 on v2

--- a/solution.py
+++ b/solution.py
@@ -29,7 +29,7 @@
 
 TILE = ("tile_0", "tile_1", "tile_2")
 FRAME = ("frame_0", "frame_1")
-ROW_Z = ("frame_1", "tile_1")
+ROW_Z = ("tile_1", "frame_1")
 PLANE = ("frame_0", "tile_0")
 PLANE_CORE = ("frame_0", "tile_0", "tile_2")
 
@@ -90,7 +90,7 @@
     return jnp.concatenate([block[:, :TILE_AT], tile, block[:, WIDE:]], axis=1)
 
 
-def start_kernel(place, latent, group, shard, out):
+def start_kernel(place, latent, group, w_spatial, w_temporal, out, left, right):
     height = place[0]
     live = (iota((1, CELLS), 1) >> 4) < height
     value = jnp.where(live, latent[...].astype(f32), 0.0)
@@ -107,7 +107,11 @@
     for n, piece in enumerate(pieces_in(stats)):
         extra += jnp.where(row == SPARE + n, piece, 0.0)
     extra = jnp.concatenate([extra, jnp.zeros((16, 128), f32)], axis=1)
-    block = (shard[...].astype(f32) + extra).astype(bf16)
+    left[...] = jnp.zeros((16, 256), f32)
+    right[...] = jnp.zeros((16, 256), f32)
+    left[:10, :180] = w_spatial[...].astype(f32)
+    right[:10, :60] = w_temporal[...].astype(f32)
+    block = (left[...] + pltpu.roll(right[...], 180, 1) + extra).astype(bf16)
     for n in range(16):
         out[n] = block
 
@@ -116,8 +120,9 @@
     total = jnp.zeros((64, PACK), f32)
     stats = jnp.zeros((64, 128), f32)
     for z_low in range(4):
-        total += dot(blocks[z_low], column_place(z_low))
-        stats += blocks[z_low, :, :128].astype(f32)
+        rows = jnp.concatenate([blocks[4 * a + z_low] for a in range(4)], axis=0)
+        total += dot(rows, column_place(z_low))
+        stats += rows[:, :128].astype(f32)
     packed = dot(row_place((40, 64), 0, 1), total.astype(bf16))
     row = iota((64, 128), 0) & 15
     stats = jnp.where((row >= SPARE) & (row < SPARE + 3), stats, 0.0)
@@ -203,10 +208,11 @@
     extra = jnp.zeros((16, 256), f32)
     for n in range(5):
         extra += jnp.where(row == SPARE + n, sums[n : n + 1], 0.0)
-    extra = jnp.concatenate([extra] * 4, axis=0)
     rows = dot(row_place((64, 40), 1, 0), total.astype(bf16)).astype(bf16)
     for z_low in range(4):
-        out[z_low] = (dot_nt(rows, column_place(z_low)) + extra).astype(bf16)
+        block = dot_nt(rows, column_place(z_low))
+        for a in range(4):
+            out[4 * a + z_low] = (block[16 * a : 16 * a + 16] + extra).astype(bf16)
 
 
 def turned(row):
@@ -352,8 +358,8 @@
 
     gain_row = chan_row(0)
     shift_row = chan_row(8)
-    grad_gain[...] = gain_row * scale
-    grad_shift[...] = shift_row * scale
+    grad_gain[...] = (gain_row * scale).reshape(CHANNELS)
+    grad_shift[...] = (shift_row * scale).reshape(CHANNELS)
     normed = (latent[...].astype(f32) - mean) * rstd
     value = g_here[:, :CELLS].astype(f32) + rstd * (
         turned(gain[...]) * pre_grad[...] - over_group(shift_row) - normed * over_group(gain_row)
@@ -407,26 +413,34 @@
     group = jnp.arange(CHANNELS, dtype=jnp.int32) // GROUP_SIZE
     group_column = group[:, None]
 
-    shard = jnp.concatenate([w_spatial, w_temporal], axis=1)
-    shard = jnp.pad(shard, ((0, 6), (0, 16)))
     near = call(
-        start_kernel, shape((16, 16, 256), bf16), smem=1, inputs=4, flops=1 << 20, moved=1 << 18
-    )(place, latent, group_column, shard)
-    near = exchange(near, ROW_Z).reshape(4, 64, 256)
-    packed = call(pack_kernel, shape((16, 40, PACK), bf16), flops=1 << 27, moved=3 << 19)(near)
-    w_own = exchange(packed, PLANE).reshape(4, 160, PACK)
+        start_kernel,
+        shape((16, 16, 256), bf16),
+        smem=1,
+        inputs=5,
+        scratch=(pltpu.VMEM((16, 256), f32), pltpu.VMEM((16, 256), f32)),
+        flops=1 << 20,
+        moved=1 << 18,
+    )(place, latent, group_column, w_spatial, w_temporal)
+    near = exchange(near, ROW_Z)
 
     both = jnp.stack([latent, grad])
     tall = height == 16
     last = jnp.where(tall, both[:, :, 240:256], both[:, :, 112:128])
     above = step_by(last, TILE, 1)
     below = step_by(both[:, :, :COLUMNS], TILE, -1)
-    w_own, above, below = lax.optimization_barrier((w_own, above, below))
-    w_other = swap_cores(w_own)
+    near, above, below = lax.optimization_barrier((near, above, below))
+    packed = call(pack_kernel, shape((16, 40, PACK), bf16), flops=1 << 27, moved=3 << 19)(
+        near
+    )
+    w_own = exchange(packed, PLANE).reshape(4, 160, PACK)
+
     latent_ext = extended(latent, above[0], below[0])
     grad_ext = extended(grad, above[1], below[1])
     grad_last = step_by(grad_ext, FRAME, 1)
     grad_next = step_by(grad_ext, FRAME, -1)
+    w_own, grad_last, grad_next = lax.optimization_barrier((w_own, grad_last, grad_next))
+    w_other = swap_cores(w_own)
 
     packed_row = jnp.arange(CHANNELS, dtype=jnp.int32)
     half, rest = packed_row // 160, packed_row % 160
@@ -459,16 +473,16 @@
         grad_own.reshape(blocks), swap_cores(grad_other).reshape(blocks)
     )
     terms = exchange(pair, PLANE)
-    parts = call(unpack_kernel, shape((4, 64, 256), bf16), flops=1 << 27, moved=1 << 21)(terms)
-    parts = exchange(parts.reshape(16, 16, 256), ROW_Z)
+    parts = call(unpack_kernel, shape((16, 16, 256), bf16), flops=1 << 27, moved=1 << 21)(terms)
+    parts = exchange(parts, ROW_Z)
     grad_input, grad_spatial, grad_temporal, grad_gain, grad_shift = call(
         end_kernel,
         (
             shape((CHANNELS, CELLS), bf16),
             shape((10, 180), f32),
             shape((10, 60), f32),
-            shape((1, CHANNELS), f32),
-            shape((1, CHANNELS), f32),
+            shape((CHANNELS,), f32),
+            shape((CHANNELS,), f32),
         ),
         smem=1,
         inputs=9,
@@ -477,7 +491,7 @@
     )(
         place, norm, gain_row, group_column, group[None, :], latent, grad_ext, pre_grad, parts,
     )
-    return grad_input[None], grad_spatial, grad_temporal, grad_gain[0], grad_shift[0]
+    return grad_input[None], grad_spatial, grad_temporal, grad_gain, grad_shift
 
 
 def solution(mesh):

time: 149 us -> 146 us (0.980)
  blocking collectives: 58.1 us -> 23.4 us
  starting transfers between devices: 29.9 us -> 59 us
    all_to_all x2 -> x1, blocking collectives: 58.1 us -> 23.4 us  [exchange(): return lax.all_to_all(blocks, axes, 0, 0, tiled=True)]
    all_to_all x2 -> x3, starting transfers between devices: 17.7 us -> 42.5 us  [exchange(): return lax.all_to_all(blocks, axes, 0, 0, tiled=True)]
    all_to_all x2 -> x3, waiting for transfers between devices: 27.6 us -> 20.1 us  [exchange(): return lax.all_to_all(blocks, axes, 0, 0, tiled=True)]
    ppermute x4, waiting for transfers between devices: 8.76 us -> 15.2 us  [step_by(): return lax.ppermute(value, axes, pairs)]
    ppermute x2, starting transfers between devices: 3.83 us -> 8.09 us  [swap_cores(): return lax.ppermute(value, 'tile_2', [(0, 1), (1, 0)])]
    ppermute x2, waiting for transfers between devices: 3 us -> 4.89 us  [swap_cores(): return lax.ppermute(value, 'tile_2', [(0, 1), (1, 0)])]
  transfers between devices with their start and end apart: 8 -> 9, of which waited for: 6 -> 8; matrix products, arithmetic and copies ran while one was open for 1% -> 1% of each run, Pallas kernels for 0% -> 0%
where the time goes in v3:
time: 146 us; the launch traced here: 145 us
  starting transfers between devices  59 us (40%)
  waiting for transfers between devices  40.3 us (28%)
  blocking collectives  23.4 us (16%)
  Pallas kernels  16.5 us (11%)
  local copies, waits for them, and re-layouts  2.43 us (2%)
  other arithmetic  1.87 us (1%)
  between operations  1.53 us (1%)
    all_to_all x3, starting transfers between devices, exchange(): return lax.all_to_all(blocks, axes, 0, 0, tiled=True)  42.5 us
    all_to_all x1, blocking collectives, exchange(): return lax.all_to_all(blocks, axes, 0, 0, tiled=True)  23.4 us
    all_to_all x3, waiting for transfers between devices, exchange(): return lax.all_to_all(blocks, axes, 0, 0, tiled=True)  20.1 us
    ppermute x4, waiting for transfers between devices, step_by(): return lax.ppermute(value, axes, pairs)  15.2 us
    ppermute x4, starting transfers between devices, step_by(): return lax.ppermute(value, axes, pairs)  8.44 us
    ppermute x2, starting transfers between devices, swap_cores(): return lax.ppermute(value, 'tile_2', [(0, 1), (1, 0)])  8.09 us
    pallas_call x1, Pallas kernels, local(): call(main_kernel, (block, block, shape((CHANNELS, CELLS), f32), shape((CH...  7.53 us
    ppermute x2, waiting for transfers between devices, swap_cores(): return lax.ppermute(value, 'tile_2', [(0, 1), (1, 0)])  4.89 us
  transfers between devices with their start and end apart: 9, of which 8 were waited for; matrix products, arithmetic and copies ran while one was open for 1% of the time, Pallas kernels for 0%

profile of v3, /device:TPU:32, one launch (start us, length us, event | category | flops | bytes accessed | tf_op | source)
XLA Modules:
  0.0 145.0 jit_solution(11944276371279419095)
XLA Ops:
  3.7 1.5 %shard_map.110 = bf16[16,16,256]{2,1,0:T(8,128)(2,1)} custom-call(s32[2]{0:T(128)S(1)} %pad_add_fusion.place, bf16[320,256]{1,0:T(8,128)(2,1)S(1)} %bitcast.19, s32[320,1]{1,0:T(8,128)S(1)} %add_select_fusion.group, bf16[10,180]{1,0:T(8,128)(2,1)S(1)} %copy-done.2, bf16[10,60]{1,0:T(8,128)(2,1)S(1)} %copy-done.3), custom_call_target="tpu_custom_call" | custom-call | flops 1048576 | bytes 262144 | tf_op jit(solution)/shard_map/pallas_call | solution.py:416
  5.2 15.2 %all-to-all-start = ((bf16[16,16,256]{2,1,0:T(8,128)(2,1)}), bf16[16,16,256]{2,1,0:T(8,128)(2,1)S(1)}, u32[]{:S(2)}, u32[]{:S(2)}) async-start(bf16[16,16,256]{2,1,0:T(8,128)(2,1)} %shard_map.110), calls=%async_computation | async-start | bytes 262144 | tf_op jit(solution)/shard_map/all_to_all | solution.py:58
  21.6 1.3 collective-permute-start
  22.9 1.3 collective-permute-start.1
  24.2 7.6 %collective-permute-done.1 = bf16[2,320,16]{2,1,0:T(8,128)(2,1)S(1)} collective-permute-done((bf16[2,320,16]{2,1,0:T(8,128)(2,1)S(1)}, bf16[2,320,16]{2,1,0:T(8,128)(2,1)S(1)}, u32[]{:S(2)}, u32[]{:S(2)}) %collective-permute-start.1) | collective-permute-done | bytes 20512 | tf_op jit(solution)/shard_map/ppermute | solution.py:392
  31.8 2.9 %all-to-all-done.blocks = bf16[16,16,256]{2,1,0:T(8,128)(2,1)S(1)} async-done(((bf16[16,16,256]{2,1,0:T(8,128)(2,1)}), bf16[16,16,256]{2,1,0:T(8,128)(2,1)S(1)}, u32[]{:S(2)}, u32[]{:S(2)}) %all-to-all-start) | async-done | bytes 131104 | tf_op jit(solution)/shard_map/all_to_all | solution.py:58
  34.7 1.6 %shard_map.111 = bf16[16,40,1024]{2,1,0:T(8,128)(2,1)} custom-call(bf16[16,16,256]{2,1,0:T(8,128)(2,1)S(1)} %all-to-all-done.blocks), custom_call_target="tpu_custom_call" | custom-call | flops 134217728 | bytes 1572864 | tf_op jit(solution)/shard_map/pallas_call | solution.py:433
  36.3 12.1 %all-to-all-start.1 = ((bf16[16,40,1024]{2,1,0:T(8,128)(2,1)}), bf16[16,40,1024]{2,1,0:T(8,128)(2,1)S(1)}, u32[]{:S(2)}, u32[]{:S(2)}) async-start(bf16[16,40,1024]{2,1,0:T(8,128)(2,1)} %shard_map.111), calls=%async_computation.1 | async-start | bytes 2621440 | tf_op jit(solution)/shard_map/all_to_all | solution.py:58
  48.7 2.6 %collective-permute-start.2 = (bf16[320,384]{1,0:T(8,128)(2,1)S(1)}, bf16[320,384]{1,0:T(8,128)(2,1)S(1)}, u32[]{:S(2)}, u32[]{:S(2)}) collective-permute-start(bf16[320,384]{1,0:T(8,128)(2,1)S(1)} %get-tuple-element.41.g_here), channel_id=1, source_target_pairs={{0,32},{32,64},{64,96},{96,128},{128,160},{160,192},{192,224},{224... | collective-permute-start | bytes 737288 | tf_op jit(solution)/shard_map/ppermute | solution.py:392
  51.3 3.3 %collective-permute-start.3 = (bf16[320,384]{1,0:T(8,128)(2,1)S(1)}, bf16[320,384]{1,0:T(8,128)(2,1)S(1)}, u32[]{:S(2)}, u32[]{:S(2)}) collective-permute-start(bf16[320,384]{1,0:T(8,128)(2,1)S(1)} %get-tuple-element.41.g_here), channel_id=1, source_target_pairs={{32,0},{64,32},{96,64},{128,96},{160,128},{192,160},{224,192},{256... | collective-permute-start | bytes 737288 | tf_op jit(solution)/shard_map/ppermute | solution.py:392
  54.6 2.2 %collective-permute-done.2.g_last = bf16[320,384]{1,0:T(8,128)(2,1)S(1)} collective-permute-done((bf16[320,384]{1,0:T(8,128)(2,1)S(1)}, bf16[320,384]{1,0:T(8,128)(2,1)S(1)}, u32[]{:S(2)}, u32[]{:S(2)}) %collective-permute-start.2) | collective-permute-done | bytes 245792 | tf_op jit(solution)/shard_map/ppermute | solution.py:392
  56.8 5.4 %collective-permute-done.3.g_next = bf16[320,384]{1,0:T(8,128)(2,1)S(1)} collective-permute-done((bf16[320,384]{1,0:T(8,128)(2,1)S(1)}, bf16[320,384]{1,0:T(8,128)(2,1)S(1)}, u32[]{:S(2)}, u32[]{:S(2)}) %collective-permute-start.3) | collective-permute-done | bytes 245792 | tf_op jit(solution)/shard_map/ppermute | solution.py:392
  62.3 4.1 %all-to-all-done.1 = bf16[16,40,1024]{2,1,0:T(8,128)(2,1)S(1)} async-done(((bf16[16,40,1024]{2,1,0:T(8,128)(2,1)}), bf16[16,40,1024]{2,1,0:T(8,128)(2,1)S(1)}, u32[]{:S(2)}, u32[]{:S(2)}) %all-to-all-start.1) | async-done | bytes 1310752 | tf_op jit(solution)/shard_map/all_to_all | solution.py:58
  66.4 5.8 %collective-permute-start.4 = (bf16[4,160,1024]{2,1,0:T(8,128)(2,1)S(1)}, bf16[4,160,1024]{2,1,0:T(8,128)(2,1)}, u32[]{:S(2)}, u32[]{:S(2)}) collective-permute-start(bf16[4,160,1024]{2,1,0:T(8,128)(2,1)S(1)} %bitcast.22), channel_id=1, source_target_pairs={{0,1},{1,0},{2,3},{3,2},{4,5},{5,4},{6,7},{7,6},{8,9},{9,8},{10,11... | collective-permute-start | bytes 3932168 | tf_op jit(solution)/shard_map/ppermute | solution.py:396
  72.8 2.2 %collective-permute-done.4.w_other = bf16[4,160,1024]{2,1,0:T(8,128)(2,1)} collective-permute-done((bf16[4,160,1024]{2,1,0:T(8,128)(2,1)S(1)}, bf16[4,160,1024]{2,1,0:T(8,128)(2,1)}, u32[]{:S(2)}, u32[]{:S(2)}) %collective-permute-start.4) | collective-permute-done | bytes 1310752 | tf_op jit(solution)/shard_map/ppermute | solution.py:396
  75.0 7.5 %shard_map.112 = (bf16[4,160,1024]{2,1,0:T(8,128)(2,1)S(1)}, bf16[4,160,1024]{2,1,0:T(8,128)(2,1)S(1)}, f32[320,256]{1,0:T(8,128)S(1)}, f32[320,128]{1,0:T(8,128)S(1)}) custom-call(s32[2]{0:T(128)S(1)} %pad_add_fusion.place, f32[1,320]{1,0:T(1,128)S(1)} %broadcast_in_dim.42.gain, f32[1,320]{1,0:T(1,128)S(1)} %broadcast_in_dim.43.shift, ...), custom_call_target="tpu_custom_call" | custom-call | flops 5368709120 | bytes 8388608 | tf_op jit(solution)/shard_map/pallas_call | solution.py:451
  82.6 2.3 %collective-permute-start.5 = (bf16[4,160,1024]{2,1,0:T(8,128)(2,1)S(1)}, bf16[4,160,1024]{2,1,0:T(8,128)(2,1)S(1)}, u32[]{:S(2)}, u32[]{:S(2)}) collective-permute-start(bf16[4,160,1024]{2,1,0:T(8,128)(2,1)S(1)} %get-tuple-element.29), channel_id=1, source_target_pairs={{0,1},{1,0},{2,3},{3,2},{4,5},{5,4},{6,7},{7,6},{8,9},{9,8},{10,11... | collective-permute-start | bytes 3932168 | tf_op jit(solution)/shard_map/ppermute | solution.py:396
  84.8 2.6 %collective-permute-done.5 = bf16[4,160,1024]{2,1,0:T(8,128)(2,1)S(1)} collective-permute-done((bf16[4,160,1024]{2,1,0:T(8,128)(2,1)S(1)}, bf16[4,160,1024]{2,1,0:T(8,128)(2,1)S(1)}, u32[]{:S(2)}, u32[]{:S(2)}) %collective-permute-start.5) | collective-permute-done | bytes 1310752 | tf_op jit(solution)/shard_map/ppermute | solution.py:396
  87.5 2.5 %shard_map.113 = bf16[16,40,1024]{2,1,0:T(8,128)(2,1)S(1)} custom-call(bf16[16,40,1024]{2,1,0:T(8,128)(2,1)S(1)} %bitcast.24, bf16[16,40,1024]{2,1,0:T(8,128)(2,1)S(1)} %bitcast.25), custom_call_target="tpu_custom_call" | custom-call | flops 1048576 | bytes 4194304 | tf_op jit(solution)/shard_map/pallas_call | solution.py:472
  90.0 23.4 %all_to_all.20.terms = bf16[16,40,1024]{2,1,0:T(8,128)(2,1)S(1)} all-to-all(bf16[16,40,1024]{2,1,0:T(8,128)(2,1)S(1)} %shard_map.113), channel_id=1, replica_groups=mesh['frame_0'=4,'frame_1'=4,'tile_0'=4,'tile_1'=4,'tile_2'=2] {'frame_0..., dimensions={0} | all-to-all | bytes 2621440 | tf_op jit(solution)/shard_map/all_to_all | solution.py:58
  113.4 1.4 shard_map.114
  114.7 15.2 %all-to-all-start.3 = ((bf16[16,16,256]{2,1,0:T(8,128)(2,1)}), bf16[16,16,256]{2,1,0:T(8,128)(2,1)S(1)}, u32[]{:S(2)}, u32[]{:S(2)}) async-start(bf16[16,16,256]{2,1,0:T(8,128)(2,1)} %shard_map.114), calls=%async_computation.3 | async-start | bytes 262144 | tf_op jit(solution)/shard_map/all_to_all | solution.py:58
  130.0 13.1 %all-to-all-done.3.terms = bf16[16,16,256]{2,1,0:T(8,128)(2,1)S(1)} async-done(((bf16[16,16,256]{2,1,0:T(8,128)(2,1)}), bf16[16,16,256]{2,1,0:T(8,128)(2,1)S(1)}, u32[]{:S(2)}, u32[]{:S(2)}) %all-to-all-start.3) | async-done | bytes 131104 | tf_op jit(solution)/shard_map/all_to_all | solution.py:58
  143.1 1.9 %shard_map.115 = (bf16[320,256]{1,0:T(8,128)(2,1)}, f32[10,180]{1,0:T(8,128)}, f32[10,60]{1,0:T(8,128)}, f32[320]{0:T(512)}, f32[320]{0:T(512)}) custom-call(s32[2]{0:T(128)S(1)} %pad_add_fusion.place, f32[320,128]{1,0:T(8,128)S(1)} %get-tuple-element.26.norm, f32[1,320]{1,0:T(1,128)S(1)} %broadcast_in_dim.42.gain, s32[320,1]{1,0:T(8,128)S(1)} %add_select_fusion.group, ...), custom_call_target="tpu_custom_call" | custom-call | flops 4194304 | bytes 1048576 | tf_op jit(solution)/shard_map/pallas_call | solution.py:478
  (30 shorter events, 4.3 us)
Async XLA Ops:
  0.6 20.8 %copy-start.1 = (bf16[1,320,256]{2,1,0:T(8,128)(2,1)S(1)}, bf16[1,320,256]{2,1,0:T(8,128)(2,1)}, u32[]{:S(2)}) copy-start(bf16[1,320,256]{2,1,0:T(8,128)(2,1)} %param.7) | copy-start | bytes 491524
  1.4 0.9 copy-start
  2.4 0.7 copy-start.2
  3.1 0.7 copy-start.3
  5.2 29.4 %all-to-all-start = ((bf16[16,16,256]{2,1,0:T(8,128)(2,1)}), bf16[16,16,256]{2,1,0:T(8,128)(2,1)S(1)}, u32[]{:S(2)}, u32[]{:S(2)}) async-start(bf16[16,16,256]{2,1,0:T(8,128)(2,1)} %shard_map.110), calls=%async_computation | async-start | bytes 262144 | tf_op jit(solution)/shard_map/all_to_all | solution.py:58
  21.6 2.6 %collective-permute-start = (bf16[2,320,16]{2,1,0:T(8,128)(2,1)S(1)}, bf16[2,320,16]{2,1,0:T(8,128)(2,1)S(1)}, u32[]{:S(2)}, u32[]{:S(2)}) collective-permute-start(bf16[2,320,16]{2,1,0:T(8,128)(2,1)S(1)} %get-tuple-element.36), channel_id=1, source_target_pairs={{0,1},{1,2},{2,3},{3,4},{4,5},{5,6},{6,7},{7,8},{8,9},{9,10},{10,1... | collective-permute-start | bytes 61448 | tf_op jit(solution)/shard_map/ppermute | solution.py:392
  22.9 8.9 %collective-permute-start.1 = (bf16[2,320,16]{2,1,0:T(8,128)(2,1)S(1)}, bf16[2,320,16]{2,1,0:T(8,128)(2,1)S(1)}, u32[]{:S(2)}, u32[]{:S(2)}) collective-permute-start(bf16[2,320,16]{2,1,0:T(8,128)(2,1)S(1)} %get-tuple-element.35), channel_id=1, source_target_pairs={{1,0},{2,1},{3,2},{4,3},{5,4},{6,5},{7,6},{8,7},{9,8},{10,9},{11,1... | collective-permute-start | bytes 61448 | tf_op jit(solution)/shard_map/ppermute | solution.py:392
  36.3 12.2 %copy-start.4 = (bf16[1,320,256]{2,1,0:T(8,128)(2,1)S(1)}, bf16[1,320,256]{2,1,0:T(8,128)(2,1)}, u32[]{:S(2)}) copy-start(bf16[1,320,256]{2,1,0:T(8,128)(2,1)} %param.8) | copy-start | bytes 491524
  36.3 30.1 %all-to-all-start.1 = ((bf16[16,40,1024]{2,1,0:T(8,128)(2,1)}), bf16[16,40,1024]{2,1,0:T(8,128)(2,1)S(1)}, u32[]{:S(2)}, u32[]{:S(2)}) async-start(bf16[16,40,1024]{2,1,0:T(8,128)(2,1)} %shard_map.111), calls=%async_computation.1 | async-start | bytes 2621440 | tf_op jit(solution)/shard_map/all_to_all | solution.py:58
  48.4 23.8 %copy-start.5 = (f32[320]{0:T(512)S(1)}, f32[320]{0:T(512)}, u32[]{:S(2)}) copy-start(f32[320]{0:T(512)} %param.11) | copy-start | bytes 3844
  48.4 23.9 %copy-start.6 = (f32[320]{0:T(512)S(1)}, f32[320]{0:T(512)}, u32[]{:S(2)}) copy-start(f32[320]{0:T(512)} %param.12) | copy-start | bytes 3844
  48.7 8.1 %collective-permute-start.2 = (bf16[320,384]{1,0:T(8,128)(2,1)S(1)}, bf16[320,384]{1,0:T(8,128)(2,1)S(1)}, u32[]{:S(2)}, u32[]{:S(2)}) collective-permute-start(bf16[320,384]{1,0:T(8,128)(2,1)S(1)} %get-tuple-element.41.g_here), channel_id=1, source_target_pairs={{0,32},{32,64},{64,96},{96,128},{128,160},{160,192},{192,224},{224... | collective-permute-start | bytes 737288 | tf_op jit(solution)/shard_map/ppermute | solution.py:392
  51.3 10.9 %collective-permute-start.3 = (bf16[320,384]{1,0:T(8,128)(2,1)S(1)}, bf16[320,384]{1,0:T(8,128)(2,1)S(1)}, u32[]{:S(2)}, u32[]{:S(2)}) collective-permute-start(bf16[320,384]{1,0:T(8,128)(2,1)S(1)} %get-tuple-element.41.g_here), channel_id=1, source_target_pairs={{32,0},{64,32},{96,64},{128,96},{160,128},{192,160},{224,192},{256... | collective-permute-start | bytes 737288 | tf_op jit(solution)/shard_map/ppermute | solution.py:392
  66.4 8.6 %collective-permute-start.4 = (bf16[4,160,1024]{2,1,0:T(8,128)(2,1)S(1)}, bf16[4,160,1024]{2,1,0:T(8,128)(2,1)}, u32[]{:S(2)}, u32[]{:S(2)}) collective-permute-start(bf16[4,160,1024]{2,1,0:T(8,128)(2,1)S(1)} %bitcast.22), channel_id=1, source_target_pairs={{0,1},{1,0},{2,3},{3,2},{4,5},{5,4},{6,7},{7,6},{8,9},{9,8},{10,11... | collective-permute-start | bytes 3932168 | tf_op jit(solution)/shard_map/ppermute | solution.py:396
  82.6 4.9 %collective-permute-start.5 = (bf16[4,160,1024]{2,1,0:T(8,128)(2,1)S(1)}, bf16[4,160,1024]{2,1,0:T(8,128)(2,1)S(1)}, u32[]{:S(2)}, u32[]{:S(2)}) collective-permute-start(bf16[4,160,1024]{2,1,0:T(8,128)(2,1)S(1)} %get-tuple-element.29), channel_id=1, source_target_pairs={{0,1},{1,0},{2,3},{3,2},{4,5},{5,4},{6,7},{7,6},{8,9},{9,8},{10,11... | collective-permute-start | bytes 3932168 | tf_op jit(solution)/shard_map/ppermute | solution.py:396
  114.7 28.3 %all-to-all-start.3 = ((bf16[16,16,256]{2,1,0:T(8,128)(2,1)}), bf16[16,16,256]{2,1,0:T(8,128)(2,1)S(1)}, u32[]{:S(2)}, u32[]{:S(2)}) async-start(bf16[16,16,256]{2,1,0:T(8,128)(2,1)} %shard_map.114), calls=%async_computation.3 | async-start | bytes 262144 | tf_op jit(solution)/shard_map/all_to_all | solution.py:58

commit v4 on v3

--- a/solution.py
+++ b/solution.py
@@ -1,5 +1,3 @@
-import functools
-
 import jax
 import jax.numpy as jnp
 from jax import lax
@@ -13,7 +11,6 @@
 CHANNELS = 320
 COLUMNS = 16
 STRIPS = 32
-FRAMES = 16
 CELLS = 256
 EXT = 384
 BELOW = 256
@@ -31,7 +28,6 @@
 FRAME = ("frame_0", "frame_1")
 ROW_Z = ("tile_1", "frame_1")
 PLANE = ("frame_0", "tile_0")
-PLANE_CORE = ("frame_0", "tile_0", "tile_2")
 
 bf16 = jnp.bfloat16
 f32 = jnp.float32
@@ -190,7 +186,7 @@
         out[n] = with_tile(total, tile).astype(bf16)
         return 0
 
-    lax.fori_loop(0, 16, body, 0)
+    lax.fori_loop(0, 16, body, 0, unroll=4)
 
 
 def unpack_kernel(terms, out):
@@ -327,7 +323,7 @@
 
 
 def end_kernel(
-    place, norm, gain, group, group_row, latent, g_here, pre_grad, terms,
+    place, norm, gain, group, latent, g_here, pre_grad, terms,
     result, grad_s, grad_t, grad_gain, grad_shift,
 ):
     height = place[0]
@@ -347,7 +343,8 @@
     channel = iota((CHANNELS, 128), 0)
     spot = ((channel >> 3) & 7) * 16 + (channel & 7)
     lane = iota((CHANNELS, 128), 1)
-    same = group[...] == group_row[...]
+    eye = iota((CHANNELS, CHANNELS), 0) == iota((CHANNELS, CHANNELS), 1)
+    same = group[...] == jnp.sum(jnp.where(eye, group[...], 0), axis=0, keepdims=True)
 
     def chan_row(offset):
         column = jnp.sum(jnp.where(lane == spot + offset, wide, 0.0), axis=1, keepdims=True)
@@ -485,11 +482,11 @@
             shape((CHANNELS,), f32),
         ),
         smem=1,
-        inputs=9,
+        inputs=8,
         flops=1 << 22,
         moved=1 << 20,
     )(
-        place, norm, gain_row, group_column, group[None, :], latent, grad_ext, pre_grad, parts,
+        place, norm, gain_row, group_column, latent, grad_ext, pre_grad, parts,
     )
     return grad_input[None], grad_spatial, grad_temporal, grad_gain, grad_shift
 

time: 146 us -> 142 us (0.973)
  blocking collectives: 23.4 us -> 51.8 us
  waiting for transfers between devices: 40.3 us -> 23.7 us
  starting transfers between devices: 59 us -> 43.4 us
  local copies, waits for them, and re-layouts: 2.43 us -> 5.7 us
  Pallas kernels: 16.5 us -> 13.4 us
    all_to_all x1 -> x2, blocking collectives: 23.4 us -> 51.8 us  [exchange(): return lax.all_to_all(blocks, axes, 0, 0, tiled=True)]
    all_to_all x3 -> x2, starting transfers between devices: 42.5 us -> 29.2 us  [exchange(): return lax.all_to_all(blocks, axes, 0, 0, tiled=True)]
    ppermute x4, waiting for transfers between devices: 15.2 us -> 6.24 us  [step_by(): return lax.ppermute(value, axes, pairs)]
    all_to_all x3 -> x2, waiting for transfers between devices: 20.1 us -> 12.1 us  [exchange(): return lax.all_to_all(blocks, axes, 0, 0, tiled=True)]
    ppermute x2, starting transfers between devices: 8.09 us -> 3.96 us  [swap_cores(): return lax.ppermute(value, 'tile_2', [(0, 1), (1, 0)])]
    unnamed x14 -> x22, local copies, waits for them, and re-layouts: 2.32 us -> 5.59 us
    ppermute x4, starting transfers between devices: 8.44 us -> 10.2 us  [step_by(): return lax.ppermute(value, axes, pairs)]
    pallas_call x1, Pallas kernels: 2.49 us -> 0.86 us  [local(): call(pair_kernel, shape(blocks, bf16), inputs=2, flops=1 << 20, moved=1 <...]
  transfers between devices with their start and end apart: 9 -> 8, of which waited for: 8 -> 7; matrix products, arithmetic and copies ran while one was open for 1% -> 1% of each run, Pallas kernels for 0% -> 0%
where the time goes in v4:
time: 142 us; the launch traced here: 141 us
  blocking collectives  51.8 us (36%)
  starting transfers between devices  43.4 us (31%)
  waiting for transfers between devices  23.7 us (17%)
  Pallas kernels  13.4 us (9%)
  local copies, waits for them, and re-layouts  5.7 us (4%)
  other arithmetic  1.86 us (1%)
  between operations  1.53 us (1%)
    all_to_all x2, blocking collectives, exchange(): return lax.all_to_all(blocks, axes, 0, 0, tiled=True)  51.8 us
    all_to_all x2, starting transfers between devices, exchange(): return lax.all_to_all(blocks, axes, 0, 0, tiled=True)  29.2 us
    all_to_all x2, waiting for transfers between devices, exchange(): return lax.all_to_all(blocks, axes, 0, 0, tiled=True)  12.1 us
    ppermute x4, starting transfers between devices, step_by(): return lax.ppermute(value, axes, pairs)  10.2 us
    pallas_call x1, Pallas kernels, local(): call(main_kernel, (block, block, shape((CHANNELS, CELLS), f32), shape((CH...  6.79 us
    ppermute x4, waiting for transfers between devices, step_by(): return lax.ppermute(value, axes, pairs)  6.24 us
    unnamed x22, local copies, waits for them, and re-layouts  5.59 us
    ppermute x2, waiting for transfers between devices, swap_cores(): return lax.ppermute(value, 'tile_2', [(0, 1), (1, 0)])  5.35 us
  transfers between devices with their start and end apart: 8, of which 7 were waited for; matrix products, arithmetic and copies ran while one was open for 1% of the time, Pallas kernels for 0%

profile of v4, /device:TPU:32, one launch (start us, length us, event | category | flops | bytes accessed | tf_op | source)
XLA Modules:
  0.0 141.3 jit_solution(3728003872511721021)
XLA Ops:
  3.7 1.5 %shard_map.110 = bf16[16,16,256]{2,1,0:T(8,128)(2,1)} custom-call(s32[2]{0:T(128)S(1)} %pad_add_fusion.place, bf16[320,256]{1,0:T(8,128)(2,1)S(1)} %bitcast.19, s32[320,1]{1,0:T(8,128)S(1)} %add_select_fusion.group, bf16[10,180]{1,0:T(8,128)(2,1)S(1)} %copy-done.2, bf16[10,60]{1,0:T(8,128)(2,1)S(1)} %copy-done.3), custom_call_target="tpu_custom_call" | custom-call | flops 1048576 | bytes 262144 | tf_op jit(solution)/shard_map/pallas_call | solution.py:413
  5.2 15.2 %all-to-all-start = ((bf16[16,16,256]{2,1,0:T(8,128)(2,1)}), bf16[16,16,256]{2,1,0:T(8,128)(2,1)S(1)}, u32[]{:S(2)}, u32[]{:S(2)}) async-start(bf16[16,16,256]{2,1,0:T(8,128)(2,1)} %shard_map.110), calls=%async_computation | async-start | bytes 262144 | tf_op jit(solution)/shard_map/all_to_all | solution.py:54
  20.5 0.9 broadcast_select_fusion
  21.6 1.3 collective-permute-start.1
  22.9 3.0 %collective-permute-start = (bf16[2,320,16]{2,1,0:T(8,128)(2,1)S(1)}, bf16[2,320,16]{2,1,0:T(8,128)(2,1)S(1)}, u32[]{:S(2)}, u32[]{:S(2)}) collective-permute-start(bf16[2,320,16]{2,1,0:T(8,128)(2,1)S(1)} %get-tuple-element.36), channel_id=1, source_target_pairs={{0,1},{1,2},{2,3},{3,4},{4,5},{5,6},{6,7},{7,8},{8,9},{9,10},{10,1... | collective-permute-start | bytes 61448 | tf_op jit(solution)/shard_map/ppermute | solution.py:389
  25.9 1.0 collective-permute-done
  26.9 7.8 %all-to-all-done.blocks = bf16[16,16,256]{2,1,0:T(8,128)(2,1)S(1)} async-done(((bf16[16,16,256]{2,1,0:T(8,128)(2,1)}), bf16[16,16,256]{2,1,0:T(8,128)(2,1)S(1)}, u32[]{:S(2)}, u32[]{:S(2)}) %all-to-all-start) | async-done | bytes 131104 | tf_op jit(solution)/shard_map/all_to_all | solution.py:54
  34.7 1.6 %shard_map.111 = bf16[16,40,1024]{2,1,0:T(8,128)(2,1)} custom-call(bf16[16,16,256]{2,1,0:T(8,128)(2,1)S(1)} %all-to-all-done.blocks), custom_call_target="tpu_custom_call" | custom-call | flops 134217728 | bytes 1572864 | tf_op jit(solution)/shard_map/pallas_call | solution.py:430
  36.3 14.0 %all-to-all-start.1 = ((bf16[16,40,1024]{2,1,0:T(8,128)(2,1)}), bf16[16,40,1024]{2,1,0:T(8,128)(2,1)S(1)}, u32[]{:S(2)}, u32[]{:S(2)}) async-start(bf16[16,40,1024]{2,1,0:T(8,128)(2,1)} %shard_map.111), calls=%async_computation.1 | async-start | bytes 2621440 | tf_op jit(solution)/shard_map/all_to_all | solution.py:54
  50.7 3.7 %collective-permute-start.3 = (bf16[320,384]{1,0:T(8,128)(2,1)S(1)}, bf16[320,384]{1,0:T(8,128)(2,1)S(1)}, u32[]{:S(2)}, u32[]{:S(2)}) collective-permute-start(bf16[320,384]{1,0:T(8,128)(2,1)S(1)} %get-tuple-element.41.g_here), channel_id=1, source_target_pairs={{32,0},{64,32},{96,64},{128,96},{160,128},{192,160},{224,192},{256... | collective-permute-start | bytes 737288 | tf_op jit(solution)/shard_map/ppermute | solution.py:389
  54.4 2.1 %collective-permute-start.2 = (bf16[320,384]{1,0:T(8,128)(2,1)S(1)}, bf16[320,384]{1,0:T(8,128)(2,1)S(1)}, u32[]{:S(2)}, u32[]{:S(2)}) collective-permute-start(bf16[320,384]{1,0:T(8,128)(2,1)S(1)} %get-tuple-element.41.g_here), channel_id=1, source_target_pairs={{0,32},{32,64},{64,96},{96,128},{128,160},{160,192},{192,224},{224... | collective-permute-start | bytes 737288 | tf_op jit(solution)/shard_map/ppermute | solution.py:389
  56.6 3.0 %collective-permute-done.3.g_next = bf16[320,384]{1,0:T(8,128)(2,1)S(1)} collective-permute-done((bf16[320,384]{1,0:T(8,128)(2,1)S(1)}, bf16[320,384]{1,0:T(8,128)(2,1)S(1)}, u32[]{:S(2)}, u32[]{:S(2)}) %collective-permute-start.3) | collective-permute-done | bytes 245792 | tf_op jit(solution)/shard_map/ppermute | solution.py:389
  60.3 2.3 %collective-permute-done.2.g_last = bf16[320,384]{1,0:T(8,128)(2,1)S(1)} collective-permute-done((bf16[320,384]{1,0:T(8,128)(2,1)S(1)}, bf16[320,384]{1,0:T(8,128)(2,1)S(1)}, u32[]{:S(2)}, u32[]{:S(2)}) %collective-permute-start.2) | collective-permute-done | bytes 245792 | tf_op jit(solution)/shard_map/ppermute | solution.py:389
  63.2 4.3 %all-to-all-done.1 = bf16[16,40,1024]{2,1,0:T(8,128)(2,1)S(1)} async-done(((bf16[16,40,1024]{2,1,0:T(8,128)(2,1)}), bf16[16,40,1024]{2,1,0:T(8,128)(2,1)S(1)}, u32[]{:S(2)}, u32[]{:S(2)}) %all-to-all-start.1) | async-done | bytes 1310752 | tf_op jit(solution)/shard_map/all_to_all | solution.py:54
  67.6 1.9 %collective-permute-start.4 = (bf16[4,160,1024]{2,1,0:T(8,128)(2,1)S(1)}, bf16[4,160,1024]{2,1,0:T(8,128)(2,1)S(1)}, u32[]{:S(2)}, u32[]{:S(2)}) collective-permute-start(bf16[4,160,1024]{2,1,0:T(8,128)(2,1)S(1)} %bitcast.22), channel_id=1, source_target_pairs={{0,1},{1,0},{2,3},{3,2},{4,5},{5,4},{6,7},{7,6},{8,9},{9,8},{10,11... | collective-permute-start | bytes 3932168 | tf_op jit(solution)/shard_map/ppermute | solution.py:393
  70.0 2.5 %collective-permute-done.4.w_other = bf16[4,160,1024]{2,1,0:T(8,128)(2,1)S(1)} collective-permute-done((bf16[4,160,1024]{2,1,0:T(8,128)(2,1)S(1)}, bf16[4,160,1024]{2,1,0:T(8,128)(2,1)S(1)}, u32[]{:S(2)}, u32[]{:S(2)}) %collective-permute-start.4) | collective-permute-done | bytes 1310752 | tf_op jit(solution)/shard_map/ppermute | solution.py:393
  72.5 0.9 copy-done.5
  73.4 0.9 copy-done.7
  74.4 6.8 %shard_map.112 = (bf16[4,160,1024]{2,1,0:T(8,128)(2,1)S(1)}, bf16[4,160,1024]{2,1,0:T(8,128)(2,1)S(1)}, f32[320,256]{1,0:T(8,128)S(1)}, f32[320,128]{1,0:T(8,128)S(1)}) custom-call(s32[2]{0:T(128)S(1)} %pad_add_fusion.place, f32[1,320]{1,0:T(1,128)S(1)} %broadcast_in_dim.41.gain, f32[1,320]{1,0:T(1,128)S(1)} %broadcast_in_dim.42.shift, ...), custom_call_target="tpu_custom_call" | custom-call | flops 5368709120 | bytes 8388608 | tf_op jit(solution)/shard_map/pallas_call | solution.py:448
  81.2 2.0 %collective-permute-start.5 = (bf16[4,160,1024]{2,1,0:T(8,128)(2,1)S(1)}, bf16[4,160,1024]{2,1,0:T(8,128)(2,1)S(1)}, u32[]{:S(2)}, u32[]{:S(2)}) collective-permute-start(bf16[4,160,1024]{2,1,0:T(8,128)(2,1)S(1)} %get-tuple-element.29), channel_id=1, source_target_pairs={{0,1},{1,0},{2,3},{3,2},{4,5},{5,4},{6,7},{7,6},{8,9},{9,8},{10,11... | collective-permute-start | bytes 3932168 | tf_op jit(solution)/shard_map/ppermute | solution.py:393
  83.2 2.9 %collective-permute-done.5 = bf16[4,160,1024]{2,1,0:T(8,128)(2,1)S(1)} collective-permute-done((bf16[4,160,1024]{2,1,0:T(8,128)(2,1)S(1)}, bf16[4,160,1024]{2,1,0:T(8,128)(2,1)S(1)}, u32[]{:S(2)}, u32[]{:S(2)}) %collective-permute-start.5) | collective-permute-done | bytes 1310752 | tf_op jit(solution)/shard_map/ppermute | solution.py:393
  87.0 24.5 %all_to_all.20.terms = bf16[16,40,1024]{2,1,0:T(8,128)(2,1)S(1)} all-to-all(bf16[16,40,1024]{2,1,0:T(8,128)(2,1)S(1)} %shard_map.113), channel_id=1, replica_groups=mesh['frame_0'=4,'frame_1'=4,'tile_0'=4,'tile_1'=4,'tile_2'=2] {'frame_0..., dimensions={0} | all-to-all | bytes 2621440 | tf_op jit(solution)/shard_map/all_to_all | solution.py:54
  112.1 27.3 %all_to_all.21.terms = bf16[16,16,256]{2,1,0:T(8,128)(2,1)S(1)} all-to-all(bf16[16,16,256]{2,1,0:T(8,128)(2,1)S(1)} %shard_map.114), channel_id=1, replica_groups=mesh['frame_0'=4,'frame_1'=4,'tile_0'=4,'tile_1'=4,'tile_2'=2] {'tile_1'..., dimensions={0} | all-to-all | bytes 262144 | tf_op jit(solution)/shard_map/all_to_all | solution.py:54
  139.4 1.9 %shard_map.115 = (bf16[320,256]{1,0:T(8,128)(2,1)}, f32[10,180]{1,0:T(8,128)}, f32[10,60]{1,0:T(8,128)}, f32[320]{0:T(512)}, f32[320]{0:T(512)}) custom-call(s32[2]{0:T(128)S(1)} %pad_add_fusion.place, f32[320,128]{1,0:T(8,128)S(1)} %get-tuple-element.26.norm, f32[1,320]{1,0:T(1,128)S(1)} %broadcast_in_dim.41.gain, s32[320,1]{1,0:T(8,128)S(1)} %add_select_fusion.group, ...), custom_call_target="tpu_custom_call" | custom-call | flops 4194304 | bytes 1048576 | tf_op jit(solution)/shard_map/pallas_call | solution.py:475
  (36 shorter events, 6.3 us)
Async XLA Ops:
  0.6 20.8 %copy-start.1 = (bf16[1,320,256]{2,1,0:T(8,128)(2,1)S(1)}, bf16[1,320,256]{2,1,0:T(8,128)(2,1)}, u32[]{:S(2)}) copy-start(bf16[1,320,256]{2,1,0:T(8,128)(2,1)} %param.7) | copy-start | bytes 491524
  1.4 0.9 copy-start
  2.4 0.7 copy-start.2
  3.1 0.7 copy-start.3
  5.2 29.4 %all-to-all-start = ((bf16[16,16,256]{2,1,0:T(8,128)(2,1)}), bf16[16,16,256]{2,1,0:T(8,128)(2,1)S(1)}, u32[]{:S(2)}, u32[]{:S(2)}) async-start(bf16[16,16,256]{2,1,0:T(8,128)(2,1)} %shard_map.110), calls=%async_computation | async-start | bytes 262144 | tf_op jit(solution)/shard_map/all_to_all | solution.py:54
  21.6 4.4 %collective-permute-start.1 = (bf16[2,320,16]{2,1,0:T(8,128)(2,1)S(1)}, bf16[2,320,16]{2,1,0:T(8,128)(2,1)S(1)}, u32[]{:S(2)}, u32[]{:S(2)}) collective-permute-start(bf16[2,320,16]{2,1,0:T(8,128)(2,1)S(1)} %get-tuple-element.35), channel_id=1, source_target_pairs={{1,0},{2,1},{3,2},{4,3},{5,4},{6,5},{7,6},{8,7},{9,8},{10,9},{11,1... | collective-permute-start | bytes 61448 | tf_op jit(solution)/shard_map/ppermute | solution.py:389
  22.9 4.0 %collective-permute-start = (bf16[2,320,16]{2,1,0:T(8,128)(2,1)S(1)}, bf16[2,320,16]{2,1,0:T(8,128)(2,1)S(1)}, u32[]{:S(2)}, u32[]{:S(2)}) collective-permute-start(bf16[2,320,16]{2,1,0:T(8,128)(2,1)S(1)} %get-tuple-element.36), channel_id=1, source_target_pairs={{0,1},{1,2},{2,3},{3,4},{4,5},{5,6},{6,7},{7,8},{8,9},{9,10},{10,1... | collective-permute-start | bytes 61448 | tf_op jit(solution)/shard_map/ppermute | solution.py:389
  36.3 14.2 %copy-start.8 = (bf16[1,320,256]{2,1,0:T(8,128)(2,1)S(1)}, bf16[1,320,256]{2,1,0:T(8,128)(2,1)}, u32[]{:S(2)}) copy-start(bf16[1,320,256]{2,1,0:T(8,128)(2,1)} %param.8) | copy-start | bytes 491524
  36.3 31.2 %all-to-all-start.1 = ((bf16[16,40,1024]{2,1,0:T(8,128)(2,1)}), bf16[16,40,1024]{2,1,0:T(8,128)(2,1)S(1)}, u32[]{:S(2)}, u32[]{:S(2)}) async-start(bf16[16,40,1024]{2,1,0:T(8,128)(2,1)} %shard_map.111), calls=%async_computation.1 | async-start | bytes 2621440 | tf_op jit(solution)/shard_map/all_to_all | solution.py:54
  50.4 19.1 %copy-start.9 = (f32[320]{0:T(512)S(1)}, f32[320]{0:T(512)}, u32[]{:S(2)}) copy-start(f32[320]{0:T(512)} %param.11) | copy-start | bytes 3844
  50.4 19.1 %copy-start.10 = (f32[320]{0:T(512)S(1)}, f32[320]{0:T(512)}, u32[]{:S(2)}) copy-start(f32[320]{0:T(512)} %param.12) | copy-start | bytes 3844
  50.7 8.8 %collective-permute-start.3 = (bf16[320,384]{1,0:T(8,128)(2,1)S(1)}, bf16[320,384]{1,0:T(8,128)(2,1)S(1)}, u32[]{:S(2)}, u32[]{:S(2)}) collective-permute-start(bf16[320,384]{1,0:T(8,128)(2,1)S(1)} %get-tuple-element.41.g_here), channel_id=1, source_target_pairs={{32,0},{64,32},{96,64},{128,96},{160,128},{192,160},{224,192},{256... | collective-permute-start | bytes 737288 | tf_op jit(solution)/shard_map/ppermute | solution.py:389
  54.4 8.1 %collective-permute-start.2 = (bf16[320,384]{1,0:T(8,128)(2,1)S(1)}, bf16[320,384]{1,0:T(8,128)(2,1)S(1)}, u32[]{:S(2)}, u32[]{:S(2)}) collective-permute-start(bf16[320,384]{1,0:T(8,128)(2,1)S(1)} %get-tuple-element.41.g_here), channel_id=1, source_target_pairs={{0,32},{32,64},{64,96},{96,128},{128,160},{160,192},{192,224},{224... | collective-permute-start | bytes 737288 | tf_op jit(solution)/shard_map/ppermute | solution.py:389
  59.6 0.7 copy-start.4
  62.5 0.7 copy-start.6
  67.6 4.9 %collective-permute-start.4 = (bf16[4,160,1024]{2,1,0:T(8,128)(2,1)S(1)}, bf16[4,160,1024]{2,1,0:T(8,128)(2,1)S(1)}, u32[]{:S(2)}, u32[]{:S(2)}) collective-permute-start(bf16[4,160,1024]{2,1,0:T(8,128)(2,1)S(1)} %bitcast.22), channel_id=1, source_target_pairs={{0,1},{1,0},{2,3},{3,2},{4,5},{5,4},{6,7},{7,6},{8,9},{9,8},{10,11... | collective-permute-start | bytes 3932168 | tf_op jit(solution)/shard_map/ppermute | solution.py:393
  72.5 0.9 copy-start.5
  73.4 0.9 copy-start.7
  81.2 4.9 %collective-permute-start.5 = (bf16[4,160,1024]{2,1,0:T(8,128)(2,1)S(1)}, bf16[4,160,1024]{2,1,0:T(8,128)(2,1)S(1)}, u32[]{:S(2)}, u32[]{:S(2)}) collective-permute-start(bf16[4,160,1024]{2,1,0:T(8,128)(2,1)S(1)} %get-tuple-element.29), channel_id=1, source_target_pairs={{0,1},{1,0},{2,3},{3,2},{4,5},{5,4},{6,7},{7,6},{8,9},{9,8},{10,11... | collective-permute-start | bytes 3932168 | tf_op jit(solution)/shard_map/ppermute | solution.py:393

commit v5 on v4

--- a/solution.py
+++ b/solution.py
@@ -86,9 +86,30 @@
     return jnp.concatenate([block[:, :TILE_AT], tile, block[:, WIDE:]], axis=1)
 
 
-def start_kernel(place, latent, group, w_spatial, w_temporal, out, left, right):
+def fetched(pairs, sems):
+    copies = [pltpu.make_async_copy(a, b, sems.at[n]) for n, (a, b) in enumerate(pairs)]
+    for copy in copies:
+        copy.start()
+    for copy in copies:
+        copy.wait()
+
+
+def start_kernel(
+    place, group, latent_at, grad_at, w_spatial_at, w_temporal_at, out, masked,
+    latent, grad, w_spatial, w_temporal, left, right, sems,
+):
+    fetched(
+        (
+            (latent_at, latent),
+            (grad_at, grad),
+            (w_spatial_at, w_spatial),
+            (w_temporal_at, w_temporal),
+        ),
+        sems,
+    )
     height = place[0]
     live = (iota((1, CELLS), 1) >> 4) < height
+    masked[...] = jnp.where(live, grad[...].astype(f32), 0.0).astype(bf16)
     value = jnp.where(live, latent[...].astype(f32), 0.0)
     chan_sum = jnp.sum(value, axis=1, keepdims=True)
     chan_square = jnp.sum(value * value, axis=1, keepdims=True)
@@ -110,6 +131,24 @@
     block = (left[...] + pltpu.roll(right[...], 180, 1) + extra).astype(bf16)
     for n in range(16):
         out[n] = block
+
+
+def row_move(set_index, first):
+    cell = iota((CELLS, 128), 0)
+    lane = iota((CELLS, 128), 1)
+    inside = (lane >> 4) == set_index
+    return zero_one(inside & (cell == first + (lane & 15)))
+
+
+def rows_kernel(place, latent, g_next, g_here, g_last, row_first, row_last):
+    last = (place[0] - 1) * COLUMNS
+    head = jnp.zeros((CHANNELS, 128), f32)
+    tail = jnp.zeros((CHANNELS, 128), f32)
+    for n, ref in enumerate((latent, g_next, g_here, g_last)):
+        head += dot(ref[...], row_move(n, 0))
+        tail += dot(ref[...], row_move(n, last))
+    row_first[...] = head.astype(bf16)
+    row_last[...] = tail.astype(bf16)
 
 
 def pack_kernel(blocks, out):
@@ -229,11 +268,30 @@
 
 
 def main_kernel(
-    place, gain, shift, order, order_row, group, latent, g_next, g_here, g_last,
-    w_own, w_other, grad_own, grad_other, pre_grad, norm, cols, turned_s, turned_t, frames, taps,
+    place, gain, shift, order, order_row, group, latent_own, g_here,
+    above_at, below_at, g_next_at, g_last_at, w_own, w_other, grad_own, grad_other, pre_grad, norm, cols, turned_s, turned_t, frames, taps,
+    g_next, g_last, above, below, sems,
 ):
+    copies = (
+        pltpu.make_async_copy(g_next_at, g_next, sems.at[0]),
+        pltpu.make_async_copy(g_last_at, g_last, sems.at[1]),
+        pltpu.make_async_copy(above_at, above, sems.at[2]),
+        pltpu.make_async_copy(below_at, below, sems.at[3]),
+    )
+    for copy in copies:
+        copy.start()
     height = place[0]
     strip = place[1]
+
+    def extended(own, set_index):
+        source = iota((128, 128), 0)
+        lane = iota((128, 128), 1)
+        from_set = (source >> 4) == set_index
+        low = from_set & (lane == (source & 15))
+        high = from_set & (lane == (source & 15) + (ABOVE - BELOW))
+        rows = dot(below[...], zero_one(low)) + dot(above[...], zero_one(high))
+        return jnp.concatenate([own, rows.astype(bf16)], axis=1)
+
     lane = iota((1, EXT), 1)
     live = ((lane < CELLS) & ((lane >> 4) < height)) | (
         (lane >= BELOW) & (lane < BELOW + COLUMNS) & (strip < STRIPS - 1)
@@ -247,19 +305,21 @@
         turned_s[y * SPAN : (y + 1) * SPAN, :] = across[:SPAN]
         turned_t[y * SPAN_T : (y + 1) * SPAN_T, :] = across[WIDE : WIDE + SPAN_T]
 
+    for copy in copies:
+        copy.wait()
     positions, mean, rstd = stat_columns(w_own, w_other, group[...])
     lane_n = iota((CHANNELS, 128), 1)
     norm[...] = jnp.where(lane_n == 0, mean, jnp.where(lane_n == 1, rstd, positions))
     gain_column = turned(gain[...])
     shift_column = turned(shift[...])
-    normed = (latent[...].astype(f32) - mean) * rstd
+    normed = (extended(latent_own[...], 0).astype(f32) - mean) * rstd
     pre_act = gain_column * normed + shift_column
     sigmoid = 1.0 / (1.0 + jnp.exp(-pre_act))
     active = jnp.where(live, pre_act * sigmoid, 0.0).astype(bf16)
 
     grad_spat = jnp.zeros((CHANNELS, EXT), f32)
     for k, ref in enumerate((g_next, g_here, g_last)):
-        packed = dot(to_packed, ref[...]).astype(bf16)
+        packed = dot(to_packed, extended(ref[...], 1 + k)).astype(bf16)
         taps[:, k * CELLS : (k + 1) * CELLS] = packed[:, :CELLS]
         grad_spat += dot(turned_t[k * CHANNELS : (k + 1) * CHANNELS, :], packed)
     grad_spat = jnp.where(live, grad_spat, 0.0).astype(bf16)
@@ -358,15 +418,17 @@
     grad_gain[...] = (gain_row * scale).reshape(CHANNELS)
     grad_shift[...] = (shift_row * scale).reshape(CHANNELS)
     normed = (latent[...].astype(f32) - mean) * rstd
-    value = g_here[:, :CELLS].astype(f32) + rstd * (
+    value = g_here[...].astype(f32) + rstd * (
         turned(gain[...]) * pre_grad[...] - over_group(shift_row) - normed * over_group(gain_row)
     )
     result[...] = jnp.where(own_live, value, 0.0).astype(bf16)
 
 
-def call(kernel, outs, smem=0, scratch=(), inputs=1, flops=0, moved=0, room=16):
+def call(kernel, outs, smem=0, scratch=(), inputs=1, apart=0, space=pltpu.HBM, flops=0, moved=0, room=16):
     vmem = pl.BlockSpec(memory_space=pltpu.VMEM)
     specs = [pl.BlockSpec(memory_space=pltpu.SMEM)] * smem + [vmem] * (inputs - smem)
+    for n in range(*apart) if apart else ():
+        specs[n] = pl.BlockSpec(memory_space=space)
     many = isinstance(outs, tuple)
     return pl.pallas_call(
         kernel,
@@ -393,50 +455,48 @@
     return lax.ppermute(value, "tile_2", [(0, 1), (1, 0)])
 
 
-def extended(own, above, below):
-    gap = jnp.zeros((CHANNELS, ABOVE - BELOW - COLUMNS), own.dtype)
-    return jnp.concatenate([own, below, gap, above], axis=1)
-
-
 def local(latents, out_grad, w_spatial, w_temporal, norm_gain, norm_shift, heights):
     height = heights[0]
     core = lax.axis_index("tile_2")
-    strip = lax.axis_index(TILE)
-    place = jnp.stack([height, strip]).astype(jnp.int32)
-    live = (jnp.arange(CELLS, dtype=jnp.int32) // COLUMNS < height)[None, :]
+    place = jnp.stack([height, lax.axis_index(TILE)]).astype(jnp.int32)
     latent = latents[0]
-    grad = jnp.where(live, out_grad[0], jnp.zeros((), bf16))
-
     group = jnp.arange(CHANNELS, dtype=jnp.int32) // GROUP_SIZE
     group_column = group[:, None]
-
-    near = call(
+    field = (CHANNELS, CELLS)
+
+    near, grad = call(
         start_kernel,
-        shape((16, 16, 256), bf16),
+        (shape((16, 16, 256), bf16), shape(field, bf16)),
         smem=1,
-        inputs=5,
-        scratch=(pltpu.VMEM((16, 256), f32), pltpu.VMEM((16, 256), f32)),
+        inputs=6,
+        apart=(2, 6),
+        scratch=(
+            pltpu.VMEM(field, bf16),
+            pltpu.VMEM(field, bf16),
+            pltpu.VMEM((10, 180), bf16),
+            pltpu.VMEM((10, 60), bf16),
+            pltpu.VMEM((16, 256), f32),
+            pltpu.VMEM((16, 256), f32),
+            pltpu.SemaphoreType.DMA((4,)),
+        ),
         flops=1 << 20,
         moved=1 << 18,
-    )(place, latent, group_column, w_spatial, w_temporal)
+        room=58,
+    )(place, group_column, latent, out_grad[0], w_spatial, w_temporal)
+
+    grad_last = step_by(grad, FRAME, 1)
+    grad_next = step_by(grad, FRAME, -1)
     near = exchange(near, ROW_Z)
-
-    both = jnp.stack([latent, grad])
-    tall = height == 16
-    last = jnp.where(tall, both[:, :, 240:256], both[:, :, 112:128])
-    above = step_by(last, TILE, 1)
-    below = step_by(both[:, :, :COLUMNS], TILE, -1)
-    near, above, below = lax.optimization_barrier((near, above, below))
-    packed = call(pack_kernel, shape((16, 40, PACK), bf16), flops=1 << 27, moved=3 << 19)(
-        near
-    )
+    packed = call(pack_kernel, shape((16, 40, PACK), bf16), flops=1 << 27, moved=3 << 19)(near)
     w_own = exchange(packed, PLANE).reshape(4, 160, PACK)
 
-    latent_ext = extended(latent, above[0], below[0])
-    grad_ext = extended(grad, above[1], below[1])
-    grad_last = step_by(grad_ext, FRAME, 1)
-    grad_next = step_by(grad_ext, FRAME, -1)
-    w_own, grad_last, grad_next = lax.optimization_barrier((w_own, grad_last, grad_next))
+    row_tile = shape((CHANNELS, 128), bf16)
+    row_first, row_last = call(
+        rows_kernel, (row_tile, row_tile), smem=1, inputs=5, flops=1 << 28, moved=1 << 20
+    )(place, latent, grad_next, grad, grad_last)
+    above = step_by(row_last, TILE, 1)
+    below = step_by(row_first, TILE, -1)
+    w_own, above, below = lax.optimization_barrier((w_own, above, below))
     w_other = swap_cores(w_own)
 
     packed_row = jnp.arange(CHANNELS, dtype=jnp.int32)
@@ -449,20 +509,27 @@
         main_kernel,
         (block, block, shape((CHANNELS, CELLS), f32), shape((CHANNELS, 128), f32)),
         smem=1,
-        inputs=12,
+        inputs=14,
+        apart=(8, 12),
+        space=pl.ANY,
         scratch=(
             pltpu.VMEM((4, WIDE, CELLS), bf16),
             pltpu.VMEM((4 * SPAN, CHANNELS), bf16),
             pltpu.VMEM((4 * SPAN_T, CHANNELS), bf16),
             pltpu.VMEM((4, CELLS, 3 * CELLS), bf16),
             pltpu.VMEM((CHANNELS, 3 * CELLS), bf16),
+            pltpu.VMEM(field, bf16),
+            pltpu.VMEM(field, bf16),
+            pltpu.VMEM((CHANNELS, 128), bf16),
+            pltpu.VMEM((CHANNELS, 128), bf16),
+            pltpu.SemaphoreType.DMA((4,)),
         ),
         flops=5 << 30,
         moved=8 << 20,
         room=28,
     )(
         place, gain_row, shift_row, order[:, None], order[None, :], group_column,
-        latent_ext, grad_next, grad_ext, grad_last, w_own, w_other,
+        latent, grad, above, below, grad_next, grad_last, w_own, w_other,
     )
 
     blocks = (16, 40, PACK)
@@ -486,7 +553,7 @@
         flops=1 << 22,
         moved=1 << 20,
     )(
-        place, norm, gain_row, group_column, latent, grad_ext, pre_grad, parts,
+        place, norm, gain_row, group_column, latent, grad, pre_grad, parts,
     )
     return grad_input[None], grad_spatial, grad_temporal, grad_gain, grad_shift
 

time: 142 us -> 147 us (1.035)
  blocking collectives: 51.8 us -> 80.9 us
  starting transfers between devices: 43.4 us -> 28.4 us
  waiting for transfers between devices: 23.7 us -> 14.4 us
  Pallas kernels: 13.4 us -> 18 us
  local copies, waits for them, and re-layouts: 5.7 us -> 1.55 us
    all_to_all x2 -> x3, blocking collectives: 51.8 us -> 80.9 us  [exchange(): return lax.all_to_all(blocks, axes, 0, 0, tiled=True)]
    all_to_all x2 -> x1, starting transfers between devices: 29.2 us -> 7.18 us  [exchange(): return lax.all_to_all(blocks, axes, 0, 0, tiled=True)]
    all_to_all x2 -> x1, waiting for transfers between devices: 12.1 us -> 0.01 us  [exchange(): return lax.all_to_all(blocks, axes, 0, 0, tiled=True)]
    ppermute x2, starting transfers between devices: 3.96 us -> 12.8 us  [swap_cores(): return lax.ppermute(value, 'tile_2', [(0, 1), (1, 0)])]
    unnamed x22 -> x16, local copies, waits for them, and re-layouts: 5.59 us -> 1.54 us
    ppermute x4, waiting for transfers between devices: 6.24 us -> 9.66 us  [step_by(): return lax.ppermute(value, axes, pairs)]
    pallas_call x1 -> x2, Pallas kernels: 1.5 us -> 4.01 us  [the longest x1 2.99 us: local(): call(start_kernel, (shape((16, 16, 256), bf16), shape(field, bf16)), smem...]
    pallas_call x1, Pallas kernels: 6.79 us -> 8.78 us  [local(): call(main_kernel, (block, block, shape((CHANNELS, CELLS), f32), shape((CH...]
  transfers between devices with their start and end apart: 8 -> 7, of which waited for: 7 -> 5; matrix products, arithmetic and copies ran while one was open for 1% -> 0% of each run, Pallas kernels for 0% -> 1%
where the time goes in v5:
time: 147 us; the launch traced here: 146 us
  blocking collectives  80.9 us (55%)
  starting transfers between devices  28.4 us (19%)
  Pallas kernels  18 us (12%)
  waiting for transfers between devices  14.4 us (10%)
  other arithmetic  1.75 us (1%)
  local copies, waits for them, and re-layouts  1.55 us (1%)
    all_to_all x3, blocking collectives, exchange(): return lax.all_to_all(blocks, axes, 0, 0, tiled=True)  80.9 us
    ppermute x2, starting transfers between devices, swap_cores(): return lax.ppermute(value, 'tile_2', [(0, 1), (1, 0)])  12.8 us
    ppermute x4, waiting for transfers between devices, step_by(): return lax.ppermute(value, axes, pairs)  9.66 us
    pallas_call x1, Pallas kernels, local(): call(main_kernel, (block, block, shape((CHANNELS, CELLS), f32), shape((CH...  8.78 us
    ppermute x4, starting transfers between devices, step_by(): return lax.ppermute(value, axes, pairs)  8.43 us
    all_to_all x1, starting transfers between devices, exchange(): return lax.all_to_all(blocks, axes, 0, 0, tiled=True)  7.18 us
    ppermute x2, waiting for transfers between devices, swap_cores(): return lax.ppermute(value, 'tile_2', [(0, 1), (1, 0)])  4.76 us
    pallas_call x1, Pallas kernels, local(): call(start_kernel, (shape((16, 16, 256), bf16), shape(field, bf16)), smem...  2.99 us
  transfers between devices with their start and end apart: 7, of which 5 were waited for; matrix products, arithmetic and copies ran while one was open for 0% of the time, Pallas kernels for 1%

profile of v5, /device:TPU:32, one launch (start us, length us, event | category | flops | bytes accessed | tf_op | source)
XLA Modules:
  0.0 146.4 jit_solution(17764444112784303797)
XLA Ops:
  0.6 0.7 add_select_fusion.group
  2.6 3.0 %shard_map.110 = (bf16[16,16,256]{2,1,0:T(8,128)(2,1)}, bf16[320,256]{1,0:T(8,128)(2,1)}) custom-call(s32[2]{0:T(128)} %pad_add_fusion.place, s32[320,1]{1,0:T(8,128)} %add_select_fusion.group, bf16[320,256]{1,0:T(8,128)(2,1)} %bitcast.11, bf16[320,256]{1,0:T(8,128)(2,1)} %bitcast.15, bf16[10,180]{1,0:T(8,128)(2,1)} %w_spatial_at.1, bf16[10,60]{1,0:T(8,128)(2,1)} %w_temporal_at.1), custom_call_target="tpu_custom_call" | custom-call | flops 1048576 | bytes 262144 | tf_op jit(solution)/shard_map/pallas_call | solution.py:467
  5.6 29.4 %all_to_all.20.blocks = bf16[16,16,256]{2,1,0:T(8,128)(2,1)S(1)} all-to-all(bf16[16,16,256]{2,1,0:T(8,128)(2,1)} %get-tuple-element.22), channel_id=1, replica_groups=mesh['frame_0'=4,'frame_1'=4,'tile_0'=4,'tile_1'=4,'tile_2'=2] {'tile_1'..., dimensions={0} | all-to-all | bytes 262144 | tf_op jit(solution)/shard_map/all_to_all | solution.py:54
  35.0 1.7 %shard_map.111 = bf16[16,40,1024]{2,1,0:T(8,128)(2,1)} custom-call(bf16[16,16,256]{2,1,0:T(8,128)(2,1)S(1)} %all_to_all.20.blocks), custom_call_target="tpu_custom_call" | custom-call | flops 134217728 | bytes 1572864 | tf_op jit(solution)/shard_map/pallas_call | solution.py:490
  36.7 7.2 %all-to-all-start.1 = ((bf16[16,40,1024]{2,1,0:T(8,128)(2,1)}), bf16[16,40,1024]{2,1,0:T(8,128)(2,1)S(1)}, u32[]{:S(2)}, u32[]{:S(2)}) async-start(bf16[16,40,1024]{2,1,0:T(8,128)(2,1)} %shard_map.111), calls=%async_computation.1 | async-start | bytes 2621440 | tf_op jit(solution)/shard_map/all_to_all | solution.py:54
  43.9 2.6 %collective-permute-start.1 = (bf16[320,256]{1,0:T(8,128)(2,1)S(1)}, bf16[320,256]{1,0:T(8,128)(2,1)S(1)}, u32[]{:S(2)}, u32[]{:S(2)}) collective-permute-start(bf16[320,256]{1,0:T(8,128)(2,1)S(1)} %copy-done.2), channel_id=1, source_target_pairs={{0,32},{32,64},{64,96},{96,128},{128,160},{160,192},{192,224},{224... | collective-permute-start | bytes 491528 | tf_op jit(solution)/shard_map/ppermute | solution.py:451
  46.5 3.2 %collective-permute-start = (bf16[320,256]{1,0:T(8,128)(2,1)S(1)}, bf16[320,256]{1,0:T(8,128)(2,1)S(1)}, u32[]{:S(2)}, u32[]{:S(2)}) collective-permute-start(bf16[320,256]{1,0:T(8,128)(2,1)S(1)} %copy-done.2), channel_id=1, source_target_pairs={{32,0},{64,32},{96,64},{128,96},{160,128},{192,160},{224,192},{256... | collective-permute-start | bytes 491528 | tf_op jit(solution)/shard_map/ppermute | solution.py:451
  49.8 1.3 collective-permute-done.1.g_last.g_last_at
  51.1 4.1 %collective-permute-done.g_next.g_next_at = bf16[320,256]{1,0:T(8,128)(2,1)S(1)} collective-permute-done((bf16[320,256]{1,0:T(8,128)(2,1)S(1)}, bf16[320,256]{1,0:T(8,128)(2,1)S(1)}, u32[]{:S(2)}, u32[]{:S(2)}) %collective-permute-start) | collective-permute-done | bytes 163872 | tf_op jit(solution)/shard_map/ppermute | solution.py:451
  55.2 1.0 shard_map.112
  56.3 1.3 collective-permute-start.2
  57.6 1.3 collective-permute-start.3
  58.9 4.2 %collective-permute-done.3.below_at = bf16[320,128]{1,0:T(8,128)(2,1)S(1)} collective-permute-done((bf16[320,128]{1,0:T(8,128)(2,1)S(1)}, bf16[320,128]{1,0:T(8,128)(2,1)S(1)}, u32[]{:S(2)}, u32[]{:S(2)}) %collective-permute-start.3) | collective-permute-done | bytes 81952 | tf_op jit(solution)/shard_map/ppermute | solution.py:451
  63.7 10.5 %collective-permute-start.4 = (bf16[4,160,1024]{2,1,0:T(8,128)(2,1)S(1)}, bf16[4,160,1024]{2,1,0:T(8,128)(2,1)S(1)}, u32[]{:S(2)}, u32[]{:S(2)}) collective-permute-start(bf16[4,160,1024]{2,1,0:T(8,128)(2,1)S(1)} %bitcast.7), channel_id=1, source_target_pairs={{0,1},{1,0},{2,3},{3,2},{4,5},{5,4},{6,7},{7,6},{8,9},{9,8},{10,11... | collective-permute-start | bytes 3932168 | tf_op jit(solution)/shard_map/ppermute | solution.py:455
  74.8 2.1 %collective-permute-done.4.w_other = bf16[4,160,1024]{2,1,0:T(8,128)(2,1)S(1)} collective-permute-done((bf16[4,160,1024]{2,1,0:T(8,128)(2,1)S(1)}, bf16[4,160,1024]{2,1,0:T(8,128)(2,1)S(1)}, u32[]{:S(2)}, u32[]{:S(2)}) %collective-permute-start.4) | collective-permute-done | bytes 1310752 | tf_op jit(solution)/shard_map/ppermute | solution.py:455
  76.9 0.9 copy-done.5
  77.8 8.8 %shard_map.113 = (bf16[4,160,1024]{2,1,0:T(8,128)(2,1)S(1)}, bf16[4,160,1024]{2,1,0:T(8,128)(2,1)S(1)}, f32[320,256]{1,0:T(8,128)S(1)}, f32[320,128]{1,0:T(8,128)S(1)}) custom-call(s32[2]{0:T(128)S(1)} %copy-done.3, f32[1,320]{1,0:T(1,128)S(1)} %broadcast_in_dim.24.gain, f32[1,320]{1,0:T(1,128)S(1)} %broadcast_in_dim.25.shift, s32[320,1]{1,0:T(8,128)S(1)} %fusion.3.order, ...), custom_call_target="tpu_custom_call" | custom-call | flops 5368709120 | bytes 8388608 | tf_op jit(solution)/shard_map/pallas_call | solution.py:508
  86.6 2.3 %collective-permute-start.5 = (bf16[4,160,1024]{2,1,0:T(8,128)(2,1)S(1)}, bf16[4,160,1024]{2,1,0:T(8,128)(2,1)S(1)}, u32[]{:S(2)}, u32[]{:S(2)}) collective-permute-start(bf16[4,160,1024]{2,1,0:T(8,128)(2,1)S(1)} %get-tuple-element.31), channel_id=1, source_target_pairs={{0,1},{1,0},{2,3},{3,2},{4,5},{5,4},{6,7},{7,6},{8,9},{9,8},{10,11... | collective-permute-start | bytes 3932168 | tf_op jit(solution)/shard_map/ppermute | solution.py:455
  88.9 2.6 %collective-permute-done.5 = bf16[4,160,1024]{2,1,0:T(8,128)(2,1)S(1)} collective-permute-done((bf16[4,160,1024]{2,1,0:T(8,128)(2,1)S(1)}, bf16[4,160,1024]{2,1,0:T(8,128)(2,1)S(1)}, u32[]{:S(2)}, u32[]{:S(2)}) %collective-permute-start.5) | collective-permute-done | bytes 1310752 | tf_op jit(solution)/shard_map/ppermute | solution.py:455
  91.5 0.9 shard_map.114
  92.4 26.1 %all_to_all.21.terms = bf16[16,40,1024]{2,1,0:T(8,128)(2,1)S(1)} all-to-all(bf16[16,40,1024]{2,1,0:T(8,128)(2,1)S(1)} %shard_map.114), channel_id=1, replica_groups=mesh['frame_0'=4,'frame_1'=4,'tile_0'=4,'tile_1'=4,'tile_2'=2] {'frame_0..., dimensions={0} | all-to-all | bytes 2621440 | tf_op jit(solution)/shard_map/all_to_all | solution.py:54
  118.5 0.7 shard_map.115
  119.2 25.3 %all_to_all.22.terms = bf16[16,16,256]{2,1,0:T(8,128)(2,1)S(1)} all-to-all(bf16[16,16,256]{2,1,0:T(8,128)(2,1)S(1)} %shard_map.115), channel_id=1, replica_groups=mesh['frame_0'=4,'frame_1'=4,'tile_0'=4,'tile_1'=4,'tile_2'=2] {'tile_1'..., dimensions={0} | all-to-all | bytes 262144 | tf_op jit(solution)/shard_map/all_to_all | solution.py:54
  144.5 1.9 %shard_map.116 = (bf16[320,256]{1,0:T(8,128)(2,1)}, f32[10,180]{1,0:T(8,128)}, f32[10,60]{1,0:T(8,128)}, f32[320]{0:T(512)}, f32[320]{0:T(512)}) custom-call(s32[2]{0:T(128)S(1)} %copy-done.3, f32[320,128]{1,0:T(8,128)S(1)} %get-tuple-element.28.norm, f32[1,320]{1,0:T(1,128)S(1)} %broadcast_in_dim.24.gain, s32[320,1]{1,0:T(8,128)S(1)} %copy-done, ...), custom_call_target="tpu_custom_call" | custom-call | flops 4194304 | bytes 1048576 | tf_op jit(solution)/shard_map/pallas_call | solution.py:542
  (22 shorter events, 1.7 us)
Async XLA Ops:
  36.7 7.2 %copy-start.2 = (bf16[320,256]{1,0:T(8,128)(2,1)S(1)}, bf16[320,256]{1,0:T(8,128)(2,1)}, u32[]{:S(2)}) copy-start(bf16[320,256]{1,0:T(8,128)(2,1)} %get-tuple-element.21.g_here) | copy-start | bytes 491524
  36.7 18.6 %copy-start.1 = (bf16[1,320,256]{2,1,0:T(8,128)(2,1)S(1)}, bf16[1,320,256]{2,1,0:T(8,128)(2,1)}, u32[]{:S(2)}) copy-start(bf16[1,320,256]{2,1,0:T(8,128)(2,1)} %param.7) | copy-start | bytes 491524
  36.7 18.6 %copy-start.3 = (s32[2]{0:T(128)S(1)}, s32[2]{0:T(128)}, u32[]{:S(2)}) copy-start(s32[2]{0:T(128)} %pad_add_fusion.place) | copy-start | bytes 28
  36.7 37.6 %copy-start.6 = (f32[320]{0:T(512)S(1)}, f32[320]{0:T(512)}, u32[]{:S(2)}) copy-start(f32[320]{0:T(512)} %param.11) | copy-start | bytes 3844
  36.7 37.6 %copy-start.7 = (f32[320]{0:T(512)S(1)}, f32[320]{0:T(512)}, u32[]{:S(2)}) copy-start(f32[320]{0:T(512)} %param.12) | copy-start | bytes 3844
  36.7 40.2 %copy-start = (s32[320,1]{1,0:T(8,128)S(1)}, s32[320,1]{1,0:T(8,128)}, u32[]{:S(2)}) copy-start(s32[320,1]{1,0:T(8,128)} %add_select_fusion.group) | copy-start | bytes 3844
  36.7 27.0 %all-to-all-start.1 = ((bf16[16,40,1024]{2,1,0:T(8,128)(2,1)}), bf16[16,40,1024]{2,1,0:T(8,128)(2,1)S(1)}, u32[]{:S(2)}, u32[]{:S(2)}) async-start(bf16[16,40,1024]{2,1,0:T(8,128)(2,1)} %shard_map.111), calls=%async_computation.1 | async-start | bytes 2621440 | tf_op jit(solution)/shard_map/all_to_all | solution.py:54
  43.9 7.2 %collective-permute-start.1 = (bf16[320,256]{1,0:T(8,128)(2,1)S(1)}, bf16[320,256]{1,0:T(8,128)(2,1)S(1)}, u32[]{:S(2)}, u32[]{:S(2)}) collective-permute-start(bf16[320,256]{1,0:T(8,128)(2,1)S(1)} %copy-done.2), channel_id=1, source_target_pairs={{0,32},{32,64},{64,96},{96,128},{128,160},{160,192},{192,224},{224... | collective-permute-start | bytes 491528 | tf_op jit(solution)/shard_map/ppermute | solution.py:451
  46.5 8.7 %collective-permute-start = (bf16[320,256]{1,0:T(8,128)(2,1)S(1)}, bf16[320,256]{1,0:T(8,128)(2,1)S(1)}, u32[]{:S(2)}, u32[]{:S(2)}) collective-permute-start(bf16[320,256]{1,0:T(8,128)(2,1)S(1)} %copy-done.2), channel_id=1, source_target_pairs={{32,0},{64,32},{96,64},{128,96},{160,128},{192,160},{224,192},{256... | collective-permute-start | bytes 491528 | tf_op jit(solution)/shard_map/ppermute | solution.py:451
  56.3 2.6 %collective-permute-start.2 = (bf16[320,128]{1,0:T(8,128)(2,1)S(1)}, bf16[320,128]{1,0:T(8,128)(2,1)S(1)}, u32[]{:S(2)}, u32[]{:S(2)}) collective-permute-start(bf16[320,128]{1,0:T(8,128)(2,1)S(1)} %get-tuple-element.23), channel_id=1, source_target_pairs={{0,1},{1,2},{2,3},{3,4},{4,5},{5,6},{6,7},{7,8},{8,9},{9,10},{10,1... | collective-permute-start | bytes 245768 | tf_op jit(solution)/shard_map/ppermute | solution.py:451
  57.6 5.5 %collective-permute-start.3 = (bf16[320,128]{1,0:T(8,128)(2,1)S(1)}, bf16[320,128]{1,0:T(8,128)(2,1)S(1)}, u32[]{:S(2)}, u32[]{:S(2)}) collective-permute-start(bf16[320,128]{1,0:T(8,128)(2,1)S(1)} %get-tuple-element.24), channel_id=1, source_target_pairs={{1,0},{2,1},{3,2},{4,3},{5,4},{6,5},{7,6},{8,7},{9,8},{10,9},{11,1... | collective-permute-start | bytes 245768 | tf_op jit(solution)/shard_map/ppermute | solution.py:451
  63.1 0.6 copy-start.4
  63.7 13.2 %collective-permute-start.4 = (bf16[4,160,1024]{2,1,0:T(8,128)(2,1)S(1)}, bf16[4,160,1024]{2,1,0:T(8,128)(2,1)S(1)}, u32[]{:S(2)}, u32[]{:S(2)}) collective-permute-start(bf16[4,160,1024]{2,1,0:T(8,128)(2,1)S(1)} %bitcast.7), channel_id=1, source_target_pairs={{0,1},{1,0},{2,3},{3,2},{4,5},{5,4},{6,7},{7,6},{8,9},{9,8},{10,11... | collective-permute-start | bytes 3932168 | tf_op jit(solution)/shard_map/ppermute | solution.py:455
  76.9 0.9 copy-start.5
  86.6 4.9 %collective-permute-start.5 = (bf16[4,160,1024]{2,1,0:T(8,128)(2,1)S(1)}, bf16[4,160,1024]{2,1,0:T(8,128)(2,1)S(1)}, u32[]{:S(2)}, u32[]{:S(2)}) collective-permute-start(bf16[4,160,1024]{2,1,0:T(8,128)(2,1)S(1)} %get-tuple-element.31), channel_id=1, source_target_pairs={{0,1},{1,0},{2,3},{3,2},{4,5},{5,4},{6,7},{7,6},{8,9},{9,8},{10,11... | collective-permute-start | bytes 3932168 | tf_op jit(solution)/shard_map/ppermute | solution.py:455

commit v6 on v5

--- a/solution.py
+++ b/solution.py
@@ -38,6 +38,10 @@
     return lax.broadcasted_iota(jnp.int32, shape, dim)
 
 
+def group_of(dims, dim):
+    return (iota(dims, dim) * 6554) >> 16
+
+
 def dot(a, b):
     return jnp.dot(a, b, preferred_element_type=f32)
 
@@ -95,7 +99,7 @@
 
 
 def start_kernel(
-    place, group, latent_at, grad_at, w_spatial_at, w_temporal_at, out, masked,
+    place, latent_at, grad_at, w_spatial_at, w_temporal_at, out, masked,
     latent, grad, w_spatial, w_temporal, left, right, sems,
 ):
     fetched(
@@ -114,8 +118,9 @@
     chan_sum = jnp.sum(value, axis=1, keepdims=True)
     chan_square = jnp.sum(value * value, axis=1, keepdims=True)
     lane = iota((CHANNELS, 128), 1)
-    terms = jnp.where(lane == group[...], chan_sum, 0.0)
-    terms += jnp.where(lane == group[...] + GROUPS, chan_square, 0.0)
+    group = group_of((CHANNELS, 128), 0)
+    terms = jnp.where(lane == group, chan_sum, 0.0)
+    terms += jnp.where(lane == group + GROUPS, chan_square, 0.0)
     cells = (height * COLUMNS).astype(f32)
     stats = jnp.sum(terms, axis=0, keepdims=True)
     stats += jnp.where(iota((1, 128), 1) == 2 * GROUPS, cells, 0.0)
@@ -176,7 +181,7 @@
         out[n] = packed
 
 
-def stat_columns(w_own, w_other, group):
+def stat_columns(w_own, w_other):
     halves = []
     for ref in (w_own, w_other):
         half = jnp.zeros((40, 128), f32)
@@ -195,6 +200,7 @@
     def pick(q):
         across = jnp.sum(jnp.where(line == lane, quantity(q), 0.0), axis=0, keepdims=True)
         wide = iota((CHANNELS, 128), 1)
+        group = group_of((CHANNELS, 128), 0)
         return jnp.sum(jnp.where(wide == group, across, 0.0), axis=1, keepdims=True)
 
     positions = quantity(2)[:1]
@@ -267,21 +273,11 @@
         start = end
 
 
-def main_kernel(
-    place, gain, shift, order, order_row, group, latent_own, g_here,
-    above_at, below_at, g_next_at, g_last_at, w_own, w_other, grad_own, grad_other, pre_grad, norm, cols, turned_s, turned_t, frames, taps,
-    g_next, g_last, above, below, sems,
+def ready_kernel(
+    place, order, latent, g_here, above, below, g_next, g_last, latent_ext, packed, moves
 ):
-    copies = (
-        pltpu.make_async_copy(g_next_at, g_next, sems.at[0]),
-        pltpu.make_async_copy(g_last_at, g_last, sems.at[1]),
-        pltpu.make_async_copy(above_at, above, sems.at[2]),
-        pltpu.make_async_copy(below_at, below, sems.at[3]),
-    )
-    for copy in copies:
-        copy.start()
     height = place[0]
-    strip = place[1]
+    to_packed = zero_one(order[...] == iota((CHANNELS, CHANNELS), 1))
 
     def extended(own, set_index):
         source = iota((128, 128), 0)
@@ -292,6 +288,26 @@
         rows = dot(below[...], zero_one(low)) + dot(above[...], zero_one(high))
         return jnp.concatenate([own, rows.astype(bf16)], axis=1)
 
+    latent_ext[...] = extended(latent[...], 0)
+    for k, ref in enumerate((g_next, g_here, g_last)):
+        packed[k] = dot(to_packed, extended(ref[...], 1 + k)).astype(bf16)
+    cell = iota((1, CELLS), 1)
+    source = iota((EXT, CELLS), 0)
+    for k in range(9):
+        row = (cell >> 4) + (k // 3 - 1)
+        column = (cell & 15) + (k % 3 - 1)
+        base = jnp.where(row < 0, ABOVE, jnp.where(row == height, BELOW, row * COLUMNS))
+        wanted = jnp.where((column >= 0) & (column < COLUMNS), base + column, -1)
+        moves[k] = zero_one(source == wanted)
+
+
+def main_kernel(
+    place, gain, shift, order, order_row, latent, packed, moves, w_own, w_other,
+    grad_own, grad_other, pre_grad, norm, cols, turned_s, turned_t, frames, taps,
+):
+    height = place[0]
+    strip = place[1]
+
     lane = iota((1, EXT), 1)
     live = ((lane < CELLS) & ((lane >> 4) < height)) | (
         (lane >= BELOW) & (lane < BELOW + COLUMNS) & (strip < STRIPS - 1)
@@ -305,37 +321,28 @@
         turned_s[y * SPAN : (y + 1) * SPAN, :] = across[:SPAN]
         turned_t[y * SPAN_T : (y + 1) * SPAN_T, :] = across[WIDE : WIDE + SPAN_T]
 
-    for copy in copies:
-        copy.wait()
-    positions, mean, rstd = stat_columns(w_own, w_other, group[...])
+    positions, mean, rstd = stat_columns(w_own, w_other)
     lane_n = iota((CHANNELS, 128), 1)
     norm[...] = jnp.where(lane_n == 0, mean, jnp.where(lane_n == 1, rstd, positions))
     gain_column = turned(gain[...])
     shift_column = turned(shift[...])
-    normed = (extended(latent_own[...], 0).astype(f32) - mean) * rstd
+    normed = (latent[...].astype(f32) - mean) * rstd
     pre_act = gain_column * normed + shift_column
     sigmoid = 1.0 / (1.0 + jnp.exp(-pre_act))
     active = jnp.where(live, pre_act * sigmoid, 0.0).astype(bf16)
 
     grad_spat = jnp.zeros((CHANNELS, EXT), f32)
-    for k, ref in enumerate((g_next, g_here, g_last)):
-        packed = dot(to_packed, extended(ref[...], 1 + k)).astype(bf16)
-        taps[:, k * CELLS : (k + 1) * CELLS] = packed[:, :CELLS]
-        grad_spat += dot(turned_t[k * CHANNELS : (k + 1) * CHANNELS, :], packed)
+    for k in range(3):
+        taps[:, k * CELLS : (k + 1) * CELLS] = packed[k, :, :CELLS]
+        grad_spat += dot(turned_t[k * CHANNELS : (k + 1) * CHANNELS, :], packed[k])
     grad_spat = jnp.where(live, grad_spat, 0.0).astype(bf16)
     spat_packed = dot(to_packed, grad_spat).astype(bf16)
 
     for y in range(4):
         cols[y, SPAN:, :] = jnp.zeros((WIDE - SPAN, CELLS), bf16)
-    cell = iota((1, CELLS), 1)
-    source = iota((EXT, CELLS), 0)
     grad_act = jnp.zeros((CHANNELS, CELLS), f32)
     for k in range(9):
-        row = (cell >> 4) + (k // 3 - 1)
-        column = (cell & 15) + (k % 3 - 1)
-        base = jnp.where(row < 0, ABOVE, jnp.where(row == height, BELOW, row * COLUMNS))
-        wanted = jnp.where((column >= 0) & (column < COLUMNS), base + column, -1)
-        move = zero_one(source == wanted)
+        move = moves[k]
         moved = dot(active, move).astype(bf16)
         for y, at, start, size in pieces_of(k * CHANNELS, (k + 1) * CHANNELS, SPAN):
             first = start - k * CHANNELS
@@ -383,7 +390,7 @@
 
 
 def end_kernel(
-    place, norm, gain, group, latent, g_here, pre_grad, terms,
+    place, norm, gain, latent, g_here, pre_grad, terms,
     result, grad_s, grad_t, grad_gain, grad_shift,
 ):
     height = place[0]
@@ -403,8 +410,8 @@
     channel = iota((CHANNELS, 128), 0)
     spot = ((channel >> 3) & 7) * 16 + (channel & 7)
     lane = iota((CHANNELS, 128), 1)
-    eye = iota((CHANNELS, CHANNELS), 0) == iota((CHANNELS, CHANNELS), 1)
-    same = group[...] == jnp.sum(jnp.where(eye, group[...], 0), axis=0, keepdims=True)
+    square = (CHANNELS, CHANNELS)
+    same = group_of(square, 0) == group_of(square, 1)
 
     def chan_row(offset):
         column = jnp.sum(jnp.where(lane == spot + offset, wide, 0.0), axis=1, keepdims=True)
@@ -460,16 +467,14 @@
     core = lax.axis_index("tile_2")
     place = jnp.stack([height, lax.axis_index(TILE)]).astype(jnp.int32)
     latent = latents[0]
-    group = jnp.arange(CHANNELS, dtype=jnp.int32) // GROUP_SIZE
-    group_column = group[:, None]
     field = (CHANNELS, CELLS)
 
     near, grad = call(
         start_kernel,
         (shape((16, 16, 256), bf16), shape(field, bf16)),
         smem=1,
-        inputs=6,
-        apart=(2, 6),
+        inputs=5,
+        apart=(1, 5),
         scratch=(
             pltpu.VMEM(field, bf16),
             pltpu.VMEM(field, bf16),
@@ -482,7 +487,7 @@
         flops=1 << 20,
         moved=1 << 18,
         room=58,
-    )(place, group_column, latent, out_grad[0], w_spatial, w_temporal)
+    )(heights, latent, out_grad[0], w_spatial, w_temporal)
 
     grad_last = step_by(grad, FRAME, 1)
     grad_next = step_by(grad, FRAME, -1)
@@ -504,32 +509,37 @@
     order = rest // 40 * 80 + rest % 40 // 10 * 20 + rest % 10
     order = order + jnp.where(half == 0, core, 1 - core) * 10
     gain_row, shift_row = norm_gain[None], norm_shift[None]
+    latent_ext, packed_grad, moves = call(
+        ready_kernel,
+        (
+            shape((CHANNELS, EXT), bf16),
+            shape((3, CHANNELS, EXT), bf16),
+            shape((9, EXT, CELLS), bf16),
+        ),
+        smem=1,
+        inputs=8,
+        flops=1 << 29,
+        moved=1 << 21,
+    )(place, order[:, None], latent, grad, above, below, grad_next, grad_last)
     block = shape((4, 160, PACK), bf16)
     grad_own, grad_other, pre_grad, norm = call(
         main_kernel,
         (block, block, shape((CHANNELS, CELLS), f32), shape((CHANNELS, 128), f32)),
         smem=1,
-        inputs=14,
-        apart=(8, 12),
-        space=pl.ANY,
+        inputs=10,
         scratch=(
             pltpu.VMEM((4, WIDE, CELLS), bf16),
             pltpu.VMEM((4 * SPAN, CHANNELS), bf16),
             pltpu.VMEM((4 * SPAN_T, CHANNELS), bf16),
             pltpu.VMEM((4, CELLS, 3 * CELLS), bf16),
             pltpu.VMEM((CHANNELS, 3 * CELLS), bf16),
-            pltpu.VMEM(field, bf16),
-            pltpu.VMEM(field, bf16),
-            pltpu.VMEM((CHANNELS, 128), bf16),
-            pltpu.VMEM((CHANNELS, 128), bf16),
-            pltpu.SemaphoreType.DMA((4,)),
         ),
         flops=5 << 30,
         moved=8 << 20,
         room=28,
     )(
-        place, gain_row, shift_row, order[:, None], order[None, :], group_column,
-        latent, grad, above, below, grad_next, grad_last, w_own, w_other,
+        place, gain_row, shift_row, order[:, None], order[None, :], latent_ext,
+        packed_grad, moves, w_own, w_other,
     )
 
     blocks = (16, 40, PACK)
@@ -549,11 +559,11 @@
             shape((CHANNELS,), f32),
         ),
         smem=1,
-        inputs=8,
+        inputs=7,
         flops=1 << 22,
         moved=1 << 20,
     )(
-        place, norm, gain_row, group_column, latent, grad, pre_grad, parts,
+        place, norm, gain_row, latent, grad, pre_grad, parts,
     )
     return grad_input[None], grad_spatial, grad_temporal, grad_gain, grad_shift
 

time: 147 us -> 141 us (0.959)
  waiting for transfers between devices: 14.4 us -> 12.2 us
  local copies, waits for them, and re-layouts: 1.55 us -> 0.02 us
  Pallas kernels: 18 us -> 16.5 us
    pallas_call x1, Pallas kernels: 8.78 us -> 6.35 us  [local(): call(main_kernel, (block, block, shape((CHANNELS, CELLS), f32), shape((CH...]
    ppermute x2, waiting for transfers between devices: 4.76 us -> 2.65 us  [swap_cores(): return lax.ppermute(value, 'tile_2', [(0, 1), (1, 0)])]
    pallas_call x0 -> x1, Pallas kernels: none -> 2.1 us  [local(): call(ready_kernel, (shape((CHANNELS, EXT), bf16), shape((3, CHANNELS, EXT...]
    unnamed x16 -> x8, local copies, waits for them, and re-layouts: 1.54 us -> 0.01 us
  transfers between devices with their start and end apart: 7 -> 7, of which waited for: 5 -> 4; matrix products, arithmetic and copies ran while one was open for 0% -> 0% of each run, Pallas kernels for 1% -> 2%
where the time goes in v6:
time: 141 us; the launch traced here: 140 us
  blocking collectives  80.9 us (57%)
  starting transfers between devices  28.4 us (20%)
  Pallas kernels  16.5 us (12%)
  waiting for transfers between devices  12.2 us (9%)
  between operations  1.44 us (1%)
    all_to_all x3, blocking collectives, exchange(): return lax.all_to_all(blocks, axes, 0, 0, tiled=True)  80.9 us
    ppermute x2, starting transfers between devices, swap_cores(): return lax.ppermute(value, 'tile_2', [(0, 1), (1, 0)])  12.8 us
    ppermute x4, waiting for transfers between devices, step_by(): return lax.ppermute(value, axes, pairs)  9.58 us
    ppermute x4, starting transfers between devices, step_by(): return lax.ppermute(value, axes, pairs)  8.43 us
    all_to_all x1, starting transfers between devices, exchange(): return lax.all_to_all(blocks, axes, 0, 0, tiled=True)  7.18 us
    pallas_call x1, Pallas kernels, local(): call(main_kernel, (block, block, shape((CHANNELS, CELLS), f32), shape((CH...  6.35 us
  transfers between devices with their start and end apart: 7, of which 4 were waited for; matrix products, arithmetic and copies ran while one was open for 0% of the time, Pallas kernels for 2%

profile of v6, /device:TPU:32, one launch (start us, length us, event | category | flops | bytes accessed | tf_op | source)
XLA Modules:
  0.0 140.1 jit_solution(18067120799996532482)
XLA Ops:
  1.3 1.9 %shard_map.110 = (bf16[16,16,256]{2,1,0:T(8,128)(2,1)}, bf16[320,256]{1,0:T(8,128)(2,1)}) custom-call(s32[1]{0:T(128)S(6)} %copy.12.place, bf16[320,256]{1,0:T(8,128)(2,1)} %bitcast.11, bf16[320,256]{1,0:T(8,128)(2,1)} %bitcast.15, bf16[10,180]{1,0:T(8,128)(2,1)} %w_spatial_at.1, bf16[10,60]{1,0:T(8,128)(2,1)} %w_temporal_at.1), custom_call_target="tpu_custom_call" | custom-call | flops 1048576 | bytes 262144 | tf_op jit(solution)/shard_map/pallas_call | solution.py:472
  3.2 29.4 %all_to_all.20.blocks = bf16[16,16,256]{2,1,0:T(8,128)(2,1)S(1)} all-to-all(bf16[16,16,256]{2,1,0:T(8,128)(2,1)} %get-tuple-element.25), channel_id=1, replica_groups=mesh['frame_0'=4,'frame_1'=4,'tile_0'=4,'tile_1'=4,'tile_2'=2] {'tile_1'..., dimensions={0} | all-to-all | bytes 262144 | tf_op jit(solution)/shard_map/all_to_all | solution.py:58
  32.6 1.6 %shard_map.111 = bf16[16,40,1024]{2,1,0:T(8,128)(2,1)} custom-call(bf16[16,16,256]{2,1,0:T(8,128)(2,1)S(1)} %all_to_all.20.blocks), custom_call_target="tpu_custom_call" | custom-call | flops 134217728 | bytes 1572864 | tf_op jit(solution)/shard_map/pallas_call | solution.py:495
  34.3 7.2 %all-to-all-start.1 = ((bf16[16,40,1024]{2,1,0:T(8,128)(2,1)}), bf16[16,40,1024]{2,1,0:T(8,128)(2,1)S(1)}, u32[]{:S(2)}, u32[]{:S(2)}) async-start(bf16[16,40,1024]{2,1,0:T(8,128)(2,1)} %shard_map.111), calls=%async_computation.1 | async-start | bytes 2621440 | tf_op jit(solution)/shard_map/all_to_all | solution.py:58
  41.5 2.6 %collective-permute-start.1 = (bf16[320,256]{1,0:T(8,128)(2,1)S(1)}, bf16[320,256]{1,0:T(8,128)(2,1)S(1)}, u32[]{:S(2)}, u32[]{:S(2)}) collective-permute-start(bf16[320,256]{1,0:T(8,128)(2,1)S(1)} %copy-done.1), channel_id=1, source_target_pairs={{0,32},{32,64},{64,96},{96,128},{128,160},{160,192},{192,224},{224... | collective-permute-start | bytes 491528 | tf_op jit(solution)/shard_map/ppermute | solution.py:458
  44.1 3.2 %collective-permute-start = (bf16[320,256]{1,0:T(8,128)(2,1)S(1)}, bf16[320,256]{1,0:T(8,128)(2,1)S(1)}, u32[]{:S(2)}, u32[]{:S(2)}) collective-permute-start(bf16[320,256]{1,0:T(8,128)(2,1)S(1)} %copy-done.1), channel_id=1, source_target_pairs={{32,0},{64,32},{96,64},{128,96},{160,128},{192,160},{224,192},{256... | collective-permute-start | bytes 491528 | tf_op jit(solution)/shard_map/ppermute | solution.py:458
  47.4 0.1 pad_add_fusion.place
  47.4 1.3 collective-permute-done.1.g_last
  48.7 4.1 %collective-permute-done.g_next = bf16[320,256]{1,0:T(8,128)(2,1)S(1)} collective-permute-done((bf16[320,256]{1,0:T(8,128)(2,1)S(1)}, bf16[320,256]{1,0:T(8,128)(2,1)S(1)}, u32[]{:S(2)}, u32[]{:S(2)}) %collective-permute-start) | collective-permute-done | bytes 163872 | tf_op jit(solution)/shard_map/ppermute | solution.py:458
  52.8 1.0 shard_map.112
  53.8 1.3 collective-permute-start.2
  55.1 1.3 collective-permute-start.3
  56.5 4.2 %collective-permute-done.3.below = bf16[320,128]{1,0:T(8,128)(2,1)S(1)} collective-permute-done((bf16[320,128]{1,0:T(8,128)(2,1)S(1)}, bf16[320,128]{1,0:T(8,128)(2,1)S(1)}, u32[]{:S(2)}, u32[]{:S(2)}) %collective-permute-start.3) | collective-permute-done | bytes 81952 | tf_op jit(solution)/shard_map/ppermute | solution.py:458
  60.7 10.5 %collective-permute-start.4 = (bf16[4,160,1024]{2,1,0:T(8,128)(2,1)S(1)}, bf16[4,160,1024]{2,1,0:T(8,128)(2,1)S(1)}, u32[]{:S(2)}, u32[]{:S(2)}) collective-permute-start(bf16[4,160,1024]{2,1,0:T(8,128)(2,1)S(1)} %bitcast.7), channel_id=1, source_target_pairs={{0,1},{1,0},{2,3},{3,2},{4,5},{5,4},{6,7},{7,6},{8,9},{9,8},{10,11... | collective-permute-start | bytes 3932168 | tf_op jit(solution)/shard_map/ppermute | solution.py:462
  71.3 0.4 fusion.3.order
  71.7 2.1 %shard_map.113 = (bf16[320,384]{1,0:T(8,128)(2,1)S(1)}, bf16[3,320,384]{2,1,0:T(8,128)(2,1)S(1)}, bf16[9,384,256]{2,1,0:T(8,128)(2,1)S(1)}) custom-call(s32[2]{0:T(128)S(1)} %pad_add_fusion.place, s32[320,1]{1,0:T(8,128)S(1)} %fusion.3.order, bf16[320,256]{1,0:T(8,128)(2,1)S(1)} %bitcast.13, bf16[320,256]{1,0:T(8,128)(2,1)S(1)} %copy-done.1, ...), custom_call_target="tpu_custom_call" | custom-call | flops 536870912 | bytes 2097152 | tf_op jit(solution)/shard_map/pallas_call | solution.py:512
  73.8 6.4 %shard_map.114 = (bf16[4,160,1024]{2,1,0:T(8,128)(2,1)S(1)}, bf16[4,160,1024]{2,1,0:T(8,128)(2,1)S(1)}, f32[320,256]{1,0:T(8,128)S(1)}, f32[320,128]{1,0:T(8,128)S(1)}) custom-call(s32[2]{0:T(128)S(1)} %pad_add_fusion.place, f32[1,320]{1,0:T(1,128)S(1)} %broadcast_in_dim.24.gain, f32[1,320]{1,0:T(1,128)S(1)} %broadcast_in_dim.25.shift, ...), custom_call_target="tpu_custom_call" | custom-call | flops 5368709120 | bytes 8388608 | tf_op jit(solution)/shard_map/pallas_call | solution.py:525
  80.2 2.3 %collective-permute-start.5 = (bf16[4,160,1024]{2,1,0:T(8,128)(2,1)S(1)}, bf16[4,160,1024]{2,1,0:T(8,128)(2,1)S(1)}, u32[]{:S(2)}, u32[]{:S(2)}) collective-permute-start(bf16[4,160,1024]{2,1,0:T(8,128)(2,1)S(1)} %get-tuple-element.37), channel_id=1, source_target_pairs={{0,1},{1,0},{2,3},{3,2},{4,5},{5,4},{6,7},{7,6},{8,9},{9,8},{10,11... | collective-permute-start | bytes 3932168 | tf_op jit(solution)/shard_map/ppermute | solution.py:462
  82.5 2.6 %collective-permute-done.5 = bf16[4,160,1024]{2,1,0:T(8,128)(2,1)S(1)} collective-permute-done((bf16[4,160,1024]{2,1,0:T(8,128)(2,1)S(1)}, bf16[4,160,1024]{2,1,0:T(8,128)(2,1)S(1)}, u32[]{:S(2)}, u32[]{:S(2)}) %collective-permute-start.5) | collective-permute-done | bytes 1310752 | tf_op jit(solution)/shard_map/ppermute | solution.py:462
  85.1 0.9 shard_map.115
  86.0 26.1 %all_to_all.21.terms = bf16[16,40,1024]{2,1,0:T(8,128)(2,1)S(1)} all-to-all(bf16[16,40,1024]{2,1,0:T(8,128)(2,1)S(1)} %shard_map.115), channel_id=1, replica_groups=mesh['frame_0'=4,'frame_1'=4,'tile_0'=4,'tile_1'=4,'tile_2'=2] {'frame_0..., dimensions={0} | all-to-all | bytes 2621440 | tf_op jit(solution)/shard_map/all_to_all | solution.py:58
  112.1 0.7 shard_map.116
  112.8 25.4 %all_to_all.22.terms = bf16[16,16,256]{2,1,0:T(8,128)(2,1)S(1)} all-to-all(bf16[16,16,256]{2,1,0:T(8,128)(2,1)S(1)} %shard_map.116), channel_id=1, replica_groups=mesh['frame_0'=4,'frame_1'=4,'tile_0'=4,'tile_1'=4,'tile_2'=2] {'tile_1'..., dimensions={0} | all-to-all | bytes 262144 | tf_op jit(solution)/shard_map/all_to_all | solution.py:58
  138.2 1.9 %shard_map.117 = (bf16[320,256]{1,0:T(8,128)(2,1)}, f32[10,180]{1,0:T(8,128)}, f32[10,60]{1,0:T(8,128)}, f32[320]{0:T(512)}, f32[320]{0:T(512)}) custom-call(s32[2]{0:T(128)S(1)} %pad_add_fusion.place, f32[320,128]{1,0:T(8,128)S(1)} %get-tuple-element.34.norm, f32[1,320]{1,0:T(1,128)S(1)} %broadcast_in_dim.24.gain, bf16[320,256]{1,0:T(8,128)(2,1)S(1)} %bitcast.14, ...), custom_call_target="tpu_custom_call" | custom-call | flops 4194304 | bytes 1048576 | tf_op jit(solution)/shard_map/pallas_call | solution.py:552
  (14 shorter events, 0.1 us)
Async XLA Ops:
  34.3 7.2 %copy-start.1 = (bf16[320,256]{1,0:T(8,128)(2,1)S(1)}, bf16[320,256]{1,0:T(8,128)(2,1)}, u32[]{:S(2)}) copy-start(bf16[320,256]{1,0:T(8,128)(2,1)} %get-tuple-element.24.g_here) | copy-start | bytes 491524
  34.3 18.5 %copy-start = (bf16[1,320,256]{2,1,0:T(8,128)(2,1)S(1)}, bf16[1,320,256]{2,1,0:T(8,128)(2,1)}, u32[]{:S(2)}) copy-start(bf16[1,320,256]{2,1,0:T(8,128)(2,1)} %param.7) | copy-start | bytes 491524
  34.3 36.9 %copy-start.2 = (f32[320]{0:T(512)S(1)}, f32[320]{0:T(512)}, u32[]{:S(2)}) copy-start(f32[320]{0:T(512)} %param.11) | copy-start | bytes 3844
  34.3 36.9 %copy-start.3 = (f32[320]{0:T(512)S(1)}, f32[320]{0:T(512)}, u32[]{:S(2)}) copy-start(f32[320]{0:T(512)} %param.12) | copy-start | bytes 3844
  34.3 26.4 %all-to-all-start.1 = ((bf16[16,40,1024]{2,1,0:T(8,128)(2,1)}), bf16[16,40,1024]{2,1,0:T(8,128)(2,1)S(1)}, u32[]{:S(2)}, u32[]{:S(2)}) async-start(bf16[16,40,1024]{2,1,0:T(8,128)(2,1)} %shard_map.111), calls=%async_computation.1 | async-start | bytes 2621440 | tf_op jit(solution)/shard_map/all_to_all | solution.py:58
  41.5 7.2 %collective-permute-start.1 = (bf16[320,256]{1,0:T(8,128)(2,1)S(1)}, bf16[320,256]{1,0:T(8,128)(2,1)S(1)}, u32[]{:S(2)}, u32[]{:S(2)}) collective-permute-start(bf16[320,256]{1,0:T(8,128)(2,1)S(1)} %copy-done.1), channel_id=1, source_target_pairs={{0,32},{32,64},{64,96},{96,128},{128,160},{160,192},{192,224},{224... | collective-permute-start | bytes 491528 | tf_op jit(solution)/shard_map/ppermute | solution.py:458
  44.1 8.7 %collective-permute-start = (bf16[320,256]{1,0:T(8,128)(2,1)S(1)}, bf16[320,256]{1,0:T(8,128)(2,1)S(1)}, u32[]{:S(2)}, u32[]{:S(2)}) collective-permute-start(bf16[320,256]{1,0:T(8,128)(2,1)S(1)} %copy-done.1), channel_id=1, source_target_pairs={{32,0},{64,32},{96,64},{128,96},{160,128},{192,160},{224,192},{256... | collective-permute-start | bytes 491528 | tf_op jit(solution)/shard_map/ppermute | solution.py:458
  53.8 2.6 %collective-permute-start.2 = (bf16[320,128]{1,0:T(8,128)(2,1)S(1)}, bf16[320,128]{1,0:T(8,128)(2,1)S(1)}, u32[]{:S(2)}, u32[]{:S(2)}) collective-permute-start(bf16[320,128]{1,0:T(8,128)(2,1)S(1)} %get-tuple-element.26), channel_id=1, source_target_pairs={{0,1},{1,2},{2,3},{3,4},{4,5},{5,6},{6,7},{7,8},{8,9},{9,10},{10,1... | collective-permute-start | bytes 245768 | tf_op jit(solution)/shard_map/ppermute | solution.py:458
  55.1 5.5 %collective-permute-start.3 = (bf16[320,128]{1,0:T(8,128)(2,1)S(1)}, bf16[320,128]{1,0:T(8,128)(2,1)S(1)}, u32[]{:S(2)}, u32[]{:S(2)}) collective-permute-start(bf16[320,128]{1,0:T(8,128)(2,1)S(1)} %get-tuple-element.27), channel_id=1, source_target_pairs={{1,0},{2,1},{3,2},{4,3},{5,4},{6,5},{7,6},{8,7},{9,8},{10,9},{11,1... | collective-permute-start | bytes 245768 | tf_op jit(solution)/shard_map/ppermute | solution.py:458
  60.7 13.2 %collective-permute-start.4 = (bf16[4,160,1024]{2,1,0:T(8,128)(2,1)S(1)}, bf16[4,160,1024]{2,1,0:T(8,128)(2,1)S(1)}, u32[]{:S(2)}, u32[]{:S(2)}) collective-permute-start(bf16[4,160,1024]{2,1,0:T(8,128)(2,1)S(1)} %bitcast.7), channel_id=1, source_target_pairs={{0,1},{1,0},{2,3},{3,2},{4,5},{5,4},{6,7},{7,6},{8,9},{9,8},{10,11... | collective-permute-start | bytes 3932168 | tf_op jit(solution)/shard_map/ppermute | solution.py:462
  80.2 4.9 %collective-permute-start.5 = (bf16[4,160,1024]{2,1,0:T(8,128)(2,1)S(1)}, bf16[4,160,1024]{2,1,0:T(8,128)(2,1)S(1)}, u32[]{:S(2)}, u32[]{:S(2)}) collective-permute-start(bf16[4,160,1024]{2,1,0:T(8,128)(2,1)S(1)} %get-tuple-element.37), channel_id=1, source_target_pairs={{0,1},{1,0},{2,3},{3,2},{4,5},{5,4},{6,7},{7,6},{8,9},{9,8},{10,11... | collective-permute-start | bytes 3932168 | tf_op jit(solution)/shard_map/ppermute | solution.py:462

commit v7 on v6

--- a/solution.py
+++ b/solution.py
@@ -152,8 +152,8 @@
     for n, ref in enumerate((latent, g_next, g_here, g_last)):
         head += dot(ref[...], row_move(n, 0))
         tail += dot(ref[...], row_move(n, last))
-    row_first[...] = head.astype(bf16)
-    row_last[...] = tail.astype(bf16)
+    row_first[...] = (head[:160] + pltpu.roll(head[160:], 64, 1)).astype(bf16)
+    row_last[...] = (tail[:160] + pltpu.roll(tail[160:], 64, 1)).astype(bf16)
 
 
 def pack_kernel(blocks, out):
@@ -282,10 +282,13 @@
     def extended(own, set_index):
         source = iota((128, 128), 0)
         lane = iota((128, 128), 1)
-        from_set = (source >> 4) == set_index
-        low = from_set & (lane == (source & 15))
-        high = from_set & (lane == (source & 15) + (ABOVE - BELOW))
-        rows = dot(below[...], zero_one(low)) + dot(above[...], zero_one(high))
+        rows = []
+        for half in range(2):
+            from_set = (source >> 4) == 4 * half + set_index
+            low = from_set & (lane == (source & 15))
+            high = from_set & (lane == (source & 15) + (ABOVE - BELOW))
+            rows.append(dot(below[...], zero_one(low)) + dot(above[...], zero_one(high)))
+        rows = jnp.concatenate(rows, axis=0)
         return jnp.concatenate([own, rows.astype(bf16)], axis=1)
 
     latent_ext[...] = extended(latent[...], 0)
@@ -492,10 +495,11 @@
     grad_last = step_by(grad, FRAME, 1)
     grad_next = step_by(grad, FRAME, -1)
     near = exchange(near, ROW_Z)
+    near, grad_last, grad_next = lax.optimization_barrier((near, grad_last, grad_next))
     packed = call(pack_kernel, shape((16, 40, PACK), bf16), flops=1 << 27, moved=3 << 19)(near)
     w_own = exchange(packed, PLANE).reshape(4, 160, PACK)
 
-    row_tile = shape((CHANNELS, 128), bf16)
+    row_tile = shape((CHANNELS // 2, 128), bf16)
     row_first, row_last = call(
         rows_kernel, (row_tile, row_tile), smem=1, inputs=5, flops=1 << 28, moved=1 << 20
     )(place, latent, grad_next, grad, grad_last)

time: 141 us -> 130 us (0.922)
  blocking collectives: 80.9 us -> 46.7 us
  waiting for transfers between devices: 12.2 us -> 28.6 us
  starting transfers between devices: 28.4 us -> 35.7 us
    all_to_all x3 -> x2, blocking collectives: 80.9 us -> 46.7 us  [exchange(): return lax.all_to_all(blocks, axes, 0, 0, tiled=True)]
    all_to_all x1 -> x2, starting transfers between devices: 7.18 us -> 23.1 us  [exchange(): return lax.all_to_all(blocks, axes, 0, 0, tiled=True)]
    all_to_all x1 -> x2, waiting for transfers between devices: 0.01 us -> 14.3 us  [exchange(): return lax.all_to_all(blocks, axes, 0, 0, tiled=True)]
    ppermute x2, starting transfers between devices: 12.8 us -> 4.06 us  [swap_cores(): return lax.ppermute(value, 'tile_2', [(0, 1), (1, 0)])]
    ppermute x4, waiting for transfers between devices: 9.58 us -> 11.3 us  [step_by(): return lax.ppermute(value, axes, pairs)]
  transfers between devices with their start and end apart: 7 -> 8, of which waited for: 4 -> 7; matrix products, arithmetic and copies ran while one was open for 0% -> 0% of each run, Pallas kernels for 2% -> 3%
where the time goes in v7:
time: 130 us
  blocking collectives  46.7 us (36%)
  starting transfers between devices  35.7 us (27%)
  waiting for transfers between devices  28.6 us (22%)
  Pallas kernels  16.7 us (13%)
  between operations  1.44 us (1%)
    all_to_all x2, blocking collectives, exchange(): return lax.all_to_all(blocks, axes, 0, 0, tiled=True)  46.7 us
    all_to_all x2, starting transfers between devices, exchange(): return lax.all_to_all(blocks, axes, 0, 0, tiled=True)  23.1 us
    all_to_all x2, waiting for transfers between devices, exchange(): return lax.all_to_all(blocks, axes, 0, 0, tiled=True)  14.3 us
    ppermute x4, waiting for transfers between devices, step_by(): return lax.ppermute(value, axes, pairs)  11.3 us
    ppermute x4, starting transfers between devices, step_by(): return lax.ppermute(value, axes, pairs)  8.54 us
    pallas_call x1, Pallas kernels, local(): call(main_kernel, (block, block, shape((CHANNELS, CELLS), f32), shape((CH...  6.32 us
    ppermute x2, starting transfers between devices, swap_cores(): return lax.ppermute(value, 'tile_2', [(0, 1), (1, 0)])  4.06 us
    ppermute x2, waiting for transfers between devices, swap_cores(): return lax.ppermute(value, 'tile_2', [(0, 1), (1, 0)])  3.04 us
  transfers between devices with their start and end apart: 8, of which 7 were waited for; matrix products, arithmetic and copies ran while one was open for 0% of the time, Pallas kernels for 3%

profile of v7, /device:TPU:32, one launch (start us, length us, event | category | flops | bytes accessed | tf_op | source)
XLA Modules:
  0.0 129.7 jit_solution(13061696548909518732)
XLA Ops:
  1.3 1.9 %shard_map.110 = (bf16[16,16,256]{2,1,0:T(8,128)(2,1)}, bf16[320,256]{1,0:T(8,128)(2,1)}) custom-call(s32[1]{0:T(128)S(6)} %copy.12.place, bf16[320,256]{1,0:T(8,128)(2,1)} %bitcast.11, bf16[320,256]{1,0:T(8,128)(2,1)} %bitcast.15, bf16[10,180]{1,0:T(8,128)(2,1)} %w_spatial_at.1, bf16[10,60]{1,0:T(8,128)(2,1)} %w_temporal_at.1), custom_call_target="tpu_custom_call" | custom-call | flops 1048576 | bytes 262144 | tf_op jit(solution)/shard_map/pallas_call | solution.py:475
  3.2 15.2 %all-to-all-start = ((bf16[16,16,256]{2,1,0:T(8,128)(2,1)}), bf16[16,16,256]{2,1,0:T(8,128)(2,1)S(1)}, u32[]{:S(2)}, u32[]{:S(2)}) async-start(bf16[16,16,256]{2,1,0:T(8,128)(2,1)} %get-tuple-element.28), calls=%async_computation | async-start | bytes 262144 | tf_op jit(solution)/shard_map/all_to_all | solution.py:58
  18.4 2.0 %collective-permute-start.1 = (bf16[320,256]{1,0:T(8,128)(2,1)}, bf16[320,256]{1,0:T(8,128)(2,1)S(1)}, u32[]{:S(2)}, u32[]{:S(2)}) collective-permute-start(bf16[320,256]{1,0:T(8,128)(2,1)} %get-tuple-element.27.g_here), channel_id=1, source_target_pairs={{32,0},{64,32},{96,64},{128,96},{160,128},{192,160},{224,192},{256... | collective-permute-start | bytes 491528 | tf_op jit(solution)/shard_map/ppermute | solution.py:461
  20.4 3.8 %collective-permute-start = (bf16[320,256]{1,0:T(8,128)(2,1)}, bf16[320,256]{1,0:T(8,128)(2,1)S(1)}, u32[]{:S(2)}, u32[]{:S(2)}) collective-permute-start(bf16[320,256]{1,0:T(8,128)(2,1)} %get-tuple-element.27.g_here), channel_id=1, source_target_pairs={{0,32},{32,64},{64,96},{96,128},{128,160},{160,192},{192,224},{224... | collective-permute-start | bytes 491528 | tf_op jit(solution)/shard_map/ppermute | solution.py:461
  24.3 5.1 %collective-permute-done.1.g_next = bf16[320,256]{1,0:T(8,128)(2,1)S(1)} collective-permute-done((bf16[320,256]{1,0:T(8,128)(2,1)}, bf16[320,256]{1,0:T(8,128)(2,1)S(1)}, u32[]{:S(2)}, u32[]{:S(2)}) %collective-permute-start.1) | collective-permute-done | bytes 163872 | tf_op jit(solution)/shard_map/ppermute | solution.py:461
  29.4 0.5 collective-permute-done.g_last
  29.9 2.8 %all-to-all-done.blocks = bf16[16,16,256]{2,1,0:T(8,128)(2,1)S(1)} async-done(((bf16[16,16,256]{2,1,0:T(8,128)(2,1)}), bf16[16,16,256]{2,1,0:T(8,128)(2,1)S(1)}, u32[]{:S(2)}, u32[]{:S(2)}) %all-to-all-start) | async-done | bytes 131104 | tf_op jit(solution)/shard_map/all_to_all | solution.py:58
  32.7 1.7 %shard_map.111 = bf16[16,40,1024]{2,1,0:T(8,128)(2,1)} custom-call(bf16[16,16,256]{2,1,0:T(8,128)(2,1)S(1)} %all-to-all-done.blocks), custom_call_target="tpu_custom_call" | custom-call | flops 134217728 | bytes 1572864 | tf_op jit(solution)/shard_map/pallas_call | solution.py:499
  34.4 7.9 %all-to-all-start.1 = ((bf16[16,40,1024]{2,1,0:T(8,128)(2,1)}), bf16[16,40,1024]{2,1,0:T(8,128)(2,1)S(1)}, u32[]{:S(2)}, u32[]{:S(2)}) async-start(bf16[16,40,1024]{2,1,0:T(8,128)(2,1)} %shard_map.111), calls=%async_computation.1 | async-start | bytes 2621440 | tf_op jit(solution)/shard_map/all_to_all | solution.py:58
  42.4 1.1 shard_map.112
  43.5 1.4 %collective-permute-start.2 = (bf16[160,128]{1,0:T(8,128)(2,1)S(1)}, bf16[160,128]{1,0:T(8,128)(2,1)S(1)}, u32[]{:S(2)}, u32[]{:S(2)}) collective-permute-start(bf16[160,128]{1,0:T(8,128)(2,1)S(1)} %get-tuple-element.32), channel_id=1, source_target_pairs={{0,1},{1,2},{2,3},{3,4},{4,5},{5,6},{6,7},{7,8},{8,9},{9,10},{10,1... | collective-permute-start | bytes 122888 | tf_op jit(solution)/shard_map/ppermute | solution.py:461
  44.9 1.3 collective-permute-start.3
  46.2 5.7 %collective-permute-done.3.below = bf16[160,128]{1,0:T(8,128)(2,1)S(1)} collective-permute-done((bf16[160,128]{1,0:T(8,128)(2,1)S(1)}, bf16[160,128]{1,0:T(8,128)(2,1)S(1)}, u32[]{:S(2)}, u32[]{:S(2)}) %collective-permute-start.3) | collective-permute-done | bytes 40992 | tf_op jit(solution)/shard_map/ppermute | solution.py:461
  51.9 11.5 %all-to-all-done.1 = bf16[16,40,1024]{2,1,0:T(8,128)(2,1)S(1)} async-done(((bf16[16,40,1024]{2,1,0:T(8,128)(2,1)}), bf16[16,40,1024]{2,1,0:T(8,128)(2,1)S(1)}, u32[]{:S(2)}, u32[]{:S(2)}) %all-to-all-start.1) | async-done | bytes 1310752 | tf_op jit(solution)/shard_map/all_to_all | solution.py:58
  63.3 1.9 %collective-permute-start.4 = (bf16[4,160,1024]{2,1,0:T(8,128)(2,1)S(1)}, bf16[4,160,1024]{2,1,0:T(8,128)(2,1)S(1)}, u32[]{:S(2)}, u32[]{:S(2)}) collective-permute-start(bf16[4,160,1024]{2,1,0:T(8,128)(2,1)S(1)} %bitcast.7), channel_id=1, source_target_pairs={{0,1},{1,0},{2,3},{3,2},{4,5},{5,4},{6,7},{7,6},{8,9},{9,8},{10,11... | collective-permute-start | bytes 3932168 | tf_op jit(solution)/shard_map/ppermute | solution.py:465
  65.8 2.2 %shard_map.113 = (bf16[320,384]{1,0:T(8,128)(2,1)S(1)}, bf16[3,320,384]{2,1,0:T(8,128)(2,1)S(1)}, bf16[9,384,256]{2,1,0:T(8,128)(2,1)S(1)}) custom-call(s32[2]{0:T(128)S(1)} %pad_add_fusion.place, s32[320,1]{1,0:T(8,128)S(1)} %fusion.3.order, bf16[320,256]{1,0:T(8,128)(2,1)S(1)} %bitcast.13, bf16[320,256]{1,0:T(8,128)(2,1)S(1)} %copy-done.1, ...), custom_call_target="tpu_custom_call" | custom-call | flops 536870912 | bytes 2097152 | tf_op jit(solution)/shard_map/pallas_call | solution.py:516
  68.2 6.3 %shard_map.114 = (bf16[4,160,1024]{2,1,0:T(8,128)(2,1)S(1)}, bf16[4,160,1024]{2,1,0:T(8,128)(2,1)S(1)}, f32[320,256]{1,0:T(8,128)S(1)}, f32[320,128]{1,0:T(8,128)S(1)}) custom-call(s32[2]{0:T(128)S(1)} %pad_add_fusion.place, f32[1,320]{1,0:T(1,128)S(1)} %broadcast_in_dim.24.gain, f32[1,320]{1,0:T(1,128)S(1)} %broadcast_in_dim.25.shift, ...), custom_call_target="tpu_custom_call" | custom-call | flops 5368709120 | bytes 8388608 | tf_op jit(solution)/shard_map/pallas_call | solution.py:529
  74.6 2.1 %collective-permute-start.5 = (bf16[4,160,1024]{2,1,0:T(8,128)(2,1)S(1)}, bf16[4,160,1024]{2,1,0:T(8,128)(2,1)S(1)}, u32[]{:S(2)}, u32[]{:S(2)}) collective-permute-start(bf16[4,160,1024]{2,1,0:T(8,128)(2,1)S(1)} %get-tuple-element.43), channel_id=1, source_target_pairs={{0,1},{1,0},{2,3},{3,2},{4,5},{5,4},{6,7},{7,6},{8,9},{9,8},{10,11... | collective-permute-start | bytes 3932168 | tf_op jit(solution)/shard_map/ppermute | solution.py:465
  76.7 2.8 %collective-permute-done.5 = bf16[4,160,1024]{2,1,0:T(8,128)(2,1)S(1)} collective-permute-done((bf16[4,160,1024]{2,1,0:T(8,128)(2,1)S(1)}, bf16[4,160,1024]{2,1,0:T(8,128)(2,1)S(1)}, u32[]{:S(2)}, u32[]{:S(2)}) %collective-permute-start.5) | collective-permute-done | bytes 1310752 | tf_op jit(solution)/shard_map/ppermute | solution.py:465
  79.5 0.9 shard_map.115
  80.4 23.3 %all_to_all.20.terms = bf16[16,40,1024]{2,1,0:T(8,128)(2,1)S(1)} all-to-all(bf16[16,40,1024]{2,1,0:T(8,128)(2,1)S(1)} %shard_map.115), channel_id=1, replica_groups=mesh['frame_0'=4,'frame_1'=4,'tile_0'=4,'tile_1'=4,'tile_2'=2] {'frame_0..., dimensions={0} | all-to-all | bytes 2621440 | tf_op jit(solution)/shard_map/all_to_all | solution.py:58
  103.6 0.7 shard_map.116
  104.3 23.5 %all_to_all.21.terms = bf16[16,16,256]{2,1,0:T(8,128)(2,1)S(1)} all-to-all(bf16[16,16,256]{2,1,0:T(8,128)(2,1)S(1)} %shard_map.116), channel_id=1, replica_groups=mesh['frame_0'=4,'frame_1'=4,'tile_0'=4,'tile_1'=4,'tile_2'=2] {'tile_1'..., dimensions={0} | all-to-all | bytes 262144 | tf_op jit(solution)/shard_map/all_to_all | solution.py:58
  127.8 1.9 %shard_map.117 = (bf16[320,256]{1,0:T(8,128)(2,1)}, f32[10,180]{1,0:T(8,128)}, f32[10,60]{1,0:T(8,128)}, f32[320]{0:T(512)}, f32[320]{0:T(512)}) custom-call(s32[2]{0:T(128)S(1)} %pad_add_fusion.place, f32[320,128]{1,0:T(8,128)S(1)} %get-tuple-element.40.norm, f32[1,320]{1,0:T(1,128)S(1)} %broadcast_in_dim.24.gain, bf16[320,256]{1,0:T(8,128)(2,1)S(1)} %bitcast.14, ...), custom_call_target="tpu_custom_call" | custom-call | flops 4194304 | bytes 1048576 | tf_op jit(solution)/shard_map/pallas_call | solution.py:556
  (15 shorter events, 0.8 us)
Async XLA Ops:
  3.2 29.5 %all-to-all-start = ((bf16[16,16,256]{2,1,0:T(8,128)(2,1)}), bf16[16,16,256]{2,1,0:T(8,128)(2,1)S(1)}, u32[]{:S(2)}, u32[]{:S(2)}) async-start(bf16[16,16,256]{2,1,0:T(8,128)(2,1)} %get-tuple-element.28), calls=%async_computation | async-start | bytes 262144 | tf_op jit(solution)/shard_map/all_to_all | solution.py:58
  18.4 11.0 %collective-permute-start.1 = (bf16[320,256]{1,0:T(8,128)(2,1)}, bf16[320,256]{1,0:T(8,128)(2,1)S(1)}, u32[]{:S(2)}, u32[]{:S(2)}) collective-permute-start(bf16[320,256]{1,0:T(8,128)(2,1)} %get-tuple-element.27.g_here), channel_id=1, source_target_pairs={{32,0},{64,32},{96,64},{128,96},{160,128},{192,160},{224,192},{256... | collective-permute-start | bytes 491528 | tf_op jit(solution)/shard_map/ppermute | solution.py:461
  20.4 9.5 %collective-permute-start = (bf16[320,256]{1,0:T(8,128)(2,1)}, bf16[320,256]{1,0:T(8,128)(2,1)S(1)}, u32[]{:S(2)}, u32[]{:S(2)}) collective-permute-start(bf16[320,256]{1,0:T(8,128)(2,1)} %get-tuple-element.27.g_here), channel_id=1, source_target_pairs={{0,32},{32,64},{64,96},{96,128},{128,160},{160,192},{192,224},{224... | collective-permute-start | bytes 491528 | tf_op jit(solution)/shard_map/ppermute | solution.py:461
  34.4 8.0 %copy-start = (bf16[1,320,256]{2,1,0:T(8,128)(2,1)S(1)}, bf16[1,320,256]{2,1,0:T(8,128)(2,1)}, u32[]{:S(2)}) copy-start(bf16[1,320,256]{2,1,0:T(8,128)(2,1)} %param.7) | copy-start | bytes 491524
  34.4 8.0 %copy-start.1 = (bf16[320,256]{1,0:T(8,128)(2,1)S(1)}, bf16[320,256]{1,0:T(8,128)(2,1)}, u32[]{:S(2)}) copy-start(bf16[320,256]{1,0:T(8,128)(2,1)} %get-tuple-element.27.g_here) | copy-start | bytes 491524
  34.4 30.9 %copy-start.2 = (f32[320]{0:T(512)S(1)}, f32[320]{0:T(512)}, u32[]{:S(2)}) copy-start(f32[320]{0:T(512)} %param.11) | copy-start | bytes 3844
  34.4 30.9 %copy-start.3 = (f32[320]{0:T(512)S(1)}, f32[320]{0:T(512)}, u32[]{:S(2)}) copy-start(f32[320]{0:T(512)} %param.12) | copy-start | bytes 3844
  34.4 28.9 %all-to-all-start.1 = ((bf16[16,40,1024]{2,1,0:T(8,128)(2,1)}), bf16[16,40,1024]{2,1,0:T(8,128)(2,1)S(1)}, u32[]{:S(2)}, u32[]{:S(2)}) async-start(bf16[16,40,1024]{2,1,0:T(8,128)(2,1)} %shard_map.111), calls=%async_computation.1 | async-start | bytes 2621440 | tf_op jit(solution)/shard_map/all_to_all | solution.py:58
  43.5 2.7 %collective-permute-start.2 = (bf16[160,128]{1,0:T(8,128)(2,1)S(1)}, bf16[160,128]{1,0:T(8,128)(2,1)S(1)}, u32[]{:S(2)}, u32[]{:S(2)}) collective-permute-start(bf16[160,128]{1,0:T(8,128)(2,1)S(1)} %get-tuple-element.32), channel_id=1, source_target_pairs={{0,1},{1,2},{2,3},{3,4},{4,5},{5,6},{6,7},{7,8},{8,9},{9,10},{10,1... | collective-permute-start | bytes 122888 | tf_op jit(solution)/shard_map/ppermute | solution.py:461
  44.9 7.0 %collective-permute-start.3 = (bf16[160,128]{1,0:T(8,128)(2,1)S(1)}, bf16[160,128]{1,0:T(8,128)(2,1)S(1)}, u32[]{:S(2)}, u32[]{:S(2)}) collective-permute-start(bf16[160,128]{1,0:T(8,128)(2,1)S(1)} %get-tuple-element.33), channel_id=1, source_target_pairs={{1,0},{2,1},{3,2},{4,3},{5,4},{6,5},{7,6},{8,7},{9,8},{10,9},{11,1... | collective-permute-start | bytes 122888 | tf_op jit(solution)/shard_map/ppermute | solution.py:461
  63.3 4.9 %collective-permute-start.4 = (bf16[4,160,1024]{2,1,0:T(8,128)(2,1)S(1)}, bf16[4,160,1024]{2,1,0:T(8,128)(2,1)S(1)}, u32[]{:S(2)}, u32[]{:S(2)}) collective-permute-start(bf16[4,160,1024]{2,1,0:T(8,128)(2,1)S(1)} %bitcast.7), channel_id=1, source_target_pairs={{0,1},{1,0},{2,3},{3,2},{4,5},{5,4},{6,7},{7,6},{8,9},{9,8},{10,11... | collective-permute-start | bytes 3932168 | tf_op jit(solution)/shard_map/ppermute | solution.py:465
  74.6 4.9 %collective-permute-start.5 = (bf16[4,160,1024]{2,1,0:T(8,128)(2,1)S(1)}, bf16[4,160,1024]{2,1,0:T(8,128)(2,1)S(1)}, u32[]{:S(2)}, u32[]{:S(2)}) collective-permute-start(bf16[4,160,1024]{2,1,0:T(8,128)(2,1)S(1)} %get-tuple-element.43), channel_id=1, source_target_pairs={{0,1},{1,0},{2,3},{3,2},{4,5},{5,4},{6,7},{7,6},{8,9},{9,8},{10,11... | collective-permute-start | bytes 3932168 | tf_op jit(solution)/shard_map/ppermute | solution.py:465
